TPU v7x, 32 devices: a whole 2x2x4 slice. The times are simulated.
32 devices in a mesh: batch: 16 (over z, y, core), tm: 2 (over x).
Axes of the slice: x: 2, y: 2, z: 4, core: 2. Of those that a mesh axis runs over, the one named last changes fastest.
Arguments:
- ref_rows: bfloat16 [8192, 1024], P(('batch', 'tm')), may hold values from -6 to 6
- neg_rows: bfloat16 [2048, 1024], P(('batch', 'tm')), may hold values from -6 to 6
- recording: bfloat16 [1024, 1024], P('tm'), may hold values from -6 to 6
- pos_owner: int32 [8192, 1], P(('batch', 'tm')), may hold values from 0 to 1; in each aligned block of 256 rows (0 to 255, 256 to 511, ...) at most 256 rows name the same one
- pos_row: int32 [8192], P(('batch', 'tm')), may hold values from 0 to 511
- ref_animal: int32 [8192], P(('batch', 'tm')), may hold values from 0 to 7
- neg_animal: int32 [2048], P(('batch', 'tm')), may hold values from 0 to 7
- w_in: bfloat16 [1024, 512], replicated, may hold values from -0.1875 to 0.1875
- bias_animal: float32 [8, 512], replicated, may hold values from -5 to 5
- w_out: bfloat16 [512, 128], replicated, may hold values from -0.25 to 0.25
Outputs:
- ref_loss: float32 [8192], P(('batch', 'tm'))
- grad_w_in: bfloat16 [1024, 512], replicated
- grad_w_out: float32 [512, 128], replicated
- grad_bias: float32 [8, 512], replicated
Inputs may be any that keep to these rules, and one draw needn't show every extreme that they name: `pos_owner`: among the 256 references of one device at most 256 name one owner, and in every draw some owner is named by exactly 256 of them.
All inputs are finite; a program needn't handle non-finite values.
Results may differ from a plain program's by a relative error of at most 0.0069.
Values may be sent and summed in bfloat16 or wider, within the bound.
No kernel may reach another device: no remote copies, remote signals or barrier semaphores. Data moves between devices by JAX's collectives and lax.ppermute only.
A program may use at most 64 MiB of HBM per device.

v0:
```python
import math

import jax
import jax.numpy as jnp
from jax import lax
from jax.sharding import PartitionSpec as P

logit_sharpness_divisor = 0.1
shift_bound = 10.0
epsilon = 1e-06


def encode_rows(samples, animal_ids, w_in, bias_animal, w_out):
    animals = bias_animal.shape[0]
    one_hot = (animal_ids[:, None] == jnp.arange(animals, dtype=jnp.int32)[None, :]).astype(
        jnp.float32
    )
    pre_act = jnp.dot(samples, w_in, preferred_element_type=jnp.float32) + jnp.dot(
        one_hot, bias_animal, precision=lax.Precision.HIGHEST
    )
    hidden = jax.nn.gelu(pre_act).astype(jnp.bfloat16)
    latent = jnp.dot(hidden, w_out, preferred_element_type=jnp.float32)
    radius = jnp.sqrt(jnp.sum(latent * latent, axis=1, keepdims=True) + epsilon)
    unit_vec = (latent / radius).astype(jnp.bfloat16)
    return (pre_act, hidden, latent, radius, unit_vec)


def on_device(
    ref_rows,
    neg_rows,
    recording,
    pos_owner,
    pos_row,
    ref_animal,
    neg_animal,
    w_in,
    bias_animal,
    w_out,
):
    anchors_each_processor = ref_rows.shape[0]
    negs_dev = neg_rows.shape[0]
    embed_width = w_out.shape[1]
    holder_processors = lax.axis_size("tm")
    minibatch_clusters = lax.axis_size("batch")
    capacity = 2 * anchors_each_processor // holder_processors
    first_enc = encode_rows(
        jnp.concatenate([ref_rows, neg_rows], 0),
        jnp.concatenate([ref_animal, neg_animal]),
        w_in,
        bias_animal,
        w_out,
    )
    reference_unit_vector = first_enc[4][:anchors_each_processor]
    neg_unit = first_enc[4][anchors_each_processor:]
    pool = lax.all_gather(neg_unit, "batch", axis=0, tiled=True)
    owner_ids = pos_owner[:, 0]
    owner_hot = (
        owner_ids[:, None] == jnp.arange(holder_processors, dtype=jnp.int32)[None, :]
    ).astype(jnp.int32)
    slot_ids = jnp.sum((jnp.cumsum(owner_hot, axis=0) - owner_hot) * owner_hot, axis=1)
    places = owner_ids * capacity + slot_ids
    requests = (
        jnp.zeros((holder_processors * capacity,), jnp.int32)
        .at[places]
        .set(pos_row)
        .reshape(holder_processors, capacity)
    )
    asked = lax.all_to_all(requests, "tm", split_axis=0, concat_axis=0, tiled=True)
    found = jnp.take(recording, asked.reshape(-1), axis=0)
    found = found.reshape(asked.shape[0], asked.shape[1], recording.shape[1])
    arrived = lax.all_to_all(found, "tm", split_axis=0, concat_axis=0, tiled=True)
    pos_rows = jnp.take(
        arrived.reshape(holder_processors * capacity, recording.shape[1]), places, axis=0
    )
    second_enc = encode_rows(pos_rows, ref_animal, w_in, bias_animal, w_out)
    positive_unit_vector = second_enc[4]
    group = math.gcd(minibatch_clusters, max(1, 2048 // negs_dev))
    width = group * negs_dev
    blocks = minibatch_clusters // group
    matching_similarity = (
        jnp.sum(
            reference_unit_vector.astype(jnp.float32) * positive_unit_vector.astype(jnp.float32),
            axis=1,
        )
        / logit_sharpness_divisor
    )

    def block_scores(start):
        block_part = lax.dynamic_slice_in_dim(pool, start, width, 0)
        similarity_table = (
            jnp.einsum(
                "ka,sa->ks", reference_unit_vector, block_part, preferred_element_type=jnp.float32
            )
            / logit_sharpness_divisor
        )
        return (block_part, similarity_table)

    def add_exp(step_index, running):
        block_part, similarity_table = block_scores(step_index * width)
        return running + jnp.sum(jnp.exp(similarity_table - shift_bound), axis=1)

    normalizer = lax.fori_loop(0, blocks, add_exp, jnp.exp(matching_similarity - shift_bound))

    def add_pull(step_index, running):
        block_part, similarity_table = block_scores(step_index * width)
        weights = (jnp.exp(similarity_table - shift_bound) / normalizer[:, None]).astype(
            jnp.bfloat16
        )
        return running + jnp.dot(weights, block_part, preferred_element_type=jnp.float32)

    pulled = lax.fori_loop(
        0, blocks, add_pull, jnp.zeros((anchors_each_processor, embed_width), jnp.float32)
    )
    ref_loss = jnp.log(normalizer) + shift_bound - matching_similarity
    pos_prob = jnp.exp(matching_similarity - shift_bound) / normalizer
    reciprocal_factor = (
        float(anchors_each_processor * minibatch_clusters * holder_processors) ** (-0.5)
        / logit_sharpness_divisor
    )
    grad_ref = reciprocal_factor * (
        pulled + (pos_prob - 1.0)[:, None] * positive_unit_vector.astype(jnp.float32)
    )
    grad_pos = (
        reciprocal_factor * (pos_prob - 1.0)[:, None] * reference_unit_vector.astype(jnp.float32)
    )
    block_part = pool
    similarity_table = (
        jnp.einsum(
            "ka,sa->ks", reference_unit_vector, block_part, preferred_element_type=jnp.float32
        )
        / logit_sharpness_divisor
    )
    weights = (jnp.exp(similarity_table - shift_bound) / normalizer[:, None]).astype(jnp.bfloat16)
    grad_neg = lax.psum_scatter(
        reciprocal_factor
        * jnp.einsum(
            "rn,re->ne", weights, reference_unit_vector, preferred_element_type=jnp.float32
        ),
        "batch",
        scatter_dimension=0,
        tiled=True,
    )
    samples = jnp.concatenate([ref_rows, neg_rows, pos_rows], 0)
    animal_ids = jnp.concatenate([ref_animal, neg_animal, ref_animal])
    pre_act = jnp.concatenate([first_enc[0], second_enc[0]], 0)
    hidden = jnp.concatenate([first_enc[1], second_enc[1]], 0)
    latent = jnp.concatenate([first_enc[2], second_enc[2]], 0)
    radius = jnp.concatenate([first_enc[3], second_enc[3]], 0)
    grad_unit = jnp.concatenate([grad_ref, grad_neg, grad_pos], 0)
    inner = jnp.sum(latent * grad_unit, axis=1, keepdims=True)
    grad_latent = ((grad_unit - latent * inner / (radius * radius)) / radius).astype(jnp.bfloat16)
    grad_hidden = jnp.dot(grad_latent, w_out.T, preferred_element_type=jnp.float32)
    grad_pre = jax.vjp(jax.nn.gelu, pre_act)[1](grad_hidden)[0].astype(jnp.bfloat16)
    animals = bias_animal.shape[0]
    animal_hot = (animal_ids[:, None] == jnp.arange(animals, dtype=jnp.int32)[None, :]).astype(
        jnp.bfloat16
    )
    local_in = jnp.dot(samples.T, grad_pre, preferred_element_type=jnp.float32)
    local_out = jnp.dot(hidden.T, grad_latent, preferred_element_type=jnp.float32)
    local_bias = jnp.dot(animal_hot.T, grad_pre, preferred_element_type=jnp.float32)
    grad_w_in, grad_w_out, grad_bias = lax.psum((local_in, local_out, local_bias), ("batch", "tm"))
    return (ref_loss, grad_w_in.astype(jnp.bfloat16), grad_w_out, grad_bias)


def solution(mesh):
    in_specs = (
        P(("batch", "tm"), None),
        P(("batch", "tm"), None),
        P("tm", None),
        P(("batch", "tm"), None),
        P(("batch", "tm")),
        P(("batch", "tm")),
        P(("batch", "tm")),
        P(),
        P(),
        P(),
    )
    out_specs = (P(("batch", "tm")), P(), P(), P())
    return jax.shard_map(
        on_device, mesh=mesh, in_specs=in_specs, out_specs=out_specs, check_vma=False
    )
```

profile of v0, /device:TPU:0, one launch (start us, length us, event | category | flops | bytes accessed | tf_op | source)
XLA Modules:
  0.0 266.8 jit_solution(9246577990645195994)
XLA Ops:
  7.2 0.8 compare_convert_fusion
  10.4 2.1 scatter_custom_fusion
  12.5 4.2 %all-to-all-start = ((s32[2,1,256]{2,1,0:T(1,128)}), s32[2,1,256]{2,1,0:T(1,128)S(1)}, u32[]{:S(2)}, u32[]{:S(2)}) async-start(s32[2,1,256]{2,1,0:T(1,128)} %bitcast.5), calls=%async_computation | async-start | bytes 4096 | tf_op jit(solution)/shard_map/all_to_all | solution.py:68
  17.5 1.9 fusion.24
  19.4 1.5 fusion.23
  22.0 22.8 %all_gather.3 = bf16[1024,128]{1,0:T(8,128)(2,1)S(1)} all-gather(bf16[64,128]{1,0:T(8,128)(2,1)S(1)} %slice.22), channel_id=1, replica_groups=mesh['batch'=16,'tm'=2] {'batch'}, dimensions={0}, use_global_device_ids=true | all-gather | bytes 278528 | tf_op jit(solution)/shard_map/all_gather | solution.py:55
  44.9 2.1 gather_fusion
  47.0 1.1 broadcast_select_fusion
  48.1 3.7 %all-to-all-start.1 = ((bf16[2,256,1024]{2,1,0:T(8,128)(2,1)}), bf16[2,256,1024]{2,1,0:T(8,128)(2,1)S(1)}, u32[]{:S(2)}, u32[]{:S(2)}) async-start(bf16[2,256,1024]{2,1,0:T(8,128)(2,1)} %broadcast_select_fusion), calls=%async_computation.1 | async-start | bytes 2097152 | tf_op jit(solution)/shard_map/all_to_all | solution.py:71
  51.9 1.2 fusion.43
  53.2 1.0 fusion.57
  54.1 12.3 %all-to-all-done.1 = bf16[2,256,1024]{2,1,0:T(8,128)(2,1)S(1)} async-done(((bf16[2,256,1024]{2,1,0:T(8,128)(2,1)}), bf16[2,256,1024]{2,1,0:T(8,128)(2,1)S(1)}, u32[]{:S(2)}, u32[]{:S(2)}) %all-to-all-start.1) | async-done | bytes 1048608 | tf_op jit(solution)/shard_map/all_to_all | solution.py:71
  66.5 2.0 gather_fusion.1
  68.4 1.2 broadcast_select_fusion.1
  69.6 2.9 %fusion.39 = (bf16[256,512]{1,0:T(8,128)(2,1)S(1)}, f32[256,512]{1,0:T(8,128)}) fusion(f32[256,512]{1,0:T(8,128)} %fusion.43, bf16[256,1024]{1,0:T(8,128)(2,1)S(1)} %broadcast_select_fusion.1, bf16[1024,512]{1,0:T(8,128)(2,1)} %param.17), kind=kOutput, calls=%fused_computation.54 | convolution fusion | flops 269746176 | bytes 2883584 | tf_op jit(solution)/shard_map/dot_general | solution.py:18
  73.9 1.2 convolution_multiply_fusion.1
  76.4 50.5 %reduce-scatter.2.cloned.1.call-done = f32[64,128]{1,0:T(8,128)} async-done(((f32[1024,128]{1,0:T(8,128)}), f32[64,128]{1,0:T(8,128)}) %reduce-scatter.2.cloned.1.call-update) | async-done | bytes 32784 | tf_op jit(solution)/shard_map/reduce_scatter | solution.py:134
  126.9 0.9 multiply_reduce_fusion
  127.9 2.2 fusion.28
  130.1 2.2 fusion.8
  132.4 1.0 fusion.9
  133.7 69.8 %all-reduce.5 = (bf16[1024,512]{1,0:T(8,128)(2,1)}, f32[8,512]{1,0:T(8,128)}) all-reduce(f32[1024,512]{1,0:T(8,128)S(1)} %fusion.9, f32[8,512]{1,0:T(8,128)S(1)} %fusion.40), channel_id=1, replica_groups=mesh['batch'=16,'tm'=2] {'batch','tm'}, use_global_device_ids=true, to_apply=%region_10.11 | all-reduce | flops 528384 | bytes 3178496 | tf_op jit(solution)/shard_map/psum | solution.py:161
  203.5 54.8 %all-reduce.4.cloned.1.call-done = f32[512,128]{1,0:T(8,128)} async-done(((f32[512,128]{1,0:T(8,128)}), f32[512,128]{1,0:T(8,128)}) %all-reduce.4.cloned.1.call-update) | async-done | bytes 262160 | tf_op jit(solution)/shard_map/psum | solution.py:161
  258.3 1.7 copy.22
  (80 shorter events, 7.3 us)
Async XLA Ops:
  7.2 37.7 %copy-start = (bf16[512,1024]{1,0:T(8,128)(2,1)S(1)}, bf16[512,1024]{1,0:T(8,128)(2,1)}, u32[]{:S(2)}) copy-start(bf16[512,1024]{1,0:T(8,128)(2,1)} %param.12) | copy-start | bytes 3145732
  12.5 32.3 %all-to-all-start = ((s32[2,1,256]{2,1,0:T(1,128)}), s32[2,1,256]{2,1,0:T(1,128)S(1)}, u32[]{:S(2)}, u32[]{:S(2)}) async-start(s32[2,1,256]{2,1,0:T(1,128)} %bitcast.5), calls=%async_computation | async-start | bytes 4096 | tf_op jit(solution)/shard_map/all_to_all | solution.py:68
  17.5 1.9 copy-start.15
  19.4 1.5 copy-start.3
  21.2 23.7 %copy-start.1 = (f32[320,128]{1,0:T(8,128)}, f32[320,128]{1,0:T(8,128)S(1)}, u32[]{:S(2)}) copy-start(f32[320,128]{1,0:T(8,128)S(1)} %get-tuple-element.52) | copy-start | bytes 491524
  48.1 3.8 %copy-start.16 = (s32[256]{0:T(256)S(1)}, s32[256]{0:T(256)}, u32[]{:S(2)}) copy-start(s32[256]{0:T(256)} %param.15) | copy-start | bytes 3076
  48.1 18.3 %all-to-all-start.1 = ((bf16[2,256,1024]{2,1,0:T(8,128)(2,1)}), bf16[2,256,1024]{2,1,0:T(8,128)(2,1)S(1)}, u32[]{:S(2)}, u32[]{:S(2)}) async-start(bf16[2,256,1024]{2,1,0:T(8,128)(2,1)} %broadcast_select_fusion), calls=%async_computation.1 | async-start | bytes 2097152 | tf_op jit(solution)/shard_map/all_to_all | solution.py:71
  51.9 75.0 %reduce-scatter.2.cloned.1.call-start = ((), (), s32[]{:S(2)}) async-start(), calls=%async_computation.3 | async-start | bytes 557056 | tf_op jit(solution)/shard_map/reduce_scatter | solution.py:134
  69.6 3.0 %copy-start.5 = (bf16[256,1024]{1,0:T(8,128)(2,1)}, bf16[256,1024]{1,0:T(8,128)(2,1)S(1)}, u32[]{:S(2)}) copy-start(bf16[256,1024]{1,0:T(8,128)(2,1)S(1)} %broadcast_select_fusion.1) | copy-start | bytes 1572868
  69.6 3.0 %copy-start.4 = (bf16[512,128]{1,0:T(8,128)(2,1)S(1)}, bf16[512,128]{1,0:T(8,128)(2,1)}, u32[]{:S(2)}) copy-start(bf16[512,128]{1,0:T(8,128)(2,1)} %param.19) | copy-start | bytes 393220
  69.6 3.5 %copy-start.19 = (f32[256]{0:T(256)S(1)}, f32[256]{0:T(256)}, u32[]{:S(2)}) copy-start(f32[256]{0:T(256)} %get-tuple-element.53) | copy-start | bytes 3076
  73.9 1.3 copy-start.12
  73.9 1.3 copy-start.17
  73.9 1.3 copy-start.20
  73.9 2.2 copy-start.18
  73.9 53.0 %copy-start.2 = (f32[320,128]{1,0:T(8,128)S(1)}, f32[320,128]{1,0:T(8,128)}, u32[]{:S(2)}) copy-start(f32[320,128]{1,0:T(8,128)} %copy-done.1) | copy-start | bytes 491524
  75.1 52.8 %copy-start.8 = (bf16[320,512]{1,0:T(8,128)(2,1)S(1)}, bf16[320,512]{1,0:T(8,128)(2,1)}, u32[]{:S(2)}) copy-start(bf16[320,512]{1,0:T(8,128)(2,1)} %copy-done.7) | copy-start | bytes 983044
  75.1 52.8 %copy-start.10 = (bf16[256,512]{1,0:T(8,128)(2,1)S(1)}, bf16[256,512]{1,0:T(8,128)(2,1)}, u32[]{:S(2)}) copy-start(bf16[256,512]{1,0:T(8,128)(2,1)} %copy-done.9) | copy-start | bytes 786436
  75.1 183.2 %all-reduce.4.cloned.1.call-start = ((), (), s32[]{:S(2)}) async-start(), calls=%async_computation.4 | async-start | bytes 524288 | tf_op jit(solution)/shard_map/psum | solution.py:161
  127.8 2.2 copy-start.13
  127.9 2.2 copy-start.23
  130.1 2.2 copy-start.6
  130.1 2.2 copy-start.21
  130.1 2.2 copy-start.22
  (4 other events, 4.1 us)
Sparse Core Ops, SparseCore 0:
  75.2 51.6 reduce-scatter.1
  133.9 124.3 all-reduce.3
where the time goes:
time: 267 us
  waiting for transfers between devices  118 us (44%)
  blocking collectives  92.6 us (35%)
  matrix products  16.3 us (6%)
  between operations  14.5 us (5%)
  other arithmetic  8.99 us (3%)
  local copies, waits for them, and re-layouts  8.77 us (3%)
  starting transfers between devices  8 us (3%)
    psum x1, blocking collectives, on_device(): lax.psum((local_in, local_out, local_bias), ('batch', 'tm'))  69.8 us
    psum x1, waiting for transfers between devices, on_device(): lax.psum((local_in, local_out, local_bias), ('batch', 'tm'))  54.8 us
    reduce_scatter x1, waiting for transfers between devices, on_device(): lax.psum_scatter(reciprocal_factor * jnp.einsum('rn,re->ne', weights, ref...  50.5 us
    all_gather x1, blocking collectives, on_device(): pool = lax.all_gather(neg_unit, 'batch', axis=0, tiled=True)  22.8 us
    all_to_all x1, waiting for transfers between devices, on_device(): lax.all_to_all(found, 'tm', split_axis=0, concat_axis=0, tiled=True)  12.3 us
  transfers between devices with their start and end apart: 4, of which 3 were waited for; matrix products, arithmetic and copies ran while one was open for 4% of the time, Pallas kernels for 0%

commit v1 on v0

v1 whole, which is shorter than its diff:
```python
import jax
import jax.numpy as jnp
from jax import lax
from jax.sharding import PartitionSpec as P

logit_sharpness_divisor = 0.1
shift_bound = 10.0
epsilon = 1e-06
AXES = ("batch", "tm")
bf16 = jnp.bfloat16
f32 = jnp.float32


def swap(x, axes, mask, n):
    return lax.ppermute(x, axes, [(i, i ^ mask) for i in range(n)])


def batch_masks(nb):
    return [1 << i for i in range(nb.bit_length() - 1)]


def gather_batch(x, nb, me):
    masks = batch_masks(nb)
    order = masks[2:][::-1] + masks[1:2] + masks[:1]
    rows = x.shape[0]
    parts = {0: x}
    for m in order:
        keys = list(parts)
        block = jnp.concatenate([parts[k] for k in keys], 0) if len(keys) > 1 else parts[keys[0]]
        got = swap(block, "batch", m, nb)
        for i, k in enumerate(keys):
            parts[k ^ m] = got[i * rows : (i + 1) * rows]
    out = jnp.zeros((nb,) + x.shape, x.dtype)
    for k, part in parts.items():
        out = lax.dynamic_update_index_in_dim(out, part, me ^ k, 0)
    return out.reshape((nb * rows,) + x.shape[1:])


def scatter_batch(x, nb, me):
    masks = batch_masks(nb)
    order = masks[:1] + masks[1:][::-1]
    xs = x.reshape((nb, x.shape[0] // nb) + x.shape[1:])
    parts = {k: lax.dynamic_index_in_dim(xs, me ^ k, 0, False) for k in range(nb)}
    for m in order:
        keep = [k for k in parts if not k & m]
        send = jnp.stack([parts[k ^ m] for k in keep], 0).astype(bf16)
        got = swap(send, "batch", m, nb)
        parts = {k: parts[k] + got[i].astype(f32) for i, k in enumerate(keep)}
    return parts[0]


def group_list(n, nt):
    bits = [1 << i for i in range(n.bit_length() - 1)]
    rest = [m for m in bits if m != nt]
    return [[nt]] + [rest[i : i + 2] for i in range(0, len(rest), 2)]


def members(group):
    found = [0]
    for m in group:
        found = found + [a ^ m for a in found]
    return found


def place(me, group):
    return sum(jnp.where((me & m) != 0, 1 << i, 0) for i, m in enumerate(group))


def all_sum(x, n, nt, me):
    done = []
    for group in group_list(n, nt):
        found = members(group)
        size = len(found)
        if x.shape[0] % (8 * size):
            terms = [x.astype(f32)] + [swap(x, AXES, m, n).astype(f32) for m in found[1:]]
            while len(terms) > 1:
                terms = [a + b for a, b in zip(terms[::2], terms[1::2])]
            x = terms[0].astype(bf16)
            continue
        h = x.shape[0] // size
        p = place(me, group)
        xs = x.reshape(size, h, x.shape[1])
        got = [
            swap(lax.dynamic_index_in_dim(xs, p ^ j, 0, False), AXES, found[j], n)
            for j in range(1, size)
        ]
        own = lax.dynamic_index_in_dim(xs, p, 0, False).astype(f32)
        x = sum((g.astype(f32) for g in got), own).astype(bf16)
        done.append((group, found, size, p))
    for group, found, size, p in reversed(done):
        out = jnp.zeros((size,) + x.shape, x.dtype)
        got = [x] + [swap(x, AXES, m, n) for m in found[1:]]
        for j in range(size):
            out = lax.dynamic_update_index_in_dim(out, got[j], p ^ j, 0)
        x = out.reshape(size * x.shape[0], x.shape[1])
    return x


def hot(ids, width, dtype):
    return (ids[:, None] == jnp.arange(width, dtype=jnp.int32)[None, :]).astype(dtype)


def encode(samples, animal_ids, w_in, bias_animal, w_out):
    one_hot = hot(animal_ids, bias_animal.shape[0], f32)
    pre_act = jnp.dot(samples, w_in, preferred_element_type=f32) + jnp.dot(
        one_hot, bias_animal, precision=lax.Precision.HIGHEST
    )
    hidden = jax.nn.gelu(pre_act).astype(bf16)
    latent = jnp.dot(hidden, w_out, preferred_element_type=f32)
    radius = jnp.sqrt(jnp.sum(latent * latent, axis=1, keepdims=True) + epsilon)
    return (pre_act, hidden, latent, radius, (latent / radius).astype(bf16))


def fetch_rows(recording, owner, row, nt, me_t):
    held = recording.shape[0]
    refs = row.shape[0]
    cap = min(refs, 2 * refs // nt)
    rows = jnp.dot(
        hot(jnp.where(owner == me_t, row, -1), held, bf16), recording, preferred_element_type=bf16
    )
    if cap < refs:
        owner_hot = hot(owner, nt, jnp.int32)
        slot = jnp.sum((jnp.cumsum(owner_hot, axis=0) - owner_hot) * owner_hot, axis=1)
    for k in range(1, nt):
        wanted = owner == (me_t ^ k)
        if cap < refs:
            pick = wanted[None, :] & (slot[None, :] == jnp.arange(cap, dtype=jnp.int32)[:, None])
            ask = jnp.max(jnp.where(pick, row[None, :], -1), axis=1)
        else:
            ask = jnp.where(wanted, row, -1)
        asked = swap(ask, "tm", k, nt)
        found = jnp.dot(hot(asked, held, bf16), recording, preferred_element_type=bf16)
        got = swap(found, "tm", k, nt)
        if cap < refs:
            got = jnp.dot(pick.T.astype(bf16), got, preferred_element_type=bf16)
        rows = rows + got
    return rows


def backward(animal_ids, enc, samples, grad_unit, w_out):
    pre_act, hidden, latent, radius, _ = enc
    inner = jnp.sum(latent * grad_unit, axis=1, keepdims=True)
    grad_latent = ((grad_unit - latent * inner / (radius * radius)) / radius).astype(bf16)
    grad_hidden = jnp.dot(grad_latent, w_out.T, preferred_element_type=f32)
    grad_pre = jax.vjp(jax.nn.gelu, pre_act)[1](grad_hidden)[0].astype(bf16)
    embed = w_out.shape[1]
    wide = jnp.concatenate([samples, hot(animal_ids, embed, bf16)], 1)
    top = lax.dot_general(wide, grad_pre, (((0,), (0,)), ((), ())), preferred_element_type=f32)
    low = lax.dot_general(grad_latent, hidden, (((0,), (0,)), ((), ())), preferred_element_type=f32)
    return jnp.concatenate([top, low], 0)


def on_device(
    ref_rows,
    neg_rows,
    recording,
    pos_owner,
    pos_row,
    ref_animal,
    neg_animal,
    w_in,
    bias_animal,
    w_out,
):
    refs = ref_rows.shape[0]
    channels = w_in.shape[0]
    embed = w_out.shape[1]
    animals = bias_animal.shape[0]
    nt = lax.axis_size("tm")
    nb = lax.axis_size("batch")
    n = nt * nb
    me_b = lax.axis_index("batch")
    me_t = lax.axis_index("tm")
    me = me_b * nt + me_t

    neg = encode(neg_rows, neg_animal, w_in, bias_animal, w_out)
    pos_rows = fetch_rows(recording, pos_owner[:, 0], pos_row, nt, me_t)
    pool = gather_batch(neg[4], nb, me_b)
    ref = encode(ref_rows, ref_animal, w_in, bias_animal, w_out)
    pos = encode(pos_rows, ref_animal, w_in, bias_animal, w_out)
    u, v = ref[4], pos[4]

    pos_score = jnp.sum(u.astype(f32) * v.astype(f32), axis=1) / logit_sharpness_divisor
    scores = (
        lax.dot_general(u, pool, (((1,), (1,)), ((), ())), preferred_element_type=f32)
        / logit_sharpness_divisor
    )
    exponent = jnp.exp(scores - shift_bound)
    pos_exp = jnp.exp(pos_score - shift_bound)
    normalizer = pos_exp + jnp.sum(exponent, axis=1)
    ref_loss = jnp.log(normalizer) + shift_bound - pos_score
    weights = (exponent / normalizer[:, None]).astype(bf16)
    pos_pull = (pos_exp / normalizer - 1.0)[:, None]
    scale = float(refs * n) ** (-0.5) / logit_sharpness_divisor
    share = scale * lax.dot_general(
        weights, u, (((0,), (0,)), ((), ())), preferred_element_type=f32
    )
    grad_neg = scatter_batch(share, nb, me_b)
    grad_ref = scale * (
        jnp.dot(weights, pool, preferred_element_type=f32) + pos_pull * v.astype(f32)
    )
    grad_pos = scale * pos_pull * u.astype(f32)

    both = tuple(jnp.concatenate([a, b], 0) for a, b in zip(ref, pos))
    total = backward(
        jnp.concatenate([ref_animal, ref_animal]),
        both,
        jnp.concatenate([ref_rows, pos_rows], 0),
        jnp.concatenate([grad_ref, grad_pos], 0),
        w_out,
    ) + backward(neg_animal, neg, neg_rows, grad_neg, w_out)
    total = all_sum(total.astype(bf16), n, nt, me)
    grad_w_in = total[:channels]
    grad_bias = total[channels : channels + animals].astype(f32)
    grad_w_out = total[channels + embed :].T.astype(f32)
    return (ref_loss, grad_w_in, grad_w_out, grad_bias)


def solution(mesh):
    in_specs = (
        P(("batch", "tm"), None),
        P(("batch", "tm"), None),
        P("tm", None),
        P(("batch", "tm"), None),
        P(("batch", "tm")),
        P(("batch", "tm")),
        P(("batch", "tm")),
        P(),
        P(),
        P(),
    )
    out_specs = (P(("batch", "tm")), P(), P(), P())
    return jax.shard_map(
        on_device, mesh=mesh, in_specs=in_specs, out_specs=out_specs, check_vma=False
    )
```

time: 267 us -> 106 us (0.40)
  blocking collectives: 92.6 us -> 0 us
  waiting for transfers between devices: 118 us -> 39 us
  starting transfers between devices: 8 us -> 28.1 us
  between operations: 14.5 us -> 1.36 us
  matrix products: 16.3 us -> 21 us
  local copies, waits for them, and re-layouts: 8.77 us -> 4.59 us
  other arithmetic: 8.99 us -> 11.7 us
    psum x1 -> x0, blocking collectives: 69.8 us -> none  [on_device(): lax.psum((local_in, local_out, local_bias), ('batch', 'tm'))]
    psum x1 -> x0, waiting for transfers between devices: 54.8 us -> none  [on_device(): lax.psum((local_in, local_out, local_bias), ('batch', 'tm'))]
    reduce_scatter x1 -> x0, waiting for transfers between devices: 50.5 us -> none  [on_device(): lax.psum_scatter(reciprocal_factor * jnp.einsum('rn,re->ne', weights, ref...]
    ppermute x0 -> x24, waiting for transfers between devices: none -> 39 us  [swap(): return lax.ppermute(x, axes, [(i, i ^ mask) for i in range(n)])]
    ppermute x0 -> x24, starting transfers between devices: none -> 28.1 us  [swap(): return lax.ppermute(x, axes, [(i, i ^ mask) for i in range(n)])]
    all_gather x1 -> x0, blocking collectives: 22.8 us -> none  [on_device(): pool = lax.all_gather(neg_unit, 'batch', axis=0, tiled=True)]
    all_to_all x2 -> x0, waiting for transfers between devices: 12.3 us -> none  [the longest x1 12.3 us: on_device(): lax.all_to_all(found, 'tm', split_axis=0, concat_axis=0, tiled=True)]
    all_to_all x2 -> x0, starting transfers between devices: 7.92 us -> none  [the longest x1 4.21 us: on_device(): lax.all_to_all(requests, 'tm', split_axis=0, concat_axis=0, tiled=True)]
  transfers between devices with their start and end apart: 4 -> 24, of which waited for: 3 -> 18; matrix products, arithmetic and copies ran while one was open for 4% -> 14% of each run, Pallas kernels for 0% -> 0%
where the time goes in v1:
time: 106 us
  waiting for transfers between devices  39 us (37%)
  starting transfers between devices  28.1 us (27%)
  matrix products  21 us (20%)
  other arithmetic  11.7 us (11%)
  local copies, waits for them, and re-layouts  4.59 us (4%)
  between operations  1.36 us (1%)
    ppermute x24, waiting for transfers between devices, swap(): return lax.ppermute(x, axes, [(i, i ^ mask) for i in range(n)])  39 us
    ppermute x24, starting transfers between devices, swap(): return lax.ppermute(x, axes, [(i, i ^ mask) for i in range(n)])  28.1 us
    dot_general x2, matrix products, backward(): lax.dot_general(wide, grad_pre, (((0,), (0,)), ((), ())), preferred_eleme...  6.14 us
    dot_general x3, matrix products, encode(): jnp.dot(samples, w_in, preferred_element_type=f32)  5.78 us
    dot_general x2, matrix products, backward(): lax.dot_general(grad_latent, hidden, (((0,), (0,)), ((), ())), preferred_...  3.78 us
    unnamed x54, local copies, waits for them, and re-layouts  2.89 us
    convert_element_type x1, other arithmetic, on_device(): total = all_sum(total.astype(bf16), n, nt, me)  2.21 us
  transfers between devices with their start and end apart: 24, of which 18 were waited for; matrix products, arithmetic and copies ran while one was open for 14% of the time, Pallas kernels for 0%

profile of v1, /device:TPU:0, one launch (start us, length us, event | category | flops | bytes accessed | tf_op | source)
XLA Modules:
  0.0 105.7 jit_solution(7826555010497192246)
XLA Ops:
  2.0 1.9 %convolution_add_fusion.3 = f32[64,512]{1,0:T(8,128)} fusion(f32[64,512]{1,0:T(8,128)S(1)} %fusion.82, bf16[64,1024]{1,0:T(8,128)(2,1)} %param.11, bf16[1024,512]{1,0:T(8,128)(2,1)S(1)} %copy-done), kind=kOutput, calls=%fused_computation.20 | convolution fusion | flops 67141632 | bytes 1441792 | tf_op jit(solution)/shard_map/dot_general | solution.py:105
  5.7 4.1 %collective-permute-start.2 = (bf16[64,128]{1,0:T(8,128)(2,1)S(1)}, bf16[64,128]{1,0:T(8,128)(2,1)S(1)}, u32[]{:S(2)}, u32[]{:S(2)}) collective-permute-start(bf16[64,128]{1,0:T(8,128)(2,1)S(1)} %get-tuple-element.21), channel_id=1, source_target_pairs={{0,16},{2,18},{4,20},{6,22},{8,24},{10,26},{12,28},{14,30},{16,0},... | collective-permute-start | bytes 49160 | tf_op jit(solution)/shard_map/ppermute | solution.py:15
  11.9 2.6 %fusion.28 = (bf16[256,512]{1,0:T(8,128)(2,1)S(1)}, f32[256,512]{1,0:T(8,128)}) fusion(f32[256,512]{1,0:T(8,128)S(1)} %fusion.67, bf16[256,1024]{1,0:T(8,128)(2,1)} %param.10, bf16[1024,512]{1,0:T(8,128)(2,1)S(1)} %copy-done), kind=kOutput, calls=%fused_computation.44 | convolution fusion | flops 269746176 | bytes 2883584 | tf_op jit(solution)/shard_map/dot_general | solution.py:105
  19.5 2.3 %collective-permute-done.3 = bf16[128,128]{1,0:T(8,128)(2,1)S(1)} collective-permute-done((bf16[128,128]{1,0:T(8,128)(2,1)S(1)}, bf16[128,128]{1,0:T(8,128)(2,1)S(1)}, u32[]{:S(2)}, u32[]{:S(2)}) %collective-permute-start.3) | collective-permute-done | bytes 32800 | tf_op jit(solution)/shard_map/ppermute | solution.py:15
  23.4 2.7 %collective-permute-done.4 = bf16[256,128]{1,0:T(8,128)(2,1)S(1)} collective-permute-done((bf16[256,128]{1,0:T(8,128)(2,1)S(1)}, bf16[256,128]{1,0:T(8,128)(2,1)S(1)}, u32[]{:S(2)}, u32[]{:S(2)}) %collective-permute-start.4) | collective-permute-done | bytes 65568 | tf_op jit(solution)/shard_map/ppermute | solution.py:15
  27.6 2.8 %collective-permute-done.1 = bf16[256,1024]{1,0:T(8,128)(2,1)S(1)} collective-permute-done((bf16[256,1024]{1,0:T(8,128)(2,1)S(1)}, bf16[256,1024]{1,0:T(8,128)(2,1)S(1)}, u32[]{:S(2)}, u32[]{:S(2)}) %collective-permute-start.1) | collective-permute-done | bytes 524320 | tf_op jit(solution)/shard_map/ppermute | solution.py:15
  37.4 5.6 %collective-permute-done.7 = bf16[4,64,128]{2,1,0:T(8,128)(2,1)S(1)} collective-permute-done((bf16[4,64,128]{2,1,0:T(8,128)(2,1)S(1)}, bf16[4,64,128]{2,1,0:T(8,128)(2,1)S(1)}, u32[]{:S(2)}, u32[]{:S(2)}) %collective-permute-start.7) | collective-permute-done | bytes 65568 | tf_op jit(solution)/shard_map/ppermute | solution.py:15
  43.9 4.4 %fusion.4 = f32[1152,512]{1,0:T(8,128)} fusion(bf16[512,128]{1,0:T(8,128)(2,1)S(1)} %copy-done.10, bf16[256,1024]{1,0:T(8,128)(2,1)S(1)} %add.335, bf16[256,1024]{1,0:T(8,128)(2,1)} %param.10, bf16[512,128]{1,0:T(8,128)(2,1)S(1)} %copy-done.3, f32[256,512]{1,0:T(8,128)} %get-tuple-element.50, f32[256,512]{1,0:T(8,128)} %get-tuple-element.46, ...), kind=kOutput, calls=%fused_computation.12 | convolution fusion | flops 680591360 | bytes 5249024 | tf_op jit(solution)/shard_map/dot_general | solution.py:148
  50.7 1.9 %fusion.37 = f32[128,512]{1,0:T(8,128)} fusion(bf16[256,512]{1,0:T(8,128)(2,1)S(1)} %get-tuple-element.49, bf16[256,512]{1,0:T(8,128)(2,1)S(1)} %copy-done.8, f32[256,128]{1,0:T(8,128)S(1)} %get-tuple-element.52, f32[256,128]{1,0:T(8,128)S(1)} %get-tuple-element.48, f32[256,128]{1,0:T(8,128)S(1)} %convert_multiply_fusion.2, f32[256,128]{1,0:T(8,128)S(1)} %fusion.10, ...), kind=kOutput, calls=%fused_computation.53 | convolution fusion | flops 68616192 | bytes 1316864 | tf_op jit(solution)/shard_map/dot_general | solution.py:149
  54.4 1.9 %fusion.117 = f32[128,512]{1,0:T(8,128)} fusion(f32[64,512]{1,0:T(8,128)} %convolution_add_fusion.3, f32[1,64,128]{2,1,0:T(8,128)S(1)} %get-tuple-element.17, f32[64,128]{1,0:T(8,128)S(1)} %get-tuple-element.54, f32[64]{0:T(128)S(1)} %copy-done.22, f32[64]{0:T(128)S(1)} %get-tuple-element.16, f32[64]{0:T(128)S(1)} %copy-done.18), kind=kOutput, calls=%fused_computation.233 | convolution fusion | flops 8724480 | bytes 459520 | tf_op jit(solution)/shard_map/dot_general | solution.py:149
  56.3 1.7 %fusion.55 = f32[1152,512]{1,0:T(8,128)S(1)} fusion(bf16[64,128]{1,0:T(8,128)(2,1)S(1)} %fusion.83, bf16[64,1024]{1,0:T(8,128)(2,1)} %param.11, f32[64,512]{1,0:T(8,128)} %convolution_add_fusion.3, bf16[512,128]{1,0:T(8,128)(2,1)S(1)} %copy-done.3, f32[1,64,128]{2,1,0:T(8,128)} %copy-done.9, f32[64,128]{1,0:T(8,128)} %copy-done.6, ...), kind=kOutput, calls=%fused_computation.92 | convolution fusion | flops 84877312 | bytes 2835200 | tf_op jit(solution)/shard_map/dot_general | solution.py:148
  58.0 2.2 %fusion = bf16[1280,512]{1,0:T(8,128)(2,1)S(1)} fusion(f32[128,512]{1,0:T(8,128)} %fusion.37, f32[1152,512]{1,0:T(8,128)} %fusion.4, f32[128,512]{1,0:T(8,128)} %fusion.117, f32[1152,512]{1,0:T(8,128)S(1)} %fusion.55), kind=kLoop, calls=%fused_computation.1 | loop fusion | flops 2621440 | bytes 6553600 | tf_op jit(solution)/shard_map/convert_element_type | solution.py:212
  61.4 2.1 %collective-permute-done.10 = bf16[640,512]{1,0:T(8,128)(2,1)S(1)} collective-permute-done((bf16[640,512]{1,0:T(8,128)(2,1)S(1)}, bf16[640,512]{1,0:T(8,128)(2,1)S(1)}, u32[]{:S(2)}, u32[]{:S(2)}) %collective-permute-start.10) | collective-permute-done | bytes 655392 | tf_op jit(solution)/shard_map/ppermute | solution.py:15
  68.4 3.6 %collective-permute-done.11 = bf16[160,512]{1,0:T(8,128)(2,1)S(1)} collective-permute-done((bf16[160,512]{1,0:T(8,128)(2,1)S(1)}, bf16[160,512]{1,0:T(8,128)(2,1)S(1)}, u32[]{:S(2)}, u32[]{:S(2)}) %collective-permute-start.11) | collective-permute-done | bytes 163872 | tf_op jit(solution)/shard_map/ppermute | solution.py:15
  71.9 2.1 %collective-permute-done.12 = bf16[160,512]{1,0:T(8,128)(2,1)S(1)} collective-permute-done((bf16[160,512]{1,0:T(8,128)(2,1)S(1)}, bf16[160,512]{1,0:T(8,128)(2,1)S(1)}, u32[]{:S(2)}, u32[]{:S(2)}) %collective-permute-start.12) | collective-permute-done | bytes 163872 | tf_op jit(solution)/shard_map/ppermute | solution.py:15
  74.0 1.6 %collective-permute-done.13 = bf16[160,512]{1,0:T(8,128)(2,1)S(1)} collective-permute-done((bf16[160,512]{1,0:T(8,128)(2,1)S(1)}, bf16[160,512]{1,0:T(8,128)(2,1)S(1)}, u32[]{:S(2)}, u32[]{:S(2)}) %collective-permute-start.13) | collective-permute-done | bytes 163872 | tf_op jit(solution)/shard_map/ppermute | solution.py:15
  75.7 1.8 %collective-permute-start.14 = (bf16[40,512]{1,0:T(8,128)(2,1)S(1)}, bf16[40,512]{1,0:T(8,128)(2,1)S(1)}, u32[]{:S(2)}, u32[]{:S(2)}) collective-permute-start(bf16[40,512]{1,0:T(8,128)(2,1)S(1)} %get-tuple-element.34), channel_id=1, source_target_pairs={{0,8},{1,9},{2,10},{3,11},{4,12},{5,13},{6,14},{7,15},{8,0},{9,1},... | collective-permute-start | bytes 122888 | tf_op jit(solution)/shard_map/ppermute | solution.py:15
  77.6 2.5 %collective-permute-start.16 = (bf16[40,512]{1,0:T(8,128)(2,1)S(1)}, bf16[40,512]{1,0:T(8,128)(2,1)S(1)}, u32[]{:S(2)}, u32[]{:S(2)}) collective-permute-start(bf16[40,512]{1,0:T(8,128)(2,1)S(1)} %get-tuple-element.35), channel_id=1, source_target_pairs={{0,24},{1,25},{2,26},{3,27},{4,28},{5,29},{6,30},{7,31},{8,16},{9,... | collective-permute-start | bytes 122888 | tf_op jit(solution)/shard_map/ppermute | solution.py:15
  80.2 2.4 %collective-permute-done.15 = bf16[40,512]{1,0:T(8,128)(2,1)S(1)} collective-permute-done((bf16[40,512]{1,0:T(8,128)(2,1)S(1)}, bf16[40,512]{1,0:T(8,128)(2,1)S(1)}, u32[]{:S(2)}, u32[]{:S(2)}) %collective-permute-start.15) | collective-permute-done | bytes 40992 | tf_op jit(solution)/shard_map/ppermute | solution.py:15
  83.7 2.9 %collective-permute-start.18 = (bf16[40,512]{1,0:T(8,128)(2,1)S(1)}, bf16[40,512]{1,0:T(8,128)(2,1)S(1)}, u32[]{:S(2)}, u32[]{:S(2)}) collective-permute-start(bf16[40,512]{1,0:T(8,128)(2,1)S(1)} %get-tuple-element.15), channel_id=1, source_target_pairs={{0,16},{1,17},{2,18},{3,19},{4,20},{5,21},{6,22},{7,23},{8,24},{9,... | collective-permute-start | bytes 122888 | tf_op jit(solution)/shard_map/ppermute | solution.py:15
  88.7 3.8 %collective-permute-done.19 = bf16[40,512]{1,0:T(8,128)(2,1)S(1)} collective-permute-done((bf16[40,512]{1,0:T(8,128)(2,1)S(1)}, bf16[40,512]{1,0:T(8,128)(2,1)S(1)}, u32[]{:S(2)}, u32[]{:S(2)}) %collective-permute-start.19) | collective-permute-done | bytes 40992 | tf_op jit(solution)/shard_map/ppermute | solution.py:15
  96.0 1.7 %collective-permute-done.20 = bf16[160,512]{1,0:T(8,128)(2,1)S(1)} collective-permute-done((bf16[160,512]{1,0:T(8,128)(2,1)S(1)}, bf16[160,512]{1,0:T(8,128)(2,1)S(1)}, u32[]{:S(2)}, u32[]{:S(2)}) %collective-permute-start.20) | collective-permute-done | bytes 163872 | tf_op jit(solution)/shard_map/ppermute | solution.py:15
  97.8 1.6 %collective-permute-done.21 = bf16[160,512]{1,0:T(8,128)(2,1)S(1)} collective-permute-done((bf16[160,512]{1,0:T(8,128)(2,1)S(1)}, bf16[160,512]{1,0:T(8,128)(2,1)S(1)}, u32[]{:S(2)}, u32[]{:S(2)}) %collective-permute-start.21) | collective-permute-done | bytes 163872 | tf_op jit(solution)/shard_map/ppermute | solution.py:15
  101.3 1.9 %collective-permute-done.23 = bf16[640,512]{1,0:T(8,128)(2,1)S(1)} collective-permute-done((bf16[640,512]{1,0:T(8,128)(2,1)S(1)}, bf16[640,512]{1,0:T(8,128)(2,1)S(1)}, u32[]{:S(2)}, u32[]{:S(2)}) %collective-permute-start.23) | collective-permute-done | bytes 655392 | tf_op jit(solution)/shard_map/ppermute | solution.py:15
  (160 shorter events, 42.2 us)
Async XLA Ops:
  5.7 12.2 %collective-permute-start.2 = (bf16[64,128]{1,0:T(8,128)(2,1)S(1)}, bf16[64,128]{1,0:T(8,128)(2,1)S(1)}, u32[]{:S(2)}, u32[]{:S(2)}) collective-permute-start(bf16[64,128]{1,0:T(8,128)(2,1)S(1)} %get-tuple-element.21), channel_id=1, source_target_pairs={{0,16},{2,18},{4,20},{6,22},{8,24},{10,26},{12,28},{14,30},{16,0},... | collective-permute-start | bytes 49160 | tf_op jit(solution)/shard_map/ppermute | solution.py:15
  9.8 6.9 %collective-permute-start = (s32[256]{0:T(256)S(1)}, s32[256]{0:T(256)S(1)}, u32[]{:S(2)}, u32[]{:S(2)}) collective-permute-start(s32[256]{0:T(256)S(1)} %get-tuple-element.41), channel_id=1, source_target_pairs={{0,1},{1,0},{2,3},{3,2},{4,5},{5,4},{6,7},{7,6},{8,9},{9,8},{10,11... | collective-permute-start | bytes 3080 | tf_op jit(solution)/shard_map/ppermute | solution.py:15
  17.3 13.2 %collective-permute-start.1 = (bf16[256,1024]{1,0:T(8,128)(2,1)S(1)}, bf16[256,1024]{1,0:T(8,128)(2,1)S(1)}, u32[]{:S(2)}, u32[]{:S(2)}) collective-permute-start(bf16[256,1024]{1,0:T(8,128)(2,1)S(1)} %fusion.48), channel_id=1, source_target_pairs={{0,1},{1,0},{2,3},{3,2},{4,5},{5,4},{6,7},{7,6},{8,9},{9,8},{10,11... | collective-permute-start | bytes 1572872 | tf_op jit(solution)/shard_map/ppermute | solution.py:15
  17.9 3.9 %collective-permute-start.3 = (bf16[128,128]{1,0:T(8,128)(2,1)S(1)}, bf16[128,128]{1,0:T(8,128)(2,1)S(1)}, u32[]{:S(2)}, u32[]{:S(2)}) collective-permute-start(bf16[128,128]{1,0:T(8,128)(2,1)S(1)} %pad_maximum_fusion.7), channel_id=1, source_target_pairs={{0,8},{2,10},{4,12},{6,14},{8,0},{10,2},{12,4},{14,6},{16,24},{18,... | collective-permute-start | bytes 98312 | tf_op jit(solution)/shard_map/ppermute | solution.py:15
  21.8 4.3 %collective-permute-start.4 = (bf16[256,128]{1,0:T(8,128)(2,1)S(1)}, bf16[256,128]{1,0:T(8,128)(2,1)S(1)}, u32[]{:S(2)}, u32[]{:S(2)}) collective-permute-start(bf16[256,128]{1,0:T(8,128)(2,1)S(1)} %pad_maximum_fusion.5), channel_id=1, source_target_pairs={{0,4},{2,6},{4,0},{6,2},{8,12},{10,14},{12,8},{14,10},{16,20},{18,... | collective-permute-start | bytes 196616 | tf_op jit(solution)/shard_map/ppermute | solution.py:15
  26.1 1.4 %collective-permute-start.5 = (bf16[512,128]{1,0:T(8,128)(2,1)S(1)}, bf16[512,128]{1,0:T(8,128)(2,1)S(1)}, u32[]{:S(2)}, u32[]{:S(2)}) collective-permute-start(bf16[512,128]{1,0:T(8,128)(2,1)S(1)} %pad_maximum_fusion.4), channel_id=1, source_target_pairs={{0,2},{2,0},{4,6},{6,4},{8,10},{10,8},{12,14},{14,12},{16,18},{18,... | collective-permute-start | bytes 393224 | tf_op jit(solution)/shard_map/ppermute | solution.py:15
  34.3 1.8 %collective-permute-start.6 = (bf16[8,64,128]{2,1,0:T(8,128)(2,1)S(1)}, bf16[8,64,128]{2,1,0:T(8,128)(2,1)S(1)}, u32[]{:S(2)}, u32[]{:S(2)}) collective-permute-start(bf16[8,64,128]{2,1,0:T(8,128)(2,1)S(1)} %constant_dynamic-update-slice_fusion), channel_id=1, source_target_pairs={{0,2},{2,0},{4,6},{6,4},{8,10},{10,8},{12,14},{14,12},{16,18},{18,... | collective-permute-start | bytes 393224 | tf_op jit(solution)/shard_map/ppermute | solution.py:15
  36.1 6.9 %collective-permute-start.7 = (bf16[4,64,128]{2,1,0:T(8,128)(2,1)S(1)}, bf16[4,64,128]{2,1,0:T(8,128)(2,1)S(1)}, u32[]{:S(2)}, u32[]{:S(2)}) collective-permute-start(bf16[4,64,128]{2,1,0:T(8,128)(2,1)S(1)} %pad_maximum_fusion.6), channel_id=1, source_target_pairs={{0,16},{2,18},{4,20},{6,22},{8,24},{10,26},{12,28},{14,30},{16,0},... | collective-permute-start | bytes 196616 | tf_op jit(solution)/shard_map/ppermute | solution.py:15
  43.6 4.7 %collective-permute-start.8 = (bf16[2,64,128]{2,1,0:T(8,128)(2,1)}, bf16[2,64,128]{2,1,0:T(8,128)(2,1)S(1)}, u32[]{:S(2)}, u32[]{:S(2)}) collective-permute-start(bf16[2,64,128]{2,1,0:T(8,128)(2,1)} %pad_maximum_fusion.8), channel_id=1, source_target_pairs={{0,8},{2,10},{4,12},{6,14},{8,0},{10,2},{12,4},{14,6},{16,24},{18,... | collective-permute-start | bytes 98312 | tf_op jit(solution)/shard_map/ppermute | solution.py:15
  49.1 3.8 %collective-permute-start.9 = (bf16[1,64,128]{2,1,0:T(8,128)(2,1)S(1)}, bf16[1,64,128]{2,1,0:T(8,128)(2,1)S(1)}, u32[]{:S(2)}, u32[]{:S(2)}) collective-permute-start(bf16[1,64,128]{2,1,0:T(8,128)(2,1)S(1)} %add_convert_fusion), channel_id=1, source_target_pairs={{0,4},{2,6},{4,0},{6,2},{8,12},{10,14},{12,8},{14,10},{16,20},{18,... | collective-permute-start | bytes 49160 | tf_op jit(solution)/shard_map/ppermute | solution.py:15
  61.3 2.2 %collective-permute-start.10 = (bf16[640,512]{1,0:T(8,128)(2,1)S(1)}, bf16[640,512]{1,0:T(8,128)(2,1)S(1)}, u32[]{:S(2)}, u32[]{:S(2)}) collective-permute-start(bf16[640,512]{1,0:T(8,128)(2,1)S(1)} %dynamic-slice_bitcast_fusion), channel_id=1, source_target_pairs={{0,2},{1,3},{2,0},{3,1},{4,6},{5,7},{6,4},{7,5},{8,10},{9,11},{10,... | collective-permute-start | bytes 1966088 | tf_op jit(solution)/shard_map/ppermute | solution.py:15
  64.8 7.1 %collective-permute-start.11 = (bf16[160,512]{1,0:T(8,128)(2,1)S(1)}, bf16[160,512]{1,0:T(8,128)(2,1)S(1)}, u32[]{:S(2)}, u32[]{:S(2)}) collective-permute-start(bf16[160,512]{1,0:T(8,128)(2,1)S(1)} %get-tuple-element.27), channel_id=1, source_target_pairs={{0,1},{1,0},{2,3},{3,2},{4,5},{5,4},{6,7},{7,6},{8,9},{9,8},{10,11... | collective-permute-start | bytes 491528 | tf_op jit(solution)/shard_map/ppermute | solution.py:15
  65.4 8.5 %collective-permute-start.12 = (bf16[160,512]{1,0:T(8,128)(2,1)S(1)}, bf16[160,512]{1,0:T(8,128)(2,1)S(1)}, u32[]{:S(2)}, u32[]{:S(2)}) collective-permute-start(bf16[160,512]{1,0:T(8,128)(2,1)S(1)} %get-tuple-element.29), channel_id=1, source_target_pairs={{0,4},{1,5},{2,6},{3,7},{4,0},{5,1},{6,2},{7,3},{8,12},{9,13},{10,... | collective-permute-start | bytes 491528 | tf_op jit(solution)/shard_map/ppermute | solution.py:15
  67.0 8.6 %collective-permute-start.13 = (bf16[160,512]{1,0:T(8,128)(2,1)S(1)}, bf16[160,512]{1,0:T(8,128)(2,1)S(1)}, u32[]{:S(2)}, u32[]{:S(2)}) collective-permute-start(bf16[160,512]{1,0:T(8,128)(2,1)S(1)} %get-tuple-element.28), channel_id=1, source_target_pairs={{0,5},{1,4},{2,7},{3,6},{4,1},{5,0},{6,3},{7,2},{8,13},{9,12},{10,... | collective-permute-start | bytes 491528 | tf_op jit(solution)/shard_map/ppermute | solution.py:15
  75.7 4.5 %collective-permute-start.14 = (bf16[40,512]{1,0:T(8,128)(2,1)S(1)}, bf16[40,512]{1,0:T(8,128)(2,1)S(1)}, u32[]{:S(2)}, u32[]{:S(2)}) collective-permute-start(bf16[40,512]{1,0:T(8,128)(2,1)S(1)} %get-tuple-element.34), channel_id=1, source_target_pairs={{0,8},{1,9},{2,10},{3,11},{4,12},{5,13},{6,14},{7,15},{8,0},{9,1},... | collective-permute-start | bytes 122888 | tf_op jit(solution)/shard_map/ppermute | solution.py:15
  77.5 5.0 %collective-permute-start.15 = (bf16[40,512]{1,0:T(8,128)(2,1)S(1)}, bf16[40,512]{1,0:T(8,128)(2,1)S(1)}, u32[]{:S(2)}, u32[]{:S(2)}) collective-permute-start(bf16[40,512]{1,0:T(8,128)(2,1)S(1)} %get-tuple-element.36), channel_id=1, source_target_pairs={{0,16},{1,17},{2,18},{3,19},{4,20},{5,21},{6,22},{7,23},{8,24},{9,... | collective-permute-start | bytes 122888 | tf_op jit(solution)/shard_map/ppermute | solution.py:15
  77.6 5.8 %collective-permute-start.16 = (bf16[40,512]{1,0:T(8,128)(2,1)S(1)}, bf16[40,512]{1,0:T(8,128)(2,1)S(1)}, u32[]{:S(2)}, u32[]{:S(2)}) collective-permute-start(bf16[40,512]{1,0:T(8,128)(2,1)S(1)} %get-tuple-element.35), channel_id=1, source_target_pairs={{0,24},{1,25},{2,26},{3,27},{4,28},{5,29},{6,30},{7,31},{8,16},{9,... | collective-permute-start | bytes 122888 | tf_op jit(solution)/shard_map/ppermute | solution.py:15
  83.5 4.5 %collective-permute-start.17 = (bf16[40,512]{1,0:T(8,128)(2,1)S(1)}, bf16[40,512]{1,0:T(8,128)(2,1)S(1)}, u32[]{:S(2)}, u32[]{:S(2)}) collective-permute-start(bf16[40,512]{1,0:T(8,128)(2,1)S(1)} %get-tuple-element.15), channel_id=1, source_target_pairs={{0,8},{1,9},{2,10},{3,11},{4,12},{5,13},{6,14},{7,15},{8,0},{9,1},... | collective-permute-start | bytes 122888 | tf_op jit(solution)/shard_map/ppermute | solution.py:15
  83.7 4.9 %collective-permute-start.18 = (bf16[40,512]{1,0:T(8,128)(2,1)S(1)}, bf16[40,512]{1,0:T(8,128)(2,1)S(1)}, u32[]{:S(2)}, u32[]{:S(2)}) collective-permute-start(bf16[40,512]{1,0:T(8,128)(2,1)S(1)} %get-tuple-element.15), channel_id=1, source_target_pairs={{0,16},{1,17},{2,18},{3,19},{4,20},{5,21},{6,22},{7,23},{8,24},{9,... | collective-permute-start | bytes 122888 | tf_op jit(solution)/shard_map/ppermute | solution.py:15
  86.7 5.8 %collective-permute-start.19 = (bf16[40,512]{1,0:T(8,128)(2,1)S(1)}, bf16[40,512]{1,0:T(8,128)(2,1)S(1)}, u32[]{:S(2)}, u32[]{:S(2)}) collective-permute-start(bf16[40,512]{1,0:T(8,128)(2,1)S(1)} %get-tuple-element.15), channel_id=1, source_target_pairs={{0,24},{1,25},{2,26},{3,27},{4,28},{5,29},{6,30},{7,31},{8,16},{9,... | collective-permute-start | bytes 122888 | tf_op jit(solution)/shard_map/ppermute | solution.py:15
  92.5 5.3 %collective-permute-start.20 = (bf16[160,512]{1,0:T(8,128)(2,1)S(1)}, bf16[160,512]{1,0:T(8,128)(2,1)S(1)}, u32[]{:S(2)}, u32[]{:S(2)}) collective-permute-start(bf16[160,512]{1,0:T(8,128)(2,1)S(1)} %bitcast.180), channel_id=1, source_target_pairs={{0,1},{1,0},{2,3},{3,2},{4,5},{5,4},{6,7},{7,6},{8,9},{9,8},{10,11... | collective-permute-start | bytes 491528 | tf_op jit(solution)/shard_map/ppermute | solution.py:15
  93.3 6.2 %collective-permute-start.21 = (bf16[160,512]{1,0:T(8,128)(2,1)S(1)}, bf16[160,512]{1,0:T(8,128)(2,1)S(1)}, u32[]{:S(2)}, u32[]{:S(2)}) collective-permute-start(bf16[160,512]{1,0:T(8,128)(2,1)S(1)} %bitcast.181), channel_id=1, source_target_pairs={{0,4},{1,5},{2,6},{3,7},{4,0},{5,1},{6,2},{7,3},{8,12},{9,13},{10,... | collective-permute-start | bytes 491528 | tf_op jit(solution)/shard_map/ppermute | solution.py:15
  94.8 6.2 %collective-permute-start.22 = (bf16[160,512]{1,0:T(8,128)(2,1)S(1)}, bf16[160,512]{1,0:T(8,128)(2,1)S(1)}, u32[]{:S(2)}, u32[]{:S(2)}) collective-permute-start(bf16[160,512]{1,0:T(8,128)(2,1)S(1)} %bitcast.182), channel_id=1, source_target_pairs={{0,5},{1,4},{2,7},{3,6},{4,1},{5,0},{6,3},{7,2},{8,13},{9,12},{10,... | collective-permute-start | bytes 491528 | tf_op jit(solution)/shard_map/ppermute | solution.py:15
  101.0 2.2 %collective-permute-start.23 = (bf16[640,512]{1,0:T(8,128)(2,1)S(1)}, bf16[640,512]{1,0:T(8,128)(2,1)S(1)}, u32[]{:S(2)}, u32[]{:S(2)}) collective-permute-start(bf16[640,512]{1,0:T(8,128)(2,1)S(1)} %bitcast.164), channel_id=1, source_target_pairs={{0,2},{1,3},{2,0},{3,1},{4,6},{5,7},{6,4},{7,5},{8,10},{9,11},{10,... | collective-permute-start | bytes 1966088 | tf_op jit(solution)/shard_map/ppermute | solution.py:15
  (23 other events, 174.3 us)

commit v2 on v1

v2 whole, which is shorter than its diff:
```python
import functools

import jax
import jax.numpy as jnp
from jax import lax
from jax.experimental import pallas as pl
from jax.experimental.pallas import tpu as pltpu
from jax.sharding import PartitionSpec as P

logit_sharpness_divisor = 0.1
shift_bound = 10.0
epsilon = 1e-06
AXES = ("batch", "tm")
bf16 = jnp.bfloat16
f32 = jnp.float32


def swap(x, axes, mask, n):
    return lax.ppermute(x, axes, [(i, i ^ mask) for i in range(n)])


def batch_masks(nb):
    return [1 << i for i in range(nb.bit_length() - 1)]


def gather_batch(x, nb, me):
    masks = batch_masks(nb)
    order = masks[2:][::-1] + masks[1:2] + masks[:1]
    rows = x.shape[0]
    parts = {0: x}
    for m in order:
        keys = list(parts)
        block = jnp.concatenate([parts[k] for k in keys], 0) if len(keys) > 1 else parts[keys[0]]
        got = swap(block, "batch", m, nb)
        for i, k in enumerate(keys):
            parts[k ^ m] = got[i * rows : (i + 1) * rows]
    out = jnp.zeros((nb,) + x.shape, x.dtype)
    for k, part in parts.items():
        out = lax.dynamic_update_index_in_dim(out, part, me ^ k, 0)
    return out.reshape((nb * rows,) + x.shape[1:])


def scatter_batch(x, nb, me, total):
    masks = batch_masks(nb)
    order = masks[:1] + masks[1:][::-1]
    xs = x.reshape((nb, x.shape[0] // nb) + x.shape[1:])
    parts = {k: lax.dynamic_index_in_dim(xs, me ^ k, 0, False) for k in range(nb)}
    for step, m in enumerate(order):
        keep = [k for k in parts if not k & m]
        send = jnp.stack([parts[k ^ m] for k in keep], 0).astype(bf16)
        if step == 2:
            send, total = lax.optimization_barrier((send, total))
        got = swap(send, "batch", m, nb)
        if len(keep) == 1:
            return parts[0], got[0], total
        parts = {k: parts[k] + got[i].astype(f32) for i, k in enumerate(keep)}


def group_list(n, nt):
    bits = [1 << i for i in range(n.bit_length() - 1)]
    rest = [m for m in bits if m != nt]
    return [[nt]] + [rest[i : i + 2] for i in range(0, len(rest), 2)]


def members(group):
    found = [0]
    for m in group:
        found = found + [a ^ m for a in found]
    return found


def place(me, group):
    return sum(jnp.where((me & m) != 0, 1 << i, 0) for i, m in enumerate(group))


def all_sum(x, n, nt, me):
    done = []
    for group in group_list(n, nt):
        found = members(group)
        size = len(found)
        if x.shape[0] % (8 * size):
            terms = [x.astype(f32)] + [swap(x, AXES, m, n).astype(f32) for m in found[1:]]
            while len(terms) > 1:
                terms = [a + b for a, b in zip(terms[::2], terms[1::2])]
            x = terms[0].astype(bf16)
            continue
        h = x.shape[0] // size
        p = place(me, group)
        xs = x.reshape(size, h, x.shape[1])
        got = [
            swap(lax.dynamic_index_in_dim(xs, p ^ j, 0, False), AXES, found[j], n)
            for j in range(1, size)
        ]
        own = lax.dynamic_index_in_dim(xs, p, 0, False).astype(f32)
        x = sum((g.astype(f32) for g in got), own).astype(bf16)
        done.append((group, found, size, p))
    for group, found, size, p in reversed(done[1:]):
        out = jnp.zeros((size,) + x.shape, x.dtype)
        got = [x] + [swap(x, AXES, m, n) for m in found[1:]]
        for j in range(size):
            out = lax.dynamic_update_index_in_dim(out, got[j], p ^ j, 0)
        x = out.reshape(size * x.shape[0], x.shape[1])
    return x, swap(x, AXES, nt, n)


def hot(ids, width, dtype):
    return (ids[:, None] == jnp.arange(width, dtype=jnp.int32)[None, :]).astype(dtype)


def nt_dot(a, b):
    return lax.dot_general(a, b, (((1,), (1,)), ((), ())), preferred_element_type=f32)


def tn_dot(a, b):
    return lax.dot_general(a, b, (((0,), (0,)), ((), ())), preferred_element_type=f32)


def hot_columns(ids, width):
    found = lax.broadcasted_iota(jnp.int32, (width, ids.shape[1]), 0) == ids
    return jnp.where(found, 1.0, 0.0).astype(bf16)


def gelu_pair(x):
    c = 0.7978845608028654
    square = x * x
    t = jnp.tanh(c * (x + 0.044715 * (square * x)))
    half = 0.5 * (1.0 + t)
    slope = half + (0.5 * x) * ((1.0 - t) * (1.0 + t)) * (c + (3.0 * 0.044715 * c) * square)
    return (x * half).astype(bf16), slope


def forward(rows, ids, w_in, bias, w_out):
    embed = w_out.shape[1]
    table = bias[...]
    table = jnp.concatenate([table, jnp.zeros((embed - table.shape[0], table.shape[1]), f32)], 0)
    one_hot = hot_columns(ids, embed)
    added = None
    for _ in range(3):
        piece = table.astype(bf16)
        table = table - piece.astype(f32)
        part = tn_dot(one_hot, piece)
        added = part if added is None else added + part
    pre = jnp.dot(rows, w_in[...], preferred_element_type=f32) + added
    latent = jnp.dot(gelu_pair(pre)[0], w_out[...], preferred_element_type=f32)
    radius = jnp.sqrt(jnp.sum(latent * latent, axis=1, keepdims=True) + epsilon)
    return pre, latent, (latent / radius).astype(bf16)


def front_kernel(count, me_ref, *refs):
    held, (u_ref, unit_ref, own_ref), scratch, sems = (
        refs[:count],
        refs[count : count + 3],
        refs[count + 3 : -1],
        refs[-1],
    )
    copies = [
        pltpu.make_async_copy(src, dst, sems.at[i]) for i, (src, dst) in enumerate(zip(held, scratch))
    ]
    for copy in copies:
        copy.start()
    w_in, bias, w_out, neg_ids, neg_rows, ref_ids, ref_rows, owner, row, recording = scratch
    for copy in copies[:5]:
        copy.wait()
    unit_ref[...] = forward(neg_rows[...], neg_ids[...], w_in, bias, w_out)[2]
    for copy in copies[5:7]:
        copy.wait()
    u_ref[...] = forward(ref_rows[...], ref_ids[...], w_in, bias, w_out)[2]
    for copy in copies[7:]:
        copy.wait()
    pick_kernel(me_ref, owner, row, recording, own_ref)


def score_kernel(
    scale, count, own, ids, u_ref, pool_ref, w_in, bias, w_out, *refs
):
    rows = own[...]
    for got in refs[:count]:
        rows = rows + got[...]
    rows_ref, share_ref, loss_ref, grad_ref, grad_pos = refs[count:]
    rows_ref[...] = rows
    v = forward(rows, ids[...], w_in, bias, w_out)[2]
    u, pool = u_ref[...], pool_ref[...]
    uf, vf = u.astype(f32), v.astype(f32)
    pos_score = jnp.sum(uf * vf, axis=1, keepdims=True) / logit_sharpness_divisor
    exponent = jnp.exp(nt_dot(u, pool) / logit_sharpness_divisor - shift_bound)
    pos_exp = jnp.exp(pos_score - shift_bound)
    normalizer = pos_exp + jnp.sum(exponent, axis=1, keepdims=True)
    weights = (exponent / normalizer).astype(bf16)
    share_ref[...] = scale * tn_dot(weights, u)
    loss = jnp.log(normalizer) + shift_bound - pos_score
    loss_ref[...] = jnp.broadcast_to(loss, uf.shape).T[:1]
    pull = pos_exp / normalizer - 1.0
    grad_ref[...] = scale * (jnp.dot(weights, pool, preferred_element_type=f32) + pull * vf)
    grad_pos[...] = scale * pull * uf


def share_of(rows, ids, grad_unit, w_in, bias, w_out):
    pre, latent, _ = forward(rows, ids, w_in, bias, w_out)
    w_out = w_out[...]
    power = jnp.sum(latent * latent, axis=1, keepdims=True) + epsilon
    radius = jnp.sqrt(power)
    inner = jnp.sum(latent * grad_unit, axis=1, keepdims=True)
    grad_latent = ((grad_unit - latent * (inner / (radius * radius))) / radius).astype(bf16)
    hidden, slope = gelu_pair(pre)
    grad_pre = (nt_dot(grad_latent, w_out) * slope).astype(bf16)
    bias = jnp.dot(hot_columns(ids, w_out.shape[1]), grad_pre, preferred_element_type=f32)
    return tn_dot(rows, grad_pre), tn_dot(grad_latent, hidden), bias


def parts_of(total, embed):
    half, small = total.shape[0] // 2 - embed, total.shape[0] // 2
    return half, slice(0, half), slice(half, small), slice(small, small + half), slice(small + half, None)


def two_sets_kernel(*refs):
    w_out, total = refs[-2], refs[-1]
    a = share_of(*(r[...] for r in refs[:3]), *refs[6:9])
    b = share_of(*(r[...] for r in refs[3:6]), *refs[6:9])
    big, low, bias = (x + y for x, y in zip(a, b))
    half, first, out, second, animals = parts_of(total, w_out.shape[1])
    total[first, :] = big[:half]
    total[out, :] = low
    total[second, :] = big[half:]
    total[animals, :] = bias


def add_set_kernel(rows, ids, kept, got, w_in, bias, w_out, before, total):
    grad_unit = kept[...] + got[...].astype(f32)
    big, low, bias = share_of(rows[...], ids[...], grad_unit, w_in, bias, w_out)
    half, first, out, second, animals = parts_of(total, w_out.shape[1])
    total[first, :] = (before[first, :] + big[:half]).astype(bf16)
    total[out, :] = (before[out, :] + low).astype(bf16)
    total[second, :] = (before[second, :] + big[half:]).astype(bf16)
    total[animals, :] = (before[animals, :] + bias).astype(bf16)


def finish_kernel(core_ref, own, other, grad_w_in, grad_w_out, grad_bias):
    half = grad_w_in.shape[0] // 2
    animals = grad_bias.shape[0]

    def put(first, second):
        grad_w_in[:half, :] = first[:half, :]
        grad_w_in[half:, :] = second[:half, :]
        grad_w_out[...] = first[half:, :].astype(f32).T
        grad_bias[...] = second[half : half + animals, :].astype(f32)

    @pl.when(core_ref[0] == 0)
    def _():
        put(own, other)

    @pl.when(core_ref[0] != 0)
    def _():
        put(other, own)


def call(kernel, name, out, *args, scalars=0, limit=12, space=pltpu.VMEM, scratch=()):
    whole = pl.BlockSpec(memory_space=pltpu.VMEM)
    given = pl.BlockSpec(memory_space=space)
    shapes = [jax.ShapeDtypeStruct(*o) for o in out]
    return pl.pallas_call(
        kernel,
        name=name,
        out_shape=shapes,
        in_specs=[pl.BlockSpec(memory_space=pltpu.SMEM)] * scalars + [given] * (len(args) - scalars),
        out_specs=[whole] * len(out),
        scratch_shapes=list(scratch),
        compiler_params=pltpu.CompilerParams(vmem_limit_bytes=limit * 2**20),
    )(*args)


def slots(owner, row, nt, me_t):
    refs = row.shape[0]
    cap = 2 * refs // nt
    owner_hot = hot(owner, nt, jnp.int32)
    slot = jnp.sum((jnp.cumsum(owner_hot, axis=0) - owner_hot) * owner_hot, axis=1)
    found = []
    for k in range(1, nt):
        wanted = owner == (me_t ^ k)
        pick = wanted[None, :] & (slot[None, :] == jnp.arange(cap, dtype=jnp.int32)[:, None])
        ask = jnp.max(jnp.where(pick, row[None, :], -1), axis=1)
        found.append((pick, jnp.where(ask < 0, -1, me_t ^ k)[None, :], ask[None, :]))
    return found


def pick_kernel(me_ref, owner, row, recording, rows):
    wanted = jnp.where(owner[...] == me_ref[0], row[...], -1)
    one_hot = hot_columns(wanted, recording.shape[0])
    rows[...] = tn_dot(one_hot, recording[...]).astype(bf16)


def pick_rows(me, owner, row, recording):
    out = [((row.shape[1], recording.shape[1]), bf16)]
    return call(pick_kernel, "pick", out, me, owner, row, recording, scalars=1)[0]


def on_device(
    ref_rows,
    neg_rows,
    recording,
    pos_owner,
    pos_row,
    ref_animal,
    neg_animal,
    w_in,
    bias_animal,
    w_out,
):
    refs = ref_rows.shape[0]
    channels = w_in.shape[0]
    embed = w_out.shape[1]
    animals = bias_animal.shape[0]
    nt = lax.axis_size("tm")
    nb = lax.axis_size("batch")
    n = nt * nb
    me_b = lax.axis_index("batch")
    me_t = lax.axis_index("tm")
    me = me_b * nt + me_t

    owner, row = pos_owner.reshape(1, refs), pos_row.reshape(1, refs)
    ref_ids, neg_ids = ref_animal[None, :], neg_animal[None, :]
    here = me_t.reshape(1)
    if nt == 2:
        asks = [(None, owner, row)]
    else:
        asks = slots(pos_owner[:, 0], pos_row, nt, me_t)
    asked = [(swap(o, "tm", k, nt), swap(r, "tm", k, nt)) for k, (_, o, r) in enumerate(asks, 1)]
    weights = (w_in, bias_animal, w_out)
    inputs = (*weights, neg_ids, neg_rows, ref_ids, ref_rows, owner, row, recording)
    inputs = [pltpu.with_memory_space_constraint(x, pltpu.HBM) for x in inputs]
    u, neg_unit, own = call(
        functools.partial(front_kernel, len(inputs)),
        "front",
        [
            ((refs, embed), bf16),
            ((neg_rows.shape[0], embed), bf16),
            ((refs, recording.shape[1]), bf16),
        ],
        here,
        *inputs,
        scalars=1,
        space=pltpu.HBM,
        scratch=[pltpu.VMEM(x.shape, x.dtype) for x in inputs]
        + [pltpu.SemaphoreType.DMA((len(inputs),))],
    )
    found = [pick_rows(here, o, r, recording) for o, r in asked]
    neg_unit, found = lax.optimization_barrier((neg_unit, found))
    got = [swap(f, "tm", k, nt) for k, f in enumerate(found, 1)]
    pool = gather_batch(neg_unit, nb, me_b)
    got = [
        g if pick is None else jnp.dot(pick.T.astype(bf16), g, preferred_element_type=bf16)
        for (pick, _, _), g in zip(asks, got)
    ]

    scale = float(refs * n) ** (-0.5) / logit_sharpness_divisor
    out = [(ref_rows.shape, bf16), ((pool.shape[0], embed), f32), ((1, refs), f32)]
    out += [(u.shape, f32), (u.shape, f32)]
    pos_rows, share, loss, grad_ref, grad_pos = call(
        functools.partial(score_kernel, scale, len(got)),
        "scores",
        out,
        own,
        ref_ids,
        u,
        pool,
        *weights,
        *got,
        limit=max(12, 20 * refs * pool.shape[0] >> 20),
    )
    total = call(
        two_sets_kernel,
        "backward",
        [((channels + 2 * embed, w_in.shape[1]), f32)],
        *(ref_rows, ref_ids, grad_ref),
        *(pos_rows, ref_ids, grad_pos),
        *weights,
    )[0]
    kept, last, total = scatter_batch(share, nb, me_b, total)
    total = call(
        add_set_kernel,
        "backward_neg",
        [(total.shape, bf16)],
        *(neg_rows, neg_ids, kept, last, *weights, total),
    )[0]
    own, other = all_sum(total, n, nt, me)
    grad_w_in, grad_w_out, grad_bias = call(
        finish_kernel,
        "finish",
        [(w_in.shape, bf16), (w_out.shape, f32), (bias_animal.shape, f32)],
        lax.rem(me_b, 2).reshape(1),
        own,
        other,
        scalars=1,
    )
    return (loss.reshape(refs), grad_w_in, grad_w_out, grad_bias)


def solution(mesh):
    in_specs = (
        P(("batch", "tm"), None),
        P(("batch", "tm"), None),
        P("tm", None),
        P(("batch", "tm"), None),
        P(("batch", "tm")),
        P(("batch", "tm")),
        P(("batch", "tm")),
        P(),
        P(),
        P(),
    )
    out_specs = (P(("batch", "tm")), P(), P(), P())
    return jax.shard_map(
        on_device, mesh=mesh, in_specs=in_specs, out_specs=out_specs, check_vma=False
    )
```

time: 106 us -> 87.2 us (0.82)
  matrix products: 21 us -> 0 us
  Pallas kernels: 0 us -> 11.6 us
  other arithmetic: 11.7 us -> 0.39 us
  starting transfers between devices: 28.1 us -> 32 us
    dot_general x17 -> x0, matrix products: 21 us -> none  [the longest x2 6.14 us: backward(): lax.dot_general(wide, grad_pre, (((0,), (0,)), ((), ())), preferred_eleme...]
    pallas_call x0 -> x6, Pallas kernels: none -> 11.6 us  [call(): pl.pallas_call(kernel, name=name, out_shape=shapes, in_specs=[pl.BlockSpe...]
    ppermute x24 -> x25, starting transfers between devices: 28.1 us -> 32 us  [swap(): return lax.ppermute(x, axes, [(i, i ^ mask) for i in range(n)])]
    convert_element_type x6 -> x0, other arithmetic: 3.85 us -> none  [the longest x1 2.21 us: on_device(): total = all_sum(total.astype(bf16), n, nt, me)]
    reduce_sum x3 -> x0, other arithmetic: 1.8 us -> none  [the longest x2 1.57 us: backward(): inner = jnp.sum(latent * grad_unit, axis=1, keepdims=True)]
    mul x3 -> x0, other arithmetic: 1.18 us -> none  [the longest x2 1.09 us: backward(): radius * radius]
    convert_element_type x2, other arithmetic: 1.35 us -> 0.27 us  [all_sum(): x = sum((g.astype(f32) for g in got), own).astype(bf16)]
    ppermute x24 -> x25, waiting for transfers between devices: 39 us -> 38.2 us  [swap(): return lax.ppermute(x, axes, [(i, i ^ mask) for i in range(n)])]
  transfers between devices with their start and end apart: 24 -> 25, of which waited for: 18 -> 20; matrix products, arithmetic and copies ran while one was open for 14% -> 0% of each run, Pallas kernels for 0% -> 8%
where the time goes in v2:
time: 87.2 us; the launch traced here: 87.1 us
  waiting for transfers between devices  38.2 us (44%)
  starting transfers between devices  32 us (37%)
  Pallas kernels  11.6 us (13%)
  local copies, waits for them, and re-layouts  3.85 us (4%)
  between operations  1.01 us (1%)
    ppermute x25, waiting for transfers between devices, swap(): return lax.ppermute(x, axes, [(i, i ^ mask) for i in range(n)])  38.2 us
    ppermute x25, starting transfers between devices, swap(): return lax.ppermute(x, axes, [(i, i ^ mask) for i in range(n)])  32 us
    pallas_call x6, Pallas kernels, call(): pl.pallas_call(kernel, name=name, out_shape=shapes, in_specs=[pl.BlockSpe...  11.6 us
    unnamed x27, local copies, waits for them, and re-layouts  3.35 us
  transfers between devices with their start and end apart: 25, of which 20 were waited for; matrix products, arithmetic and copies ran while one was open for 0% of the time, Pallas kernels for 8%

profile of v2, /device:TPU:0, one launch (start us, length us, event | category | flops | bytes accessed | tf_op | source)
XLA Modules:
  0.0 87.1 jit_solution(17928989677490043145)
XLA Ops:
  0.6 3.0 %collective-permute-start = (s32[1,256]{1,0:T(1,128)}, s32[1,256]{1,0:T(1,128)S(1)}, u32[]{:S(2)}, u32[]{:S(2)}) collective-permute-start(s32[1,256]{1,0:T(1,128)} %bitcast.149), channel_id=1, source_target_pairs={{0,1},{1,0},{2,3},{3,2},{4,5},{5,4},{6,7},{7,6},{8,9},{9,8},{10,11... | collective-permute-start | bytes 3080 | tf_op jit(solution)/shard_map/ppermute | solution.py:19
  3.7 3.6 %front.1 = (bf16[256,128]{1,0:T(8,128)(2,1)S(1)}, bf16[64,128]{1,0:T(8,128)(2,1)S(1)}, bf16[256,1024]{1,0:T(8,128)(2,1)S(1)}) custom-call(s32[1]{0:T(128)} %bitcast.me_ref, bf16[1024,512]{1,0:T(8,128)(2,1)} %w_in.3, f32[8,512]{1,0:T(8,128)} %bias.3, bf16[512,128]{1,0:T(8,128)(2,1)} %w_out.3, s32[1,64]{1,0:T(1,128)} %bitcast.139, bf16[64,1024]{1,0:T(8,128)(2,1)} %rows.1, ...), custom_call_target="tpu_custom_call" | custom-call | tf_op jit(solution)/shard_map/front/pallas_call | solution.py:260
  7.9 3.1 %collective-permute-start.2 = (bf16[64,128]{1,0:T(8,128)(2,1)S(1)}, bf16[64,128]{1,0:T(8,128)(2,1)S(1)}, u32[]{:S(2)}, u32[]{:S(2)}) collective-permute-start(bf16[64,128]{1,0:T(8,128)(2,1)S(1)} %get-tuple-element.22), channel_id=1, source_target_pairs={{0,16},{2,18},{4,20},{6,22},{8,24},{10,26},{12,28},{14,30},{16,0},... | collective-permute-start | bytes 49160 | tf_op jit(solution)/shard_map/ppermute | solution.py:19
  12.7 1.9 %collective-permute-start.3 = (bf16[128,128]{1,0:T(8,128)(2,1)S(1)}, bf16[128,128]{1,0:T(8,128)(2,1)S(1)}, u32[]{:S(2)}, u32[]{:S(2)}) collective-permute-start(bf16[128,128]{1,0:T(8,128)(2,1)S(1)} %pad_maximum_fusion.3), channel_id=1, source_target_pairs={{0,8},{2,10},{4,12},{6,14},{8,0},{10,2},{12,4},{14,6},{16,24},{18,... | collective-permute-start | bytes 98312 | tf_op jit(solution)/shard_map/ppermute | solution.py:19
  14.6 2.0 %collective-permute-done.3 = bf16[128,128]{1,0:T(8,128)(2,1)S(1)} collective-permute-done((bf16[128,128]{1,0:T(8,128)(2,1)S(1)}, bf16[128,128]{1,0:T(8,128)(2,1)S(1)}, u32[]{:S(2)}, u32[]{:S(2)}) %collective-permute-start.3) | collective-permute-done | bytes 32800 | tf_op jit(solution)/shard_map/ppermute | solution.py:19
  16.6 1.8 %collective-permute-start.4 = (bf16[256,128]{1,0:T(8,128)(2,1)S(1)}, bf16[256,128]{1,0:T(8,128)(2,1)S(1)}, u32[]{:S(2)}, u32[]{:S(2)}) collective-permute-start(bf16[256,128]{1,0:T(8,128)(2,1)S(1)} %pad_maximum_fusion.1), channel_id=1, source_target_pairs={{0,4},{2,6},{4,0},{6,2},{8,12},{10,14},{12,8},{14,10},{16,20},{18,... | collective-permute-start | bytes 196616 | tf_op jit(solution)/shard_map/ppermute | solution.py:19
  18.5 2.4 %collective-permute-done.4 = bf16[256,128]{1,0:T(8,128)(2,1)S(1)} collective-permute-done((bf16[256,128]{1,0:T(8,128)(2,1)S(1)}, bf16[256,128]{1,0:T(8,128)(2,1)S(1)}, u32[]{:S(2)}, u32[]{:S(2)}) %collective-permute-start.4) | collective-permute-done | bytes 65568 | tf_op jit(solution)/shard_map/ppermute | solution.py:19
  23.8 2.1 %scores.1 = (bf16[256,1024]{1,0:T(8,128)(2,1)S(1)}, f32[1024,128]{1,0:T(8,128)S(1)}, f32[1,256]{1,0:T(1,128)}, f32[256,128]{1,0:T(8,128)S(1)}, f32[256,128]{1,0:T(8,128)S(1)}) custom-call(bf16[256,1024]{1,0:T(8,128)(2,1)S(1)} %get-tuple-element.19.own, s32[1,256]{1,0:T(1,128)S(1)} %bitcast.136, bf16[256,128]{1,0:T(8,128)(2,1)S(1)} %get-tuple-element.20.u_ref, ...), custom_call_target="tpu_custom_call" | custom-call | tf_op jit(solution)/shard_map/scores/pallas_call | solution.py:260
  29.2 3.0 %backward.1.before = f32[1280,512]{1,0:T(8,128)S(1)} custom-call(bf16[256,1024]{1,0:T(8,128)(2,1)S(1)} %copy-done.5, s32[1,256]{1,0:T(1,128)S(1)} %bitcast.137, f32[256,128]{1,0:T(8,128)S(1)} %get-tuple-element.26.refs_2_, bf16[256,1024]{1,0:T(8,128)(2,1)S(1)} %get-tuple-element.27.refs_3_, s32[1,256]{1,0:T(1,128)S(1)} %bitcast.138, ...), custom_call_target="tpu_custom_call" | custom-call | tf_op jit(solution)/shard_map/backward/pallas_call | solution.py:260
  35.4 2.8 %collective-permute-done.9 = bf16[2,64,128]{2,1,0:T(8,128)(2,1)S(1)} collective-permute-done((bf16[2,64,128]{2,1,0:T(8,128)(2,1)S(1)}, bf16[2,64,128]{2,1,0:T(8,128)(2,1)S(1)}, u32[]{:S(2)}, u32[]{:S(2)}) %collective-permute-start.9) | collective-permute-done | bytes 32800 | tf_op jit(solution)/shard_map/ppermute | solution.py:19
  39.8 2.2 %collective-permute-done.10 = bf16[1,64,128]{2,1,0:T(8,128)(2,1)S(1)} collective-permute-done((bf16[1,64,128]{2,1,0:T(8,128)(2,1)S(1)}, bf16[1,64,128]{2,1,0:T(8,128)(2,1)S(1)}, u32[]{:S(2)}, u32[]{:S(2)}) %collective-permute-start.10) | collective-permute-done | bytes 16416 | tf_op jit(solution)/shard_map/ppermute | solution.py:19
  42.0 1.7 %copy-done.2 = f32[1280,512]{1,0:T(8,128)S(1)} copy-done((f32[1280,512]{1,0:T(8,128)S(1)}, f32[1280,512]{1,0:T(8,128)}, u32[]{:S(2)}) %copy-start.2) | copy-done | bytes 2621464
  45.2 2.1 %collective-permute-done.11 = bf16[640,512]{1,0:T(8,128)(2,1)S(1)} collective-permute-done((bf16[640,512]{1,0:T(8,128)(2,1)S(1)}, bf16[640,512]{1,0:T(8,128)(2,1)S(1)}, u32[]{:S(2)}, u32[]{:S(2)}) %collective-permute-start.11) | collective-permute-done | bytes 655392 | tf_op jit(solution)/shard_map/ppermute | solution.py:19
  51.1 3.6 %collective-permute-done.12 = bf16[160,512]{1,0:T(8,128)(2,1)S(1)} collective-permute-done((bf16[160,512]{1,0:T(8,128)(2,1)S(1)}, bf16[160,512]{1,0:T(8,128)(2,1)S(1)}, u32[]{:S(2)}, u32[]{:S(2)}) %collective-permute-start.12) | collective-permute-done | bytes 163872 | tf_op jit(solution)/shard_map/ppermute | solution.py:19
  54.6 3.9 %collective-permute-done.13 = bf16[160,512]{1,0:T(8,128)(2,1)S(1)} collective-permute-done((bf16[160,512]{1,0:T(8,128)(2,1)S(1)}, bf16[160,512]{1,0:T(8,128)(2,1)S(1)}, u32[]{:S(2)}, u32[]{:S(2)}) %collective-permute-start.13) | collective-permute-done | bytes 163872 | tf_op jit(solution)/shard_map/ppermute | solution.py:19
  59.8 1.8 %collective-permute-start.16 = (bf16[40,512]{1,0:T(8,128)(2,1)S(1)}, bf16[40,512]{1,0:T(8,128)(2,1)S(1)}, u32[]{:S(2)}, u32[]{:S(2)}) collective-permute-start(bf16[40,512]{1,0:T(8,128)(2,1)S(1)} %get-tuple-element.49), channel_id=1, source_target_pairs={{0,16},{1,17},{2,18},{3,19},{4,20},{5,21},{6,22},{7,23},{8,24},{9,... | collective-permute-start | bytes 122888 | tf_op jit(solution)/shard_map/ppermute | solution.py:19
  63.1 2.5 %collective-permute-done.16 = bf16[40,512]{1,0:T(8,128)(2,1)S(1)} collective-permute-done((bf16[40,512]{1,0:T(8,128)(2,1)S(1)}, bf16[40,512]{1,0:T(8,128)(2,1)S(1)}, u32[]{:S(2)}, u32[]{:S(2)}) %collective-permute-start.16) | collective-permute-done | bytes 40992 | tf_op jit(solution)/shard_map/ppermute | solution.py:19
  65.6 2.0 %collective-permute-done.17 = bf16[40,512]{1,0:T(8,128)(2,1)S(1)} collective-permute-done((bf16[40,512]{1,0:T(8,128)(2,1)S(1)}, bf16[40,512]{1,0:T(8,128)(2,1)S(1)}, u32[]{:S(2)}, u32[]{:S(2)}) %collective-permute-start.17) | collective-permute-done | bytes 40992 | tf_op jit(solution)/shard_map/ppermute | solution.py:19
  67.7 1.9 %collective-permute-start.19 = (bf16[40,512]{1,0:T(8,128)(2,1)S(1)}, bf16[40,512]{1,0:T(8,128)(2,1)S(1)}, u32[]{:S(2)}, u32[]{:S(2)}) collective-permute-start(bf16[40,512]{1,0:T(8,128)(2,1)S(1)} %get-tuple-element.35), channel_id=1, source_target_pairs={{0,16},{1,17},{2,18},{3,19},{4,20},{5,21},{6,22},{7,23},{8,24},{9,... | collective-permute-start | bytes 122888 | tf_op jit(solution)/shard_map/ppermute | solution.py:19
  69.6 2.5 %collective-permute-start.20 = (bf16[40,512]{1,0:T(8,128)(2,1)S(1)}, bf16[40,512]{1,0:T(8,128)(2,1)S(1)}, u32[]{:S(2)}, u32[]{:S(2)}) collective-permute-start(bf16[40,512]{1,0:T(8,128)(2,1)S(1)} %get-tuple-element.35), channel_id=1, source_target_pairs={{0,24},{1,25},{2,26},{3,27},{4,28},{5,29},{6,30},{7,31},{8,16},{9,... | collective-permute-start | bytes 122888 | tf_op jit(solution)/shard_map/ppermute | solution.py:19
  72.7 2.7 %collective-permute-done.20 = bf16[40,512]{1,0:T(8,128)(2,1)S(1)} collective-permute-done((bf16[40,512]{1,0:T(8,128)(2,1)S(1)}, bf16[40,512]{1,0:T(8,128)(2,1)S(1)}, u32[]{:S(2)}, u32[]{:S(2)}) %collective-permute-start.20) | collective-permute-done | bytes 40992 | tf_op jit(solution)/shard_map/ppermute | solution.py:19
  79.0 1.7 %collective-permute-done.21 = bf16[160,512]{1,0:T(8,128)(2,1)S(1)} collective-permute-done((bf16[160,512]{1,0:T(8,128)(2,1)S(1)}, bf16[160,512]{1,0:T(8,128)(2,1)S(1)}, u32[]{:S(2)}, u32[]{:S(2)}) %collective-permute-start.21) | collective-permute-done | bytes 163872 | tf_op jit(solution)/shard_map/ppermute | solution.py:19
  82.0 1.7 %collective-permute-done.23 = bf16[160,512]{1,0:T(8,128)(2,1)S(1)} collective-permute-done((bf16[160,512]{1,0:T(8,128)(2,1)S(1)}, bf16[160,512]{1,0:T(8,128)(2,1)S(1)}, u32[]{:S(2)}, u32[]{:S(2)}) %collective-permute-start.23) | collective-permute-done | bytes 163872 | tf_op jit(solution)/shard_map/ppermute | solution.py:19
  83.8 2.1 %collective-permute-done.24.other = bf16[640,512]{1,0:T(8,128)(2,1)S(1)} collective-permute-done((bf16[640,512]{1,0:T(8,128)(2,1)S(1)}, bf16[640,512]{1,0:T(8,128)(2,1)S(1)}, u32[]{:S(2)}, u32[]{:S(2)}) %collective-permute-start.24) | collective-permute-done | bytes 655392 | tf_op jit(solution)/shard_map/ppermute | solution.py:19
  (100 shorter events, 27.9 us)
Async XLA Ops:
  0.6 6.7 %collective-permute-start = (s32[1,256]{1,0:T(1,128)}, s32[1,256]{1,0:T(1,128)S(1)}, u32[]{:S(2)}, u32[]{:S(2)}) collective-permute-start(s32[1,256]{1,0:T(1,128)} %bitcast.149), channel_id=1, source_target_pairs={{0,1},{1,0},{2,3},{3,2},{4,5},{5,4},{6,7},{7,6},{8,9},{9,8},{10,11... | collective-permute-start | bytes 3080 | tf_op jit(solution)/shard_map/ppermute | solution.py:19
  3.6 3.8 %collective-permute-start.1 = (s32[1,256]{1,0:T(1,128)}, s32[1,256]{1,0:T(1,128)S(1)}, u32[]{:S(2)}, u32[]{:S(2)}) collective-permute-start(s32[1,256]{1,0:T(1,128)} %bitcast.151), channel_id=1, source_target_pairs={{0,1},{1,0},{2,3},{3,2},{4,5},{5,4},{6,7},{7,6},{8,9},{9,8},{10,11... | collective-permute-start | bytes 3080 | tf_op jit(solution)/shard_map/ppermute | solution.py:19
  7.9 4.8 %collective-permute-start.2 = (bf16[64,128]{1,0:T(8,128)(2,1)S(1)}, bf16[64,128]{1,0:T(8,128)(2,1)S(1)}, u32[]{:S(2)}, u32[]{:S(2)}) collective-permute-start(bf16[64,128]{1,0:T(8,128)(2,1)S(1)} %get-tuple-element.22), channel_id=1, source_target_pairs={{0,16},{2,18},{4,20},{6,22},{8,24},{10,26},{12,28},{14,30},{16,0},... | collective-permute-start | bytes 49160 | tf_op jit(solution)/shard_map/ppermute | solution.py:19
  11.0 12.8 %collective-permute-start.6 = (bf16[256,1024]{1,0:T(8,128)(2,1)S(1)}, bf16[256,1024]{1,0:T(8,128)(2,1)S(1)}, u32[]{:S(2)}, u32[]{:S(2)}) collective-permute-start(bf16[256,1024]{1,0:T(8,128)(2,1)S(1)} %pick.1), channel_id=1, source_target_pairs={{0,1},{1,0},{2,3},{3,2},{4,5},{5,4},{6,7},{7,6},{8,9},{9,8},{10,11... | collective-permute-start | bytes 1572872 | tf_op jit(solution)/shard_map/ppermute | solution.py:19
  12.7 3.9 %collective-permute-start.3 = (bf16[128,128]{1,0:T(8,128)(2,1)S(1)}, bf16[128,128]{1,0:T(8,128)(2,1)S(1)}, u32[]{:S(2)}, u32[]{:S(2)}) collective-permute-start(bf16[128,128]{1,0:T(8,128)(2,1)S(1)} %pad_maximum_fusion.3), channel_id=1, source_target_pairs={{0,8},{2,10},{4,12},{6,14},{8,0},{10,2},{12,4},{14,6},{16,24},{18,... | collective-permute-start | bytes 98312 | tf_op jit(solution)/shard_map/ppermute | solution.py:19
  16.6 4.3 %collective-permute-start.4 = (bf16[256,128]{1,0:T(8,128)(2,1)S(1)}, bf16[256,128]{1,0:T(8,128)(2,1)S(1)}, u32[]{:S(2)}, u32[]{:S(2)}) collective-permute-start(bf16[256,128]{1,0:T(8,128)(2,1)S(1)} %pad_maximum_fusion.1), channel_id=1, source_target_pairs={{0,4},{2,6},{4,0},{6,2},{8,12},{10,14},{12,8},{14,10},{16,20},{18,... | collective-permute-start | bytes 196616 | tf_op jit(solution)/shard_map/ppermute | solution.py:19
  20.9 1.4 %collective-permute-start.5 = (bf16[512,128]{1,0:T(8,128)(2,1)S(1)}, bf16[512,128]{1,0:T(8,128)(2,1)S(1)}, u32[]{:S(2)}, u32[]{:S(2)}) collective-permute-start(bf16[512,128]{1,0:T(8,128)(2,1)S(1)} %pad_maximum_fusion), channel_id=1, source_target_pairs={{0,2},{2,0},{4,6},{6,4},{8,10},{10,8},{12,14},{14,12},{16,18},{18,... | collective-permute-start | bytes 393224 | tf_op jit(solution)/shard_map/ppermute | solution.py:19
  27.6 6.6 %collective-permute-start.8 = (bf16[4,64,128]{2,1,0:T(8,128)(2,1)S(1)}, bf16[4,64,128]{2,1,0:T(8,128)(2,1)S(1)}, u32[]{:S(2)}, u32[]{:S(2)}) collective-permute-start(bf16[4,64,128]{2,1,0:T(8,128)(2,1)S(1)} %pad_maximum_fusion.2), channel_id=1, source_target_pairs={{0,16},{2,18},{4,20},{6,22},{8,24},{10,26},{12,28},{14,30},{16,0},... | collective-permute-start | bytes 196616 | tf_op jit(solution)/shard_map/ppermute | solution.py:19
  34.2 4.0 %collective-permute-start.9 = (bf16[2,64,128]{2,1,0:T(8,128)(2,1)S(1)}, bf16[2,64,128]{2,1,0:T(8,128)(2,1)S(1)}, u32[]{:S(2)}, u32[]{:S(2)}) collective-permute-start(bf16[2,64,128]{2,1,0:T(8,128)(2,1)S(1)} %pad_maximum_fusion.4), channel_id=1, source_target_pairs={{0,8},{2,10},{4,12},{6,14},{8,0},{10,2},{12,4},{14,6},{16,24},{18,... | collective-permute-start | bytes 98312 | tf_op jit(solution)/shard_map/ppermute | solution.py:19
  38.2 3.8 %collective-permute-start.10 = (bf16[1,64,128]{2,1,0:T(8,128)(2,1)S(1)}, bf16[1,64,128]{2,1,0:T(8,128)(2,1)S(1)}, u32[]{:S(2)}, u32[]{:S(2)}) collective-permute-start(bf16[1,64,128]{2,1,0:T(8,128)(2,1)S(1)} %get-tuple-element.36), channel_id=1, source_target_pairs={{0,4},{2,6},{4,0},{6,2},{8,12},{10,14},{12,8},{14,10},{16,20},{18,... | collective-permute-start | bytes 49160 | tf_op jit(solution)/shard_map/ppermute | solution.py:19
  45.1 2.2 %collective-permute-start.11 = (bf16[640,512]{1,0:T(8,128)(2,1)S(1)}, bf16[640,512]{1,0:T(8,128)(2,1)S(1)}, u32[]{:S(2)}, u32[]{:S(2)}) collective-permute-start(bf16[640,512]{1,0:T(8,128)(2,1)S(1)} %dynamic-slice_bitcast_fusion), channel_id=1, source_target_pairs={{0,2},{1,3},{2,0},{3,1},{4,6},{5,7},{6,4},{7,5},{8,10},{9,11},{10,... | collective-permute-start | bytes 1966088 | tf_op jit(solution)/shard_map/ppermute | solution.py:19
  47.5 7.1 %collective-permute-start.12 = (bf16[160,512]{1,0:T(8,128)(2,1)S(1)}, bf16[160,512]{1,0:T(8,128)(2,1)S(1)}, u32[]{:S(2)}, u32[]{:S(2)}) collective-permute-start(bf16[160,512]{1,0:T(8,128)(2,1)S(1)} %get-tuple-element.40), channel_id=1, source_target_pairs={{0,1},{1,0},{2,3},{3,2},{4,5},{5,4},{6,7},{7,6},{8,9},{9,8},{10,11... | collective-permute-start | bytes 491528 | tf_op jit(solution)/shard_map/ppermute | solution.py:19
  49.1 9.5 %collective-permute-start.13 = (bf16[160,512]{1,0:T(8,128)(2,1)S(1)}, bf16[160,512]{1,0:T(8,128)(2,1)S(1)}, u32[]{:S(2)}, u32[]{:S(2)}) collective-permute-start(bf16[160,512]{1,0:T(8,128)(2,1)S(1)} %get-tuple-element.42), channel_id=1, source_target_pairs={{0,4},{1,5},{2,6},{3,7},{4,0},{5,1},{6,2},{7,3},{8,12},{9,13},{10,... | collective-permute-start | bytes 491528 | tf_op jit(solution)/shard_map/ppermute | solution.py:19
  50.6 8.0 %collective-permute-start.14 = (bf16[160,512]{1,0:T(8,128)(2,1)S(1)}, bf16[160,512]{1,0:T(8,128)(2,1)S(1)}, u32[]{:S(2)}, u32[]{:S(2)}) collective-permute-start(bf16[160,512]{1,0:T(8,128)(2,1)S(1)} %get-tuple-element.41), channel_id=1, source_target_pairs={{0,5},{1,4},{2,7},{3,6},{4,1},{5,0},{6,3},{7,2},{8,13},{9,12},{10,... | collective-permute-start | bytes 491528 | tf_op jit(solution)/shard_map/ppermute | solution.py:19
  58.7 4.5 %collective-permute-start.15 = (bf16[40,512]{1,0:T(8,128)(2,1)S(1)}, bf16[40,512]{1,0:T(8,128)(2,1)S(1)}, u32[]{:S(2)}, u32[]{:S(2)}) collective-permute-start(bf16[40,512]{1,0:T(8,128)(2,1)S(1)} %get-tuple-element.47), channel_id=1, source_target_pairs={{0,8},{1,9},{2,10},{3,11},{4,12},{5,13},{6,14},{7,15},{8,0},{9,1},... | collective-permute-start | bytes 122888 | tf_op jit(solution)/shard_map/ppermute | solution.py:19
  59.8 5.8 %collective-permute-start.16 = (bf16[40,512]{1,0:T(8,128)(2,1)S(1)}, bf16[40,512]{1,0:T(8,128)(2,1)S(1)}, u32[]{:S(2)}, u32[]{:S(2)}) collective-permute-start(bf16[40,512]{1,0:T(8,128)(2,1)S(1)} %get-tuple-element.49), channel_id=1, source_target_pairs={{0,16},{1,17},{2,18},{3,19},{4,20},{5,21},{6,22},{7,23},{8,24},{9,... | collective-permute-start | bytes 122888 | tf_op jit(solution)/shard_map/ppermute | solution.py:19
  61.7 5.9 %collective-permute-start.17 = (bf16[40,512]{1,0:T(8,128)(2,1)S(1)}, bf16[40,512]{1,0:T(8,128)(2,1)S(1)}, u32[]{:S(2)}, u32[]{:S(2)}) collective-permute-start(bf16[40,512]{1,0:T(8,128)(2,1)S(1)} %get-tuple-element.48), channel_id=1, source_target_pairs={{0,24},{1,25},{2,26},{3,27},{4,28},{5,29},{6,30},{7,31},{8,16},{9,... | collective-permute-start | bytes 122888 | tf_op jit(solution)/shard_map/ppermute | solution.py:19
  67.6 4.5 %collective-permute-start.18 = (bf16[40,512]{1,0:T(8,128)(2,1)S(1)}, bf16[40,512]{1,0:T(8,128)(2,1)S(1)}, u32[]{:S(2)}, u32[]{:S(2)}) collective-permute-start(bf16[40,512]{1,0:T(8,128)(2,1)S(1)} %get-tuple-element.35), channel_id=1, source_target_pairs={{0,8},{1,9},{2,10},{3,11},{4,12},{5,13},{6,14},{7,15},{8,0},{9,1},... | collective-permute-start | bytes 122888 | tf_op jit(solution)/shard_map/ppermute | solution.py:19
  67.7 5.0 %collective-permute-start.19 = (bf16[40,512]{1,0:T(8,128)(2,1)S(1)}, bf16[40,512]{1,0:T(8,128)(2,1)S(1)}, u32[]{:S(2)}, u32[]{:S(2)}) collective-permute-start(bf16[40,512]{1,0:T(8,128)(2,1)S(1)} %get-tuple-element.35), channel_id=1, source_target_pairs={{0,16},{1,17},{2,18},{3,19},{4,20},{5,21},{6,22},{7,23},{8,24},{9,... | collective-permute-start | bytes 122888 | tf_op jit(solution)/shard_map/ppermute | solution.py:19
  69.6 5.8 %collective-permute-start.20 = (bf16[40,512]{1,0:T(8,128)(2,1)S(1)}, bf16[40,512]{1,0:T(8,128)(2,1)S(1)}, u32[]{:S(2)}, u32[]{:S(2)}) collective-permute-start(bf16[40,512]{1,0:T(8,128)(2,1)S(1)} %get-tuple-element.35), channel_id=1, source_target_pairs={{0,24},{1,25},{2,26},{3,27},{4,28},{5,29},{6,30},{7,31},{8,16},{9,... | collective-permute-start | bytes 122888 | tf_op jit(solution)/shard_map/ppermute | solution.py:19
  75.4 5.3 %collective-permute-start.21 = (bf16[160,512]{1,0:T(8,128)(2,1)S(1)}, bf16[160,512]{1,0:T(8,128)(2,1)S(1)}, u32[]{:S(2)}, u32[]{:S(2)}) collective-permute-start(bf16[160,512]{1,0:T(8,128)(2,1)S(1)} %bitcast.143), channel_id=1, source_target_pairs={{0,1},{1,0},{2,3},{3,2},{4,5},{5,4},{6,7},{7,6},{8,9},{9,8},{10,11... | collective-permute-start | bytes 491528 | tf_op jit(solution)/shard_map/ppermute | solution.py:19
  76.7 5.3 %collective-permute-start.22 = (bf16[160,512]{1,0:T(8,128)(2,1)S(1)}, bf16[160,512]{1,0:T(8,128)(2,1)S(1)}, u32[]{:S(2)}, u32[]{:S(2)}) collective-permute-start(bf16[160,512]{1,0:T(8,128)(2,1)S(1)} %bitcast.144), channel_id=1, source_target_pairs={{0,4},{1,5},{2,6},{3,7},{4,0},{5,1},{6,2},{7,3},{8,12},{9,13},{10,... | collective-permute-start | bytes 491528 | tf_op jit(solution)/shard_map/ppermute | solution.py:19
  77.5 6.3 %collective-permute-start.23 = (bf16[160,512]{1,0:T(8,128)(2,1)S(1)}, bf16[160,512]{1,0:T(8,128)(2,1)S(1)}, u32[]{:S(2)}, u32[]{:S(2)}) collective-permute-start(bf16[160,512]{1,0:T(8,128)(2,1)S(1)} %bitcast.145), channel_id=1, source_target_pairs={{0,5},{1,4},{2,7},{3,6},{4,1},{5,0},{6,3},{7,2},{8,13},{9,12},{10,... | collective-permute-start | bytes 491528 | tf_op jit(solution)/shard_map/ppermute | solution.py:19
  83.8 2.2 %collective-permute-start.24 = (bf16[640,512]{1,0:T(8,128)(2,1)S(1)}, bf16[640,512]{1,0:T(8,128)(2,1)S(1)}, u32[]{:S(2)}, u32[]{:S(2)}) collective-permute-start(bf16[640,512]{1,0:T(8,128)(2,1)S(1)} %bitcast.120), channel_id=1, source_target_pairs={{0,2},{1,3},{2,0},{3,1},{4,6},{5,7},{6,4},{7,5},{8,10},{9,11},{10,... | collective-permute-start | bytes 1966088 | tf_op jit(solution)/shard_map/ppermute | solution.py:19
  (11 other events, 105.2 us)

commit v3 on v2

v3 whole, which is shorter than its diff:
```python
import functools

import jax
import jax.numpy as jnp
from jax import lax
from jax.experimental import pallas as pl
from jax.experimental.pallas import tpu as pltpu
from jax.sharding import PartitionSpec as P

logit_sharpness_divisor = 0.1
shift_bound = 10.0
epsilon = 1e-06
AXES = ("batch", "tm")
bf16 = jnp.bfloat16
f32 = jnp.float32


def swap(x, axes, mask, n):
    return lax.ppermute(x, axes, [(i, i ^ mask) for i in range(n)])


def batch_masks(nb):
    return [1 << i for i in range(nb.bit_length() - 1)]


def gather_batch(x, nb, w, wide):
    masks = batch_masks(nb)
    order = masks[2:][::-1] + masks[1:2] + masks[:1]
    rows = x.shape[0]
    parts = {0: x}
    for m in order:
        keys = list(parts)
        block = jnp.concatenate([parts[k] for k in keys], 0) if len(keys) > 1 else parts[keys[0]]
        if m == masks[1]:
            block, wide = lax.optimization_barrier((block, wide))
        got = swap(block, "batch", m, nb)
        for i, k in enumerate(keys):
            parts[k ^ m] = got[i * rows : (i + 1) * rows]
    out = jnp.zeros((nb,) + x.shape, x.dtype)
    for k, part in parts.items():
        out = put(out, part, w["b", k])
    return out.reshape((nb * rows,) + x.shape[1:]), wide


def near_masks(nb):
    return batch_masks(nb)[1:3]


def spread(x, masks, nb):
    for m in masks:
        x = jnp.concatenate([x, swap(x, "batch", m, nb)], 0)
    return x


def kept_order(nb):
    masks = batch_masks(nb)
    high = [sum(m for i, m in enumerate(masks[3:]) if j >> i & 1) for j in range(nb >> 3)]
    return [h ^ k for h in high for k in members(near_masks(nb))]


def scatter_batch(kept, sent, nb, wide):
    masks = batch_masks(nb)
    x = kept + swap(sent, "batch", masks[0], nb).astype(f32)
    for m in masks[3:][::-1]:
        half = x.shape[0] // 2
        send, wide = lax.optimization_barrier((x[half:].astype(bf16), wide))
        x = x[:half] + swap(send, "batch", m, nb).astype(f32)
    return x, wide


def near_sum(x, m, nb, other):
    keep = members(near_masks(nb))
    send, other = lax.optimization_barrier((x.astype(bf16), other))
    got = swap(send, "batch", m, nb)
    rows = x.shape[0] // len(keep)
    at = [keep.index(k ^ m) * rows for k in keep]
    return x + jnp.concatenate([got[i : i + rows] for i in at], 0).astype(f32), other


def far_groups(nb, nt):
    rest = [1 << i for i in range(nt.bit_length() - 1)] + [m * nt for m in batch_masks(nb)[3:]]
    return [rest[i : i + 2] for i in range(0, len(rest), 2)]


def members(group):
    found = [0]
    for m in group:
        found = found + [a ^ m for a in found]
    return found


def place(me, group):
    return sum(jnp.where((me & m) != 0, 1 << i, 0) for i, m in enumerate(group))


def take(x, i):
    return lax.dynamic_index_in_dim(x, i, 0, False, allow_negative_indices=False)


def put(x, part, i):
    return lax.dynamic_update_index_in_dim(x, part, i, 0, allow_negative_indices=False)


def positions(nb, nt, me_b, me_t):
    me = me_b * nt + me_t
    near = [m * nt for m in near_masks(nb)]
    w = {("b", k): me_b ^ k for k in range(nb)}
    for group in [[nt], near] + far_groups(nb, nt):
        p = place(me, group)
        for j in range(1 << len(group)):
            w[tuple(group), j] = p ^ j
    w["at"] = w[(nt,), 0] * (1 << len(near)) + w[tuple(near), 0]
    return w


def split_pair(x, nb, nt, w):
    near = [m * nt for m in near_masks(nb)]
    n, found = nb * nt, members(near)
    halves = x.reshape(2, x.shape[0] // 2, x.shape[1])
    got = swap(take(halves, w[(nt,), 1]), AXES, nt, n)
    own = take(halves, w[(nt,), 0])
    x = (own.astype(f32) + got.astype(f32)).astype(bf16)
    xs = x.reshape(len(found), x.shape[0] // len(found), x.shape[1])
    return [take(xs, w[tuple(near), j]) for j in range(len(found))]


def split_near(pieces, nb, nt):
    found = members([m * nt for m in near_masks(nb)])
    return pieces[:1] + [swap(x, AXES, m, nb * nt) for x, m in zip(pieces[1:], found[1:])]


def join(x, group, w, n):
    found = members(group)
    out = jnp.zeros((len(found),) + x.shape, x.dtype)
    got = [x] + [swap(x, AXES, m, n) for m in found[1:]]
    for j, g in enumerate(got):
        out = put(out, g, w[tuple(group), j])
    return out.reshape(len(found) * x.shape[0], x.shape[1])


def finish_sum(x, nb, nt, w):
    n = nb * nt
    done = [[m * nt for m in near_masks(nb)]]
    for group in far_groups(nb, nt):
        found = members(group)
        size = len(found)
        if x.shape[0] % (8 * size):
            terms = [x.astype(f32)] + [swap(x, AXES, m, n).astype(f32) for m in found[1:]]
            while len(terms) > 1:
                terms = [a + b for a, b in zip(terms[::2], terms[1::2])]
            x = terms[0].astype(bf16)
            continue
        xs = x.reshape(size, x.shape[0] // size, x.shape[1])
        got = [
            swap(take(xs, w[tuple(group), j]), AXES, found[j], n)
            for j in range(1, size)
        ]
        own = take(xs, w[tuple(group), 0]).astype(f32)
        x = sum((g.astype(f32) for g in got), own).astype(bf16)
        done.append(group)
    for group in reversed(done):
        x = join(x, group, w, n)
    return x, swap(x, AXES, nt, n)


def hot(ids, width, dtype):
    return (ids[:, None] == jnp.arange(width, dtype=jnp.int32)[None, :]).astype(dtype)


def nt_dot(a, b):
    return lax.dot_general(a, b, (((1,), (1,)), ((), ())), preferred_element_type=f32)


def tn_dot(a, b, preferred_element_type=f32):
    return lax.dot_general(
        a, b, (((0,), (0,)), ((), ())), preferred_element_type=preferred_element_type
    )


def hot_columns(ids, width):
    found = lax.broadcasted_iota(jnp.int32, (width, ids.shape[1]), 0) == ids
    return jnp.where(found, 1.0, 0.0).astype(bf16)


def gelu_pair(x):
    c = 0.7978845608028654
    square = x * x
    t = jnp.tanh(c * (x + 0.044715 * (square * x)))
    half = 0.5 * (1.0 + t)
    slope = half + (0.5 * x) * ((1.0 - t) * (1.0 + t)) * (c + (3.0 * 0.044715 * c) * square)
    return (x * half).astype(bf16), slope


def forward(rows, one_hot, w_in, bias, w_out, dot=tn_dot):
    embed = w_out.shape[1]
    table = bias[...]
    table = jnp.concatenate([table, jnp.zeros((embed - table.shape[0], table.shape[1]), f32)], 0)
    added = None
    for _ in range(3):
        piece = table.astype(bf16)
        table = table - piece.astype(f32)
        part = dot(one_hot, piece, preferred_element_type=f32)
        added = part if added is None else added + part
    pre = jnp.dot(rows, w_in[...], preferred_element_type=f32) + added
    latent = jnp.dot(gelu_pair(pre)[0], w_out[...], preferred_element_type=f32)
    radius = jnp.sqrt(jnp.sum(latent * latent, axis=1, keepdims=True) + epsilon)
    return pre, latent, (latent / radius).astype(bf16)


def front_kernel(count, me_ref, *refs):
    held, (u_ref, unit_ref, own_ref, wide_ref), scratch, sems = (
        refs[:count],
        refs[count : count + 4],
        refs[count + 4 : -1],
        refs[-1],
    )
    copies = [
        pltpu.make_async_copy(src, dst, sems.at[i]) for i, (src, dst) in enumerate(zip(held, scratch))
    ]
    for copy in copies:
        copy.start()
    w_in, bias, w_out, neg_ids, neg_rows, ref_ids, ref_rows, owner, row, recording = scratch
    for copy in copies[:5]:
        copy.wait()
    embed, channels = w_out.shape[1], w_in.shape[0]
    one_hot = hot_columns(neg_ids[...], embed)
    unit_ref[...] = forward(neg_rows[...], one_hot, w_in, bias, w_out)[2]
    wide_ref[:, :channels] = neg_rows[...]
    wide_ref[:, channels:] = one_hot.astype(f32).T.astype(bf16)
    for copy in copies[5:7]:
        copy.wait()
    one_hot = hot_columns(ref_ids[...], embed)
    u_ref[...] = forward(ref_rows[...], one_hot, w_in, bias, w_out)[2]
    for copy in copies[7:]:
        copy.wait()
    pick_kernel(me_ref, owner, row, recording, own_ref)


def score_kernel(scale, count, order, me_ref, own, ids, u_ref, pool_ref, w_in, bias, w_out, *refs):
    rows = own[...]
    for got in refs[:count]:
        rows = rows + got[...]
    rows_ref, kept_ref, sent_ref, loss_ref, grad_ref, grad_pos, share_ref = refs[count:]
    rows_ref[...] = rows
    v = forward(rows, hot_columns(ids[...], w_out.shape[1]), w_in, bias, w_out)[2]
    u, pool = u_ref[...], pool_ref[...]
    uf, vf = u.astype(f32), v.astype(f32)
    pos_score = jnp.sum(uf * vf, axis=1, keepdims=True) / logit_sharpness_divisor
    exponent = jnp.exp(nt_dot(u, pool) / logit_sharpness_divisor - shift_bound)
    pos_exp = jnp.exp(pos_score - shift_bound)
    normalizer = pos_exp + jnp.sum(exponent, axis=1, keepdims=True)
    weights = (exponent / normalizer).astype(bf16)
    share_ref[...] = scale * tn_dot(weights, u)
    rows = kept_ref.shape[0] // len(order)
    for i, k in enumerate(order):
        at = pl.multiple_of((me_ref[0] ^ k) * rows, rows)
        kept_ref[i * rows : (i + 1) * rows, :] = share_ref[pl.ds(at, rows), :]
        at = pl.multiple_of((me_ref[0] ^ k ^ 1) * rows, rows)
        sent_ref[i * rows : (i + 1) * rows, :] = share_ref[pl.ds(at, rows), :].astype(bf16)
    loss = jnp.log(normalizer) + shift_bound - pos_score
    loss_ref[...] = jnp.broadcast_to(loss, uf.shape).T[:1]
    pull = pos_exp / normalizer - 1.0
    grad_ref[...] = scale * (jnp.dot(weights, pool, preferred_element_type=f32) + pull * vf)
    grad_pos[...] = scale * pull * uf


def pulled_back(rows, one_hot, grad_unit, w_in, bias, w_out, dot=tn_dot):
    pre, latent, _ = forward(rows, one_hot, w_in, bias, w_out, dot)
    power = jnp.sum(latent * latent, axis=1, keepdims=True) + epsilon
    radius = jnp.sqrt(power)
    inner = jnp.sum(latent * grad_unit, axis=1, keepdims=True)
    grad_latent = ((grad_unit - latent * (inner / (radius * radius))) / radius).astype(bf16)
    hidden, slope = gelu_pair(pre)
    return hidden, grad_latent, (nt_dot(grad_latent, w_out[...]) * slope).astype(bf16)


def piece_sizes(channels, embed, pieces):
    return channels // (2 * pieces), embed // pieces


def two_sets_kernel(pieces, a_rows, a_ids, a_grad, b_rows, b_ids, b_grad, w_in, bias, w_out, total):
    embed = w_out.shape[1]
    big, low, animal = 0.0, 0.0, 0.0
    for rows, ids, grad in ((a_rows, a_ids, a_grad), (b_rows, b_ids, b_grad)):
        one_hot = hot_columns(ids[...], embed)
        hidden, grad_latent, grad_pre = pulled_back(
            rows[...], one_hot, grad[...], w_in, bias, w_out
        )
        big = big + tn_dot(rows[...], grad_pre)
        low = low + tn_dot(grad_latent, hidden)
        animal = animal + jnp.dot(one_hot, grad_pre, preferred_element_type=f32)
    top, small = piece_sizes(w_in.shape[0], embed, pieces)
    for i in range(2 * pieces):
        at, q = i * (top + small), i % pieces
        below = low if i < pieces else animal
        total[at : at + top, :] = big[i * top : (i + 1) * top].astype(bf16)
        total[at + top : at + top + small, :] = below[q * small : (q + 1) * small].astype(bf16)


def near_kernel(pieces, at_ref, wide, mine, other, w_in, bias, w_out, *refs):
    terms, out, smalls = refs[:pieces], refs[pieces], refs[pieces + 1]
    channels, embed = w_in.shape[0], w_out.shape[1]
    grad_unit = jnp.concatenate([mine[...], other[...]], 0).astype(f32)
    one_hot = wide[:, channels:]
    hidden, grad_latent, grad_pre = pulled_back(
        wide[:, :channels], one_hot, grad_unit, w_in, bias, w_out, jnp.dot
    )
    top, small = piece_sizes(channels, embed, pieces)
    smalls[:embed, :] = tn_dot(grad_latent, hidden)
    smalls[embed:, :] = tn_dot(one_hot, grad_pre)
    at = at_ref[0]
    big = tn_dot(wide[:, pl.ds(pl.multiple_of(at * top, top), top)], grad_pre)
    low = smalls[pl.ds(pl.multiple_of(at * small, small), small), :]
    got = terms[0][...].astype(f32)
    for term in terms[1:]:
        got = got + term[...].astype(f32)
    out[:top, :] = (got[:top] + big).astype(bf16)
    out[top:, :] = (got[top:] + low).astype(bf16)


def finish_kernel(pieces, core_ref, own, other, grad_w_in, grad_w_out, grad_bias):
    half = grad_w_in.shape[0] // 2
    animals = grad_bias.shape[0]
    top, small = piece_sizes(2 * half, grad_w_out.shape[1], pieces)

    def put(first, second):
        lows = []
        for q in range(pieces):
            at = q * (top + small)
            grad_w_in[q * top : (q + 1) * top, :] = first[at : at + top, :]
            grad_w_in[half + q * top : half + (q + 1) * top, :] = second[at : at + top, :]
            lows.append(first[at + top : at + top + small, :])
        grad_w_out[...] = jnp.concatenate(lows, 0).astype(f32).T
        grad_bias[...] = second[top : top + animals, :].astype(f32)

    @pl.when(core_ref[0] == 0)
    def _():
        put(own, other)

    @pl.when(core_ref[0] != 0)
    def _():
        put(other, own)


def call(kernel, name, out, *args, scalars=0, limit=12, space=pltpu.VMEM, scratch=()):
    whole = pl.BlockSpec(memory_space=pltpu.VMEM)
    given = pl.BlockSpec(memory_space=space)
    shapes = [jax.ShapeDtypeStruct(*o) for o in out]
    return pl.pallas_call(
        kernel,
        name=name,
        out_shape=shapes,
        in_specs=[pl.BlockSpec(memory_space=pltpu.SMEM)] * scalars + [given] * (len(args) - scalars),
        out_specs=[whole] * len(out),
        scratch_shapes=list(scratch),
        compiler_params=pltpu.CompilerParams(vmem_limit_bytes=limit * 2**20),
    )(*args)


def slots(owner, row, nt, me_t):
    refs = row.shape[0]
    cap = 2 * refs // nt
    owner_hot = hot(owner, nt, jnp.int32)
    slot = jnp.sum((jnp.cumsum(owner_hot, axis=0) - owner_hot) * owner_hot, axis=1)
    found = []
    for k in range(1, nt):
        wanted = owner == (me_t ^ k)
        pick = wanted[None, :] & (slot[None, :] == jnp.arange(cap, dtype=jnp.int32)[:, None])
        ask = jnp.max(jnp.where(pick, row[None, :], -1), axis=1)
        found.append((pick, jnp.where(ask < 0, -1, me_t ^ k)[None, :], ask[None, :]))
    return found


def pick_kernel(me_ref, owner, row, recording, rows):
    wanted = jnp.where(owner[...] == me_ref[0], row[...], -1)
    one_hot = hot_columns(wanted, recording.shape[0])
    rows[...] = tn_dot(one_hot, recording[...]).astype(bf16)


def pick_rows(me, owner, row, recording):
    out = [((row.shape[1], recording.shape[1]), bf16)]
    return call(pick_kernel, "pick", out, me, owner, row, recording, scalars=1)[0]


def on_device(
    ref_rows,
    neg_rows,
    recording,
    pos_owner,
    pos_row,
    ref_animal,
    neg_animal,
    w_in,
    bias_animal,
    w_out,
):
    refs = ref_rows.shape[0]
    channels = w_in.shape[0]
    embed = w_out.shape[1]
    animals = bias_animal.shape[0]
    nt = lax.axis_size("tm")
    nb = lax.axis_size("batch")
    n = nt * nb
    me_b = lax.axis_index("batch")
    me_t = lax.axis_index("tm")
    w = positions(nb, nt, me_b, me_t)
    here, *found = lax.optimization_barrier((me_t.reshape(1), *w.values()))
    w = dict(zip(w, found))

    owner, row = pos_owner.reshape(1, refs), pos_row.reshape(1, refs)
    ref_ids, neg_ids = ref_animal[None, :], neg_animal[None, :]
    if nt == 2:
        asks = [(None, owner, row)]
    else:
        asks = slots(pos_owner[:, 0], pos_row, nt, me_t)
    asked = [(swap(o, "tm", k, nt), swap(r, "tm", k, nt)) for k, (_, o, r) in enumerate(asks, 1)]
    weights = (w_in, bias_animal, w_out)
    inputs = (*weights, neg_ids, neg_rows, ref_ids, ref_rows, owner, row, recording)
    inputs = [pltpu.with_memory_space_constraint(x, pltpu.HBM) for x in inputs]
    u, neg_unit, own, wide = call(
        functools.partial(front_kernel, len(inputs)),
        "front",
        [
            ((refs, embed), bf16),
            ((neg_rows.shape[0], embed), bf16),
            ((refs, recording.shape[1]), bf16),
            ((neg_rows.shape[0], channels + embed), bf16),
        ],
        here,
        *inputs,
        scalars=1,
        space=pltpu.HBM,
        scratch=[pltpu.VMEM(x.shape, x.dtype) for x in inputs]
        + [pltpu.SemaphoreType.DMA((len(inputs),))],
    )
    found = [pick_rows(here, o, r, recording) for o, r in asked]
    neg_unit, found = lax.optimization_barrier((neg_unit, found))
    got = [swap(f, "tm", k, nt) for k, f in enumerate(found, 1)]
    near = near_masks(nb)
    wide = spread(wide, near[:1], nb)
    pool, wide = gather_batch(neg_unit, nb, w, wide)
    wide = spread(wide, near[1:], nb)
    got = [
        g if pick is None else jnp.dot(pick.T.astype(bf16), g, preferred_element_type=bf16)
        for (pick, _, _), g in zip(asks, got)
    ]

    scale = float(refs * n) ** (-0.5) / logit_sharpness_divisor
    half = pool.shape[0] // 2
    out = [(ref_rows.shape, bf16), ((half, embed), f32), ((half, embed), bf16), ((1, refs), f32)]
    out += [(u.shape, f32), (u.shape, f32)]
    pos_rows, kept, sent, loss, grad_ref, grad_pos = call(
        functools.partial(score_kernel, scale, len(got), kept_order(nb)),
        "scores",
        out,
        w["b", 0].reshape(1),
        own,
        ref_ids,
        u,
        pool,
        *weights,
        *got,
        scalars=1,
        limit=max(12, 20 * refs * pool.shape[0] >> 20),
        scratch=[pltpu.VMEM((pool.shape[0], embed), f32)],
    )
    pieces = 1 << len(near)
    columns = w_in.shape[1]
    total = call(
        functools.partial(two_sets_kernel, pieces),
        "backward",
        [((channels + 2 * embed, columns), bf16)],
        *(ref_rows, ref_ids, grad_ref),
        *(pos_rows, ref_ids, grad_pos),
        *weights,
    )[0]
    mine, wide = scatter_batch(kept, sent, nb, wide)
    mine, total = near_sum(mine, near[0], nb, total)
    parts = split_pair(total, nb, nt, w)
    mine, parts = near_sum(mine, near[1], nb, parts)
    terms = split_near(parts, nb, nt)
    wide = spread(wide, [1], nb)
    mine = mine.astype(bf16)
    other = swap(mine, "batch", 1, nb)
    total = call(
        functools.partial(near_kernel, pieces),
        "backward_near",
        [(terms[0].shape, bf16)],
        w["at"].reshape(1),
        *(wide, mine, other, *weights, *terms),
        scalars=1,
        scratch=[pltpu.VMEM((2 * embed, columns), f32)],
    )[0]
    own, other = finish_sum(total, nb, nt, w)
    grad_w_in, grad_w_out, grad_bias = call(
        functools.partial(finish_kernel, pieces),
        "finish",
        [(w_in.shape, bf16), (w_out.shape, f32), (bias_animal.shape, f32)],
        w[(nt,), 0].reshape(1),
        own,
        other,
        scalars=1,
    )
    return (loss.reshape(refs), grad_w_in, grad_w_out, grad_bias)


def solution(mesh):
    in_specs = (
        P(("batch", "tm"), None),
        P(("batch", "tm"), None),
        P("tm", None),
        P(("batch", "tm"), None),
        P(("batch", "tm")),
        P(("batch", "tm")),
        P(("batch", "tm")),
        P(),
        P(),
        P(),
    )
    out_specs = (P(("batch", "tm")), P(), P(), P())
    return jax.shard_map(
        on_device, mesh=mesh, in_specs=in_specs, out_specs=out_specs, check_vma=False
    )
```

time: 87.2 us -> 83.4 us (0.956)
  local copies, waits for them, and re-layouts: 3.85 us -> 0.57 us
  waiting for transfers between devices: 38.2 us -> 36.5 us
  Pallas kernels: 11.6 us -> 12.6 us
    unnamed x27 -> x12, local copies, waits for them, and re-layouts: 3.35 us -> 0.03 us
    ppermute x25 -> x29, waiting for transfers between devices: 38.2 us -> 36.5 us  [swap(): return lax.ppermute(x, axes, [(i, i ^ mask) for i in range(n)])]
    pallas_call x6, Pallas kernels: 11.6 us -> 12.6 us  [call(): pl.pallas_call(kernel, name=name, out_shape=shapes, in_specs=[pl.BlockSpe...]
    ppermute x25 -> x29, starting transfers between devices: 32 us -> 32.1 us  [swap(): return lax.ppermute(x, axes, [(i, i ^ mask) for i in range(n)])]
  transfers between devices with their start and end apart: 25 -> 29, of which waited for: 20 -> 20; matrix products, arithmetic and copies ran while one was open for 0% -> 1% of each run, Pallas kernels for 8% -> 11%
where the time goes in v3:
time: 83.4 us; the launch traced here: 83.2 us
  waiting for transfers between devices  36.5 us (44%)
  starting transfers between devices  32.1 us (38%)
  Pallas kernels  12.6 us (15%)
  between operations  0.97 us (1%)
    ppermute x29, waiting for transfers between devices, swap(): return lax.ppermute(x, axes, [(i, i ^ mask) for i in range(n)])  36.5 us
    ppermute x29, starting transfers between devices, swap(): return lax.ppermute(x, axes, [(i, i ^ mask) for i in range(n)])  32.1 us
    pallas_call x6, Pallas kernels, call(): pl.pallas_call(kernel, name=name, out_shape=shapes, in_specs=[pl.BlockSpe...  12.6 us
  transfers between devices with their start and end apart: 29, of which 20 were waited for; matrix products, arithmetic and copies ran while one was open for 1% of the time, Pallas kernels for 11%

profile of v3, /device:TPU:0, one launch (start us, length us, event | category | flops | bytes accessed | tf_op | source)
XLA Modules:
  0.0 83.2 jit_solution(1063078581753302401)
XLA Ops:
  0.6 3.0 %collective-permute-start = (s32[1,256]{1,0:T(1,128)}, s32[1,256]{1,0:T(1,128)S(1)}, u32[]{:S(2)}, u32[]{:S(2)}) collective-permute-start(s32[1,256]{1,0:T(1,128)} %bitcast.131), channel_id=1, source_target_pairs={{0,1},{1,0},{2,3},{3,2},{4,5},{5,4},{6,7},{7,6},{8,9},{9,8},{10,11... | collective-permute-start | bytes 3080 | tf_op jit(solution)/shard_map/ppermute | solution.py:19
  3.7 3.6 %front.1 = (bf16[256,128]{1,0:T(8,128)(2,1)S(1)}, bf16[64,128]{1,0:T(8,128)(2,1)S(1)}, bf16[256,1024]{1,0:T(8,128)(2,1)S(1)}, bf16[64,1152]{1,0:T(8,128)(2,1)S(1)}) custom-call(s32[1]{0:T(128)} %bitcast.me_ref, bf16[1024,512]{1,0:T(8,128)(2,1)} %w_in.5, f32[8,512]{1,0:T(8,128)} %bias.5, bf16[512,128]{1,0:T(8,128)(2,1)} %w_out.5, s32[1,64]{1,0:T(1,128)} %bitcast.135, ...), custom_call_target="tpu_custom_call" | custom-call | tf_op jit(solution)/shard_map/front/pallas_call | solution.py:349
  7.3 2.0 %collective-permute-start.4 = (bf16[64,1152]{1,0:T(8,128)(2,1)S(1)}, bf16[64,1152]{1,0:T(8,128)(2,1)S(1)}, u32[]{:S(2)}, u32[]{:S(2)}) collective-permute-start(bf16[64,1152]{1,0:T(8,128)(2,1)S(1)} %get-tuple-element.67), channel_id=1, source_target_pairs={{0,4},{2,6},{4,0},{6,2},{8,12},{10,14},{12,8},{14,10},{16,20},{18,... | collective-permute-start | bytes 442376 | tf_op jit(solution)/shard_map/ppermute | solution.py:19
  9.9 2.7 %collective-permute-start.2 = (bf16[64,128]{1,0:T(8,128)(2,1)S(1)}, bf16[64,128]{1,0:T(8,128)(2,1)S(1)}, u32[]{:S(2)}, u32[]{:S(2)}) collective-permute-start(bf16[64,128]{1,0:T(8,128)(2,1)S(1)} %get-tuple-element.63), channel_id=1, source_target_pairs={{0,16},{2,18},{4,20},{6,22},{8,24},{10,26},{12,28},{14,30},{16,0},... | collective-permute-start | bytes 49160 | tf_op jit(solution)/shard_map/ppermute | solution.py:19
  16.2 2.5 %collective-permute-done.3 = bf16[128,128]{1,0:T(8,128)(2,1)S(1)} collective-permute-done((bf16[128,128]{1,0:T(8,128)(2,1)S(1)}, bf16[128,128]{1,0:T(8,128)(2,1)S(1)}, u32[]{:S(2)}, u32[]{:S(2)}) %collective-permute-start.3) | collective-permute-done | bytes 32800 | tf_op jit(solution)/shard_map/ppermute | solution.py:19
  18.8 1.9 %collective-permute-start.9 = (bf16[128,1152]{1,0:T(8,128)(2,1)S(1)}, bf16[128,1152]{1,0:T(8,128)(2,1)S(1)}, u32[]{:S(2)}, u32[]{:S(2)}) collective-permute-start(bf16[128,1152]{1,0:T(8,128)(2,1)S(1)} %pad_maximum_fusion.2), channel_id=1, source_target_pairs={{0,8},{2,10},{4,12},{6,14},{8,0},{10,2},{12,4},{14,6},{16,24},{18,... | collective-permute-start | bytes 884744 | tf_op jit(solution)/shard_map/ppermute | solution.py:19
  20.7 2.3 %collective-permute-done.5 = bf16[256,128]{1,0:T(8,128)(2,1)S(1)} collective-permute-done((bf16[256,128]{1,0:T(8,128)(2,1)S(1)}, bf16[256,128]{1,0:T(8,128)(2,1)S(1)}, u32[]{:S(2)}, u32[]{:S(2)}) %collective-permute-start.5) | collective-permute-done | bytes 65568 | tf_op jit(solution)/shard_map/ppermute | solution.py:19
  25.1 2.1 %scores.1 = (bf16[256,1024]{1,0:T(8,128)(2,1)S(1)}, f32[512,128]{1,0:T(8,128)S(1)}, bf16[512,128]{1,0:T(8,128)(2,1)S(1)}, f32[1,256]{1,0:T(1,128)}, f32[256,128]{1,0:T(8,128)S(1)}, /*index=5*/f32[256,128]{1,0:T(8,128)S(1)}) custom-call(s32[1]{0:T(128)} %bitcast.1.me_ref, bf16[256,1024]{1,0:T(8,128)(2,1)S(1)} %get-tuple-element.60.own, ...), custom_call_target="tpu_custom_call" | custom-call | tf_op jit(solution)/shard_map/scores/pallas_call | solution.py:349
  28.7 2.1 %collective-permute-start.11 = (bf16[256,128]{1,0:T(8,128)(2,1)S(1)}, bf16[256,128]{1,0:T(8,128)(2,1)S(1)}, u32[]{:S(2)}, u32[]{:S(2)}) collective-permute-start(bf16[256,128]{1,0:T(8,128)(2,1)S(1)} %slice.168), channel_id=1, source_target_pairs={{0,16},{2,18},{4,20},{6,22},{8,24},{10,26},{12,28},{14,30},{16,0},... | collective-permute-start | bytes 196616 | tf_op jit(solution)/shard_map/ppermute | solution.py:19
  30.8 3.0 %backward.1 = bf16[1280,512]{1,0:T(8,128)(2,1)S(1)} custom-call(bf16[256,1024]{1,0:T(8,128)(2,1)S(1)} %copy-done.2, s32[1,256]{1,0:T(1,128)S(1)} %bitcast.124, f32[256,128]{1,0:T(8,128)S(1)} %get-tuple-element.90.a_grad, bf16[256,1024]{1,0:T(8,128)(2,1)S(1)} %get-tuple-element.91.b_rows, s32[1,256]{1,0:T(1,128)S(1)} %bitcast.125, ...), custom_call_target="tpu_custom_call" | custom-call | tf_op jit(solution)/shard_map/backward/pallas_call | solution.py:349
  36.2 3.8 %collective-permute-done.12 = bf16[256,128]{1,0:T(8,128)(2,1)S(1)} collective-permute-done((bf16[256,128]{1,0:T(8,128)(2,1)S(1)}, bf16[256,128]{1,0:T(8,128)(2,1)S(1)}, u32[]{:S(2)}, u32[]{:S(2)}) %collective-permute-start.12) | collective-permute-done | bytes 65568 | tf_op jit(solution)/shard_map/ppermute | solution.py:19
  41.0 1.8 %collective-permute-start.17 = (bf16[160,512]{1,0:T(8,128)(2,1)S(1)}, bf16[160,512]{1,0:T(8,128)(2,1)S(1)}, u32[]{:S(2)}, u32[]{:S(2)}) collective-permute-start(bf16[160,512]{1,0:T(8,128)(2,1)S(1)} %get-tuple-element.103), channel_id=1, source_target_pairs={{0,8},{1,9},{2,10},{3,11},{4,12},{5,13},{6,14},{7,15},{8,0},{9,1},... | collective-permute-start | bytes 491528 | tf_op jit(solution)/shard_map/ppermute | solution.py:19
  46.7 2.1 %collective-permute-done.17.refs_2_ = bf16[160,512]{1,0:T(8,128)(2,1)S(1)} collective-permute-done((bf16[160,512]{1,0:T(8,128)(2,1)S(1)}, bf16[160,512]{1,0:T(8,128)(2,1)S(1)}, u32[]{:S(2)}, u32[]{:S(2)}) %collective-permute-start.17) | collective-permute-done | bytes 163872 | tf_op jit(solution)/shard_map/ppermute | solution.py:19
  48.8 2.7 %collective-permute-done.18.refs_3_ = bf16[160,512]{1,0:T(8,128)(2,1)S(1)} collective-permute-done((bf16[160,512]{1,0:T(8,128)(2,1)S(1)}, bf16[160,512]{1,0:T(8,128)(2,1)S(1)}, u32[]{:S(2)}, u32[]{:S(2)}) %collective-permute-start.18) | collective-permute-done | bytes 163872 | tf_op jit(solution)/shard_map/ppermute | solution.py:19
  51.6 2.2 %backward_near.1 = bf16[160,512]{1,0:T(8,128)(2,1)S(1)} custom-call(s32[1]{0:T(128)} %bitcast.25.at_ref, bf16[512,1152]{1,0:T(8,128)(2,1)S(1)} %pad_maximum_fusion.wide, bf16[256,128]{1,0:T(8,128)(2,1)S(1)} %add_convert_fusion.mine, bf16[256,128]{1,0:T(8,128)(2,1)S(1)} %collective-permute-done.15.other, bf16[1024,512]{1,0:T(8,128)(2,1)S(1)} %copy-done, ...), custom_call_target="tpu_custom_call" | custom-call | tf_op jit(solution)/shard_map/backward_near/pallas_call | solution.py:349
  55.4 2.3 %collective-permute-start.20 = (bf16[40,512]{1,0:T(8,128)(2,1)S(1)}, bf16[40,512]{1,0:T(8,128)(2,1)S(1)}, u32[]{:S(2)}, u32[]{:S(2)}) collective-permute-start(bf16[40,512]{1,0:T(8,128)(2,1)S(1)} %get-tuple-element.120), channel_id=1, source_target_pairs={{0,16},{1,17},{2,18},{3,19},{4,20},{5,21},{6,22},{7,23},{8,24},{9,... | collective-permute-start | bytes 122888 | tf_op jit(solution)/shard_map/ppermute | solution.py:19
  58.3 2.9 %collective-permute-done.20 = bf16[40,512]{1,0:T(8,128)(2,1)S(1)} collective-permute-done((bf16[40,512]{1,0:T(8,128)(2,1)S(1)}, bf16[40,512]{1,0:T(8,128)(2,1)S(1)}, u32[]{:S(2)}, u32[]{:S(2)}) %collective-permute-start.20) | collective-permute-done | bytes 40992 | tf_op jit(solution)/shard_map/ppermute | solution.py:19
  61.2 2.4 %collective-permute-done.21 = bf16[40,512]{1,0:T(8,128)(2,1)S(1)} collective-permute-done((bf16[40,512]{1,0:T(8,128)(2,1)S(1)}, bf16[40,512]{1,0:T(8,128)(2,1)S(1)}, u32[]{:S(2)}, u32[]{:S(2)}) %collective-permute-start.21) | collective-permute-done | bytes 40992 | tf_op jit(solution)/shard_map/ppermute | solution.py:19
  64.8 3.3 %collective-permute-start.24 = (bf16[40,512]{1,0:T(8,128)(2,1)S(1)}, bf16[40,512]{1,0:T(8,128)(2,1)S(1)}, u32[]{:S(2)}, u32[]{:S(2)}) collective-permute-start(bf16[40,512]{1,0:T(8,128)(2,1)S(1)} %get-tuple-element.113), channel_id=1, source_target_pairs={{0,17},{1,16},{2,19},{3,18},{4,21},{5,20},{6,23},{7,22},{8,25},{9,... | collective-permute-start | bytes 122888 | tf_op jit(solution)/shard_map/ppermute | solution.py:19
  69.1 1.8 %collective-permute-done.24 = bf16[40,512]{1,0:T(8,128)(2,1)S(1)} collective-permute-done((bf16[40,512]{1,0:T(8,128)(2,1)S(1)}, bf16[40,512]{1,0:T(8,128)(2,1)S(1)}, u32[]{:S(2)}, u32[]{:S(2)}) %collective-permute-start.24) | collective-permute-done | bytes 40992 | tf_op jit(solution)/shard_map/ppermute | solution.py:19
  71.8 1.8 %collective-permute-start.26 = (bf16[160,512]{1,0:T(8,128)(2,1)S(1)}, bf16[160,512]{1,0:T(8,128)(2,1)S(1)}, u32[]{:S(2)}, u32[]{:S(2)}) collective-permute-start(bf16[160,512]{1,0:T(8,128)(2,1)S(1)} %bitcast.128), channel_id=1, source_target_pairs={{0,8},{1,9},{2,10},{3,11},{4,12},{5,13},{6,14},{7,15},{8,0},{9,1},... | collective-permute-start | bytes 491528 | tf_op jit(solution)/shard_map/ppermute | solution.py:19
  74.5 1.8 %collective-permute-done.25 = bf16[160,512]{1,0:T(8,128)(2,1)S(1)} collective-permute-done((bf16[160,512]{1,0:T(8,128)(2,1)S(1)}, bf16[160,512]{1,0:T(8,128)(2,1)S(1)}, u32[]{:S(2)}, u32[]{:S(2)}) %collective-permute-start.25) | collective-permute-done | bytes 163872 | tf_op jit(solution)/shard_map/ppermute | solution.py:19
  77.2 2.7 %collective-permute-done.27 = bf16[160,512]{1,0:T(8,128)(2,1)S(1)} collective-permute-done((bf16[160,512]{1,0:T(8,128)(2,1)S(1)}, bf16[160,512]{1,0:T(8,128)(2,1)S(1)}, u32[]{:S(2)}, u32[]{:S(2)}) %collective-permute-start.27) | collective-permute-done | bytes 163872 | tf_op jit(solution)/shard_map/ppermute | solution.py:19
  80.0 2.1 %collective-permute-done.28.other = bf16[640,512]{1,0:T(8,128)(2,1)S(1)} collective-permute-done((bf16[640,512]{1,0:T(8,128)(2,1)S(1)}, bf16[640,512]{1,0:T(8,128)(2,1)S(1)}, u32[]{:S(2)}, u32[]{:S(2)}) %collective-permute-start.28) | collective-permute-done | bytes 655392 | tf_op jit(solution)/shard_map/ppermute | solution.py:19
  (96 shorter events, 23.4 us)
Async XLA Ops:
  0.6 8.7 %collective-permute-start = (s32[1,256]{1,0:T(1,128)}, s32[1,256]{1,0:T(1,128)S(1)}, u32[]{:S(2)}, u32[]{:S(2)}) collective-permute-start(s32[1,256]{1,0:T(1,128)} %bitcast.131), channel_id=1, source_target_pairs={{0,1},{1,0},{2,3},{3,2},{4,5},{5,4},{6,7},{7,6},{8,9},{9,8},{10,11... | collective-permute-start | bytes 3080 | tf_op jit(solution)/shard_map/ppermute | solution.py:19
  3.6 5.7 %collective-permute-start.1 = (s32[1,256]{1,0:T(1,128)}, s32[1,256]{1,0:T(1,128)S(1)}, u32[]{:S(2)}, u32[]{:S(2)}) collective-permute-start(s32[1,256]{1,0:T(1,128)} %bitcast.133), channel_id=1, source_target_pairs={{0,1},{1,0},{2,3},{3,2},{4,5},{5,4},{6,7},{7,6},{8,9},{9,8},{10,11... | collective-permute-start | bytes 3080 | tf_op jit(solution)/shard_map/ppermute | solution.py:19
  7.3 11.4 %collective-permute-start.4 = (bf16[64,1152]{1,0:T(8,128)(2,1)S(1)}, bf16[64,1152]{1,0:T(8,128)(2,1)S(1)}, u32[]{:S(2)}, u32[]{:S(2)}) collective-permute-start(bf16[64,1152]{1,0:T(8,128)(2,1)S(1)} %get-tuple-element.67), channel_id=1, source_target_pairs={{0,4},{2,6},{4,0},{6,2},{8,12},{10,14},{12,8},{14,10},{16,20},{18,... | collective-permute-start | bytes 442376 | tf_op jit(solution)/shard_map/ppermute | solution.py:19
  9.9 4.7 %collective-permute-start.2 = (bf16[64,128]{1,0:T(8,128)(2,1)S(1)}, bf16[64,128]{1,0:T(8,128)(2,1)S(1)}, u32[]{:S(2)}, u32[]{:S(2)}) collective-permute-start(bf16[64,128]{1,0:T(8,128)(2,1)S(1)} %get-tuple-element.63), channel_id=1, source_target_pairs={{0,16},{2,18},{4,20},{6,22},{8,24},{10,26},{12,28},{14,30},{16,0},... | collective-permute-start | bytes 49160 | tf_op jit(solution)/shard_map/ppermute | solution.py:19
  12.5 12.5 %collective-permute-start.7 = (bf16[256,1024]{1,0:T(8,128)(2,1)S(1)}, bf16[256,1024]{1,0:T(8,128)(2,1)S(1)}, u32[]{:S(2)}, u32[]{:S(2)}) collective-permute-start(bf16[256,1024]{1,0:T(8,128)(2,1)S(1)} %pick.1), channel_id=1, source_target_pairs={{0,1},{1,0},{2,3},{3,2},{4,5},{5,4},{6,7},{7,6},{8,9},{9,8},{10,11... | collective-permute-start | bytes 1572872 | tf_op jit(solution)/shard_map/ppermute | solution.py:19
  18.7 4.3 %collective-permute-start.5 = (bf16[256,128]{1,0:T(8,128)(2,1)S(1)}, bf16[256,128]{1,0:T(8,128)(2,1)S(1)}, u32[]{:S(2)}, u32[]{:S(2)}) collective-permute-start(bf16[256,128]{1,0:T(8,128)(2,1)S(1)} %pad_maximum_fusion.4), channel_id=1, source_target_pairs={{0,4},{2,6},{4,0},{6,2},{8,12},{10,14},{12,8},{14,10},{16,20},{18,... | collective-permute-start | bytes 196616 | tf_op jit(solution)/shard_map/ppermute | solution.py:19
  18.8 8.4 %collective-permute-start.9 = (bf16[128,1152]{1,0:T(8,128)(2,1)S(1)}, bf16[128,1152]{1,0:T(8,128)(2,1)S(1)}, u32[]{:S(2)}, u32[]{:S(2)}) collective-permute-start(bf16[128,1152]{1,0:T(8,128)(2,1)S(1)} %pad_maximum_fusion.2), channel_id=1, source_target_pairs={{0,8},{2,10},{4,12},{6,14},{8,0},{10,2},{12,4},{14,6},{16,24},{18,... | collective-permute-start | bytes 884744 | tf_op jit(solution)/shard_map/ppermute | solution.py:19
  28.7 6.6 %collective-permute-start.11 = (bf16[256,128]{1,0:T(8,128)(2,1)S(1)}, bf16[256,128]{1,0:T(8,128)(2,1)S(1)}, u32[]{:S(2)}, u32[]{:S(2)}) collective-permute-start(bf16[256,128]{1,0:T(8,128)(2,1)S(1)} %slice.168), channel_id=1, source_target_pairs={{0,16},{2,18},{4,20},{6,22},{8,24},{10,26},{12,28},{14,30},{16,0},... | collective-permute-start | bytes 196616 | tf_op jit(solution)/shard_map/ppermute | solution.py:19
  35.4 4.6 %collective-permute-start.13 = (bf16[640,512]{1,0:T(8,128)(2,1)S(1)}, bf16[640,512]{1,0:T(8,128)(2,1)S(1)}, u32[]{:S(2)}, u32[]{:S(2)}) collective-permute-start(bf16[640,512]{1,0:T(8,128)(2,1)S(1)} %dynamic-slice_bitcast_fusion), channel_id=1, source_target_pairs={{0,2},{1,3},{2,0},{3,1},{4,6},{5,7},{6,4},{7,5},{8,10},{9,11},{10,... | collective-permute-start | bytes 1966088 | tf_op jit(solution)/shard_map/ppermute | solution.py:19
  35.4 4.5 %collective-permute-start.12 = (bf16[256,128]{1,0:T(8,128)(2,1)S(1)}, bf16[256,128]{1,0:T(8,128)(2,1)S(1)}, u32[]{:S(2)}, u32[]{:S(2)}) collective-permute-start(bf16[256,128]{1,0:T(8,128)(2,1)S(1)} %fusion.5), channel_id=1, source_target_pairs={{0,4},{2,6},{4,0},{6,2},{8,12},{10,14},{12,8},{14,10},{16,20},{18,... | collective-permute-start | bytes 196616 | tf_op jit(solution)/shard_map/ppermute | solution.py:19
  36.0 9.4 %collective-permute-start.10 = (bf16[256,1152]{1,0:T(8,128)(2,1)S(1)}, bf16[256,1152]{1,0:T(8,128)(2,1)S(1)}, u32[]{:S(2)}, u32[]{:S(2)}) collective-permute-start(bf16[256,1152]{1,0:T(8,128)(2,1)S(1)} %pad_maximum_fusion.1), channel_id=1, source_target_pairs={{0,2},{2,0},{4,6},{6,4},{8,10},{10,8},{12,14},{14,12},{16,18},{18,... | collective-permute-start | bytes 1769480 | tf_op jit(solution)/shard_map/ppermute | solution.py:19
  40.3 5.1 %collective-permute-start.14 = (bf16[256,128]{1,0:T(8,128)(2,1)S(1)}, bf16[256,128]{1,0:T(8,128)(2,1)S(1)}, u32[]{:S(2)}, u32[]{:S(2)}) collective-permute-start(bf16[256,128]{1,0:T(8,128)(2,1)S(1)} %fusion.1), channel_id=1, source_target_pairs={{0,8},{2,10},{4,12},{6,14},{8,0},{10,2},{12,4},{14,6},{16,24},{18,... | collective-permute-start | bytes 196616 | tf_op jit(solution)/shard_map/ppermute | solution.py:19
  40.5 6.2 %collective-permute-start.16 = (bf16[160,512]{1,0:T(8,128)(2,1)S(1)}, bf16[160,512]{1,0:T(8,128)(2,1)S(1)}, u32[]{:S(2)}, u32[]{:S(2)}) collective-permute-start(bf16[160,512]{1,0:T(8,128)(2,1)S(1)} %get-tuple-element.102), channel_id=1, source_target_pairs={{0,4},{1,5},{2,6},{3,7},{4,0},{5,1},{6,2},{7,3},{8,12},{9,13},{10,... | collective-permute-start | bytes 491528 | tf_op jit(solution)/shard_map/ppermute | solution.py:19
  41.0 7.8 %collective-permute-start.17 = (bf16[160,512]{1,0:T(8,128)(2,1)S(1)}, bf16[160,512]{1,0:T(8,128)(2,1)S(1)}, u32[]{:S(2)}, u32[]{:S(2)}) collective-permute-start(bf16[160,512]{1,0:T(8,128)(2,1)S(1)} %get-tuple-element.103), channel_id=1, source_target_pairs={{0,8},{1,9},{2,10},{3,11},{4,12},{5,13},{6,14},{7,15},{8,0},{9,1},... | collective-permute-start | bytes 491528 | tf_op jit(solution)/shard_map/ppermute | solution.py:19
  42.9 8.7 %collective-permute-start.18 = (bf16[160,512]{1,0:T(8,128)(2,1)S(1)}, bf16[160,512]{1,0:T(8,128)(2,1)S(1)}, u32[]{:S(2)}, u32[]{:S(2)}) collective-permute-start(bf16[160,512]{1,0:T(8,128)(2,1)S(1)} %get-tuple-element.104), channel_id=1, source_target_pairs={{0,12},{1,13},{2,14},{3,15},{4,8},{5,9},{6,10},{7,11},{8,4},{9,5},... | collective-permute-start | bytes 491528 | tf_op jit(solution)/shard_map/ppermute | solution.py:19
  53.8 4.5 %collective-permute-start.19 = (bf16[40,512]{1,0:T(8,128)(2,1)S(1)}, bf16[40,512]{1,0:T(8,128)(2,1)S(1)}, u32[]{:S(2)}, u32[]{:S(2)}) collective-permute-start(bf16[40,512]{1,0:T(8,128)(2,1)S(1)} %get-tuple-element.118), channel_id=1, source_target_pairs={{0,1},{1,0},{2,3},{3,2},{4,5},{5,4},{6,7},{7,6},{8,9},{9,8},{10,11... | collective-permute-start | bytes 122888 | tf_op jit(solution)/shard_map/ppermute | solution.py:19
  55.4 5.8 %collective-permute-start.20 = (bf16[40,512]{1,0:T(8,128)(2,1)S(1)}, bf16[40,512]{1,0:T(8,128)(2,1)S(1)}, u32[]{:S(2)}, u32[]{:S(2)}) collective-permute-start(bf16[40,512]{1,0:T(8,128)(2,1)S(1)} %get-tuple-element.120), channel_id=1, source_target_pairs={{0,16},{1,17},{2,18},{3,19},{4,20},{5,21},{6,22},{7,23},{8,24},{9,... | collective-permute-start | bytes 122888 | tf_op jit(solution)/shard_map/ppermute | solution.py:19
  57.7 5.8 %collective-permute-start.21 = (bf16[40,512]{1,0:T(8,128)(2,1)S(1)}, bf16[40,512]{1,0:T(8,128)(2,1)S(1)}, u32[]{:S(2)}, u32[]{:S(2)}) collective-permute-start(bf16[40,512]{1,0:T(8,128)(2,1)S(1)} %get-tuple-element.119), channel_id=1, source_target_pairs={{0,17},{1,16},{2,19},{3,18},{4,21},{5,20},{6,23},{7,22},{8,25},{9,... | collective-permute-start | bytes 122888 | tf_op jit(solution)/shard_map/ppermute | solution.py:19
  63.6 4.5 %collective-permute-start.22 = (bf16[40,512]{1,0:T(8,128)(2,1)S(1)}, bf16[40,512]{1,0:T(8,128)(2,1)S(1)}, u32[]{:S(2)}, u32[]{:S(2)}) collective-permute-start(bf16[40,512]{1,0:T(8,128)(2,1)S(1)} %get-tuple-element.113), channel_id=1, source_target_pairs={{0,1},{1,0},{2,3},{3,2},{4,5},{5,4},{6,7},{7,6},{8,9},{9,8},{10,11... | collective-permute-start | bytes 122888 | tf_op jit(solution)/shard_map/ppermute | solution.py:19
  64.2 4.9 %collective-permute-start.23 = (bf16[40,512]{1,0:T(8,128)(2,1)S(1)}, bf16[40,512]{1,0:T(8,128)(2,1)S(1)}, u32[]{:S(2)}, u32[]{:S(2)}) collective-permute-start(bf16[40,512]{1,0:T(8,128)(2,1)S(1)} %get-tuple-element.113), channel_id=1, source_target_pairs={{0,16},{1,17},{2,18},{3,19},{4,20},{5,21},{6,22},{7,23},{8,24},{9,... | collective-permute-start | bytes 122888 | tf_op jit(solution)/shard_map/ppermute | solution.py:19
  64.8 6.1 %collective-permute-start.24 = (bf16[40,512]{1,0:T(8,128)(2,1)S(1)}, bf16[40,512]{1,0:T(8,128)(2,1)S(1)}, u32[]{:S(2)}, u32[]{:S(2)}) collective-permute-start(bf16[40,512]{1,0:T(8,128)(2,1)S(1)} %get-tuple-element.113), channel_id=1, source_target_pairs={{0,17},{1,16},{2,19},{3,18},{4,21},{5,20},{6,23},{7,22},{8,25},{9,... | collective-permute-start | bytes 122888 | tf_op jit(solution)/shard_map/ppermute | solution.py:19
  70.9 5.3 %collective-permute-start.25 = (bf16[160,512]{1,0:T(8,128)(2,1)S(1)}, bf16[160,512]{1,0:T(8,128)(2,1)S(1)}, u32[]{:S(2)}, u32[]{:S(2)}) collective-permute-start(bf16[160,512]{1,0:T(8,128)(2,1)S(1)} %bitcast.127), channel_id=1, source_target_pairs={{0,4},{1,5},{2,6},{3,7},{4,0},{5,1},{6,2},{7,3},{8,12},{9,13},{10,... | collective-permute-start | bytes 491528 | tf_op jit(solution)/shard_map/ppermute | solution.py:19
  71.8 5.3 %collective-permute-start.26 = (bf16[160,512]{1,0:T(8,128)(2,1)S(1)}, bf16[160,512]{1,0:T(8,128)(2,1)S(1)}, u32[]{:S(2)}, u32[]{:S(2)}) collective-permute-start(bf16[160,512]{1,0:T(8,128)(2,1)S(1)} %bitcast.128), channel_id=1, source_target_pairs={{0,8},{1,9},{2,10},{3,11},{4,12},{5,13},{6,14},{7,15},{8,0},{9,1},... | collective-permute-start | bytes 491528 | tf_op jit(solution)/shard_map/ppermute | solution.py:19
  73.6 6.2 %collective-permute-start.27 = (bf16[160,512]{1,0:T(8,128)(2,1)S(1)}, bf16[160,512]{1,0:T(8,128)(2,1)S(1)}, u32[]{:S(2)}, u32[]{:S(2)}) collective-permute-start(bf16[160,512]{1,0:T(8,128)(2,1)S(1)} %bitcast.129), channel_id=1, source_target_pairs={{0,12},{1,13},{2,14},{3,15},{4,8},{5,9},{6,10},{7,11},{8,4},{9,5},... | collective-permute-start | bytes 491528 | tf_op jit(solution)/shard_map/ppermute | solution.py:19
  (11 other events, 80.4 us)

commit v4 on v3

--- a/solution.py
+++ b/solution.py
@@ -23,7 +23,7 @@
     return [1 << i for i in range(nb.bit_length() - 1)]
 
 
-def gather_batch(x, nb, w, wide):
+def gather_batch(x, nb, w, wide, later):
     masks = batch_masks(nb)
     order = masks[2:][::-1] + masks[1:2] + masks[:1]
     rows = x.shape[0]
@@ -31,6 +31,8 @@
     for m in order:
         keys = list(parts)
         block = jnp.concatenate([parts[k] for k in keys], 0) if len(keys) > 1 else parts[keys[0]]
+        if len(keys) == 2:
+            block, later = lax.optimization_barrier((block, later))
         if m == masks[1]:
             block, wide = lax.optimization_barrier((block, wide))
         got = swap(block, "batch", m, nb)
@@ -39,7 +41,7 @@
     out = jnp.zeros((nb,) + x.shape, x.dtype)
     for k, part in parts.items():
         out = put(out, part, w["b", k])
-    return out.reshape((nb * rows,) + x.shape[1:]), wide
+    return out.reshape((nb * rows,) + x.shape[1:]), wide, later
 
 
 def near_masks(nb):
@@ -140,7 +142,7 @@
 
 def finish_sum(x, nb, nt, w):
     n = nb * nt
-    done = [[m * nt for m in near_masks(nb)]]
+    done = []
     for group in far_groups(nb, nt):
         found = members(group)
         size = len(found)
@@ -160,7 +162,9 @@
         done.append(group)
     for group in reversed(done):
         x = join(x, group, w, n)
-    return x, swap(x, AXES, nt, n)
+    found = members([m * nt for m in near_masks(nb)])
+    own = [x] + [swap(x, AXES, m, n) for m in found[1:]]
+    return own, [swap(x, AXES, nt, n) for x in own]
 
 
 def hot(ids, width, dtype):
@@ -202,16 +206,17 @@
         part = dot(one_hot, piece, preferred_element_type=f32)
         added = part if added is None else added + part
     pre = jnp.dot(rows, w_in[...], preferred_element_type=f32) + added
-    latent = jnp.dot(gelu_pair(pre)[0], w_out[...], preferred_element_type=f32)
+    hidden, slope = gelu_pair(pre)
+    latent = jnp.dot(hidden, w_out[...], preferred_element_type=f32)
     radius = jnp.sqrt(jnp.sum(latent * latent, axis=1, keepdims=True) + epsilon)
-    return pre, latent, (latent / radius).astype(bf16)
-
-
-def front_kernel(count, me_ref, *refs):
-    held, (u_ref, unit_ref, own_ref, wide_ref), scratch, sems = (
+    return (latent / radius).astype(bf16), latent, hidden, slope, pre
+
+
+def front_kernel(count, *refs):
+    held, (unit_ref, wide_ref), scratch, sems = (
         refs[:count],
-        refs[count : count + 4],
-        refs[count + 4 : -1],
+        refs[count : count + 2],
+        refs[count + 2 : -1],
         refs[-1],
     )
     copies = [
@@ -219,30 +224,44 @@
     ]
     for copy in copies:
         copy.start()
-    w_in, bias, w_out, neg_ids, neg_rows, ref_ids, ref_rows, owner, row, recording = scratch
-    for copy in copies[:5]:
+    w_in, bias, w_out, ids, rows = scratch
+    for copy in copies:
         copy.wait()
     embed, channels = w_out.shape[1], w_in.shape[0]
-    one_hot = hot_columns(neg_ids[...], embed)
-    unit_ref[...] = forward(neg_rows[...], one_hot, w_in, bias, w_out)[2]
-    wide_ref[:, :channels] = neg_rows[...]
+    one_hot = hot_columns(ids[...], embed)
+    unit_ref[...] = forward(rows[...], one_hot, w_in, bias, w_out)[0]
+    wide_ref[:, :channels] = rows[...]
     wide_ref[:, channels:] = one_hot.astype(f32).T.astype(bf16)
-    for copy in copies[5:7]:
-        copy.wait()
-    one_hot = hot_columns(ref_ids[...], embed)
-    u_ref[...] = forward(ref_rows[...], one_hot, w_in, bias, w_out)[2]
-    for copy in copies[7:]:
-        copy.wait()
-    pick_kernel(me_ref, owner, row, recording, own_ref)
-
-
-def score_kernel(scale, count, order, me_ref, own, ids, u_ref, pool_ref, w_in, bias, w_out, *refs):
-    rows = own[...]
-    for got in refs[:count]:
+
+
+def refs_kernel(rows, ids, w_in, bias, w_out, unit, latent, hidden, slope):
+    values = forward(rows[...], hot_columns(ids[...], w_out.shape[1]), w_in, bias, w_out)
+    for out, value in zip((unit, latent, hidden, slope), values):
+        out[...] = value
+
+
+def near_forward_kernel(wide, w_in, bias, w_out, latent, hidden, slope):
+    channels = w_in.shape[0]
+    values = forward(wide[:, :channels], wide[:, channels:], w_in, bias, w_out, jnp.dot)
+    for out, value in zip((latent, hidden, slope), values[1:]):
+        out[...] = value
+
+
+def score_kernel(
+    scale, count, order, me_ref, here_ref, owner, own, ids, u_ref, pool_ref, w_in, bias, w_out, *refs
+):
+    held = jnp.where(owner[...] == here_ref[0], 1.0, 0.0)
+    held = jnp.broadcast_to(held, (w_out.shape[1], held.shape[1])).T[:, :1] > 0.5
+    rows = refs[0][...]
+    for got in refs[1:count]:
         rows = rows + got[...]
-    rows_ref, kept_ref, sent_ref, loss_ref, grad_ref, grad_pos, share_ref = refs[count:]
+    rows = jnp.where(held, own[...].astype(f32), rows.astype(f32)).astype(bf16)
+    rows_ref, latent_ref, pre_ref, kept_ref, sent_ref, loss_ref, grad_ref, grad_pos = refs[count:-1]
+    share_ref = refs[-1]
     rows_ref[...] = rows
-    v = forward(rows, hot_columns(ids[...], w_out.shape[1]), w_in, bias, w_out)[2]
+    values = forward(rows, hot_columns(ids[...], w_out.shape[1]), w_in, bias, w_out)
+    v = values[0]
+    latent_ref[...], pre_ref[...] = values[1], values[4]
     u, pool = u_ref[...], pool_ref[...]
     uf, vf = u.astype(f32), v.astype(f32)
     pos_score = jnp.sum(uf * vf, axis=1, keepdims=True) / logit_sharpness_divisor
@@ -264,32 +283,31 @@
     grad_pos[...] = scale * pull * uf
 
 
-def pulled_back(rows, one_hot, grad_unit, w_in, bias, w_out, dot=tn_dot):
-    pre, latent, _ = forward(rows, one_hot, w_in, bias, w_out, dot)
+def pulled_back(latent, slope, grad_unit, w_out):
     power = jnp.sum(latent * latent, axis=1, keepdims=True) + epsilon
     radius = jnp.sqrt(power)
     inner = jnp.sum(latent * grad_unit, axis=1, keepdims=True)
     grad_latent = ((grad_unit - latent * (inner / (radius * radius))) / radius).astype(bf16)
-    hidden, slope = gelu_pair(pre)
-    return hidden, grad_latent, (nt_dot(grad_latent, w_out[...]) * slope).astype(bf16)
+    return grad_latent, (nt_dot(grad_latent, w_out[...]) * slope).astype(bf16)
 
 
 def piece_sizes(channels, embed, pieces):
     return channels // (2 * pieces), embed // pieces
 
 
-def two_sets_kernel(pieces, a_rows, a_ids, a_grad, b_rows, b_ids, b_grad, w_in, bias, w_out, total):
-    embed = w_out.shape[1]
-    big, low, animal = 0.0, 0.0, 0.0
-    for rows, ids, grad in ((a_rows, a_ids, a_grad), (b_rows, b_ids, b_grad)):
-        one_hot = hot_columns(ids[...], embed)
-        hidden, grad_latent, grad_pre = pulled_back(
-            rows[...], one_hot, grad[...], w_in, bias, w_out
-        )
-        big = big + tn_dot(rows[...], grad_pre)
-        low = low + tn_dot(grad_latent, hidden)
-        animal = animal + jnp.dot(one_hot, grad_pre, preferred_element_type=f32)
-    top, small = piece_sizes(w_in.shape[0], embed, pieces)
+def two_sets_kernel(
+    pieces, ids, a_rows, a_latent, a_hidden, a_slope, a_grad, b_rows, b_latent, b_pre, b_grad, w_out, total
+):
+    embed, channels = w_out.shape[1], a_rows.shape[1]
+    one_hot = hot_columns(ids[...], embed)
+    a_latent_grad, a_pre_grad = pulled_back(a_latent[...], a_slope[...], a_grad[...], w_out)
+    b_hidden, b_slope = gelu_pair(b_pre[...])
+    b_latent_grad, b_pre_grad = pulled_back(b_latent[...], b_slope, b_grad[...], w_out)
+    big = tn_dot(a_rows[...], a_pre_grad) + tn_dot(b_rows[...], b_pre_grad)
+    low = tn_dot(a_latent_grad, a_hidden[...]) + tn_dot(b_latent_grad, b_hidden)
+    animal = jnp.dot(one_hot, a_pre_grad, preferred_element_type=f32)
+    animal = animal + jnp.dot(one_hot, b_pre_grad, preferred_element_type=f32)
+    top, small = piece_sizes(channels, embed, pieces)
     for i in range(2 * pieces):
         at, q = i * (top + small), i % pieces
         below = low if i < pieces else animal
@@ -297,16 +315,15 @@
         total[at + top : at + top + small, :] = below[q * small : (q + 1) * small].astype(bf16)
 
 
-def near_kernel(pieces, at_ref, wide, mine, other, w_in, bias, w_out, *refs):
+def near_kernel(pieces, at_ref, wide, latent, hidden, slope, mine, other, w_out, *refs):
     terms, out, smalls = refs[:pieces], refs[pieces], refs[pieces + 1]
-    channels, embed = w_in.shape[0], w_out.shape[1]
+    embed = w_out.shape[1]
+    channels = wide.shape[1] - embed
     grad_unit = jnp.concatenate([mine[...], other[...]], 0).astype(f32)
     one_hot = wide[:, channels:]
-    hidden, grad_latent, grad_pre = pulled_back(
-        wide[:, :channels], one_hot, grad_unit, w_in, bias, w_out, jnp.dot
-    )
+    grad_latent, grad_pre = pulled_back(latent[...], slope[...], grad_unit, w_out)
     top, small = piece_sizes(channels, embed, pieces)
-    smalls[:embed, :] = tn_dot(grad_latent, hidden)
+    smalls[:embed, :] = tn_dot(grad_latent, hidden[...])
     smalls[embed:, :] = tn_dot(one_hot, grad_pre)
     at = at_ref[0]
     big = tn_dot(wide[:, pl.ds(pl.multiple_of(at * top, top), top)], grad_pre)
@@ -318,28 +335,18 @@
     out[top:, :] = (got[top:] + low).astype(bf16)
 
 
-def finish_kernel(pieces, core_ref, own, other, grad_w_in, grad_w_out, grad_bias):
-    half = grad_w_in.shape[0] // 2
-    animals = grad_bias.shape[0]
-    top, small = piece_sizes(2 * half, grad_w_out.shape[1], pieces)
-
-    def put(first, second):
-        lows = []
-        for q in range(pieces):
-            at = q * (top + small)
-            grad_w_in[q * top : (q + 1) * top, :] = first[at : at + top, :]
-            grad_w_in[half + q * top : half + (q + 1) * top, :] = second[at : at + top, :]
-            lows.append(first[at + top : at + top + small, :])
-        grad_w_out[...] = jnp.concatenate(lows, 0).astype(f32).T
-        grad_bias[...] = second[top : top + animals, :].astype(f32)
-
-    @pl.when(core_ref[0] == 0)
-    def _():
-        put(own, other)
-
-    @pl.when(core_ref[0] != 0)
-    def _():
-        put(other, own)
+def finish_kernel(pieces, core_ref, *refs):
+    places, own, other = (refs[i * pieces : (i + 1) * pieces] for i in range(3))
+    grad_w_in, grad_w_out, grad_bias, lows = refs[3 * pieces :]
+    embed = grad_w_out.shape[1]
+    top, small = piece_sizes(grad_w_in.shape[0], embed, pieces)
+    for half, held in ((core_ref[0], own), (1 - core_ref[0], other)):
+        for place_ref, piece in zip(places, held):
+            at = half * pieces + place_ref[0]
+            grad_w_in[pl.ds(pl.multiple_of(at * top, top), top), :] = piece[:top, :]
+            lows[pl.ds(pl.multiple_of(at * small, small), small), :] = piece[top:, :].astype(f32)
+    grad_w_out[...] = lows[:embed, :].T
+    grad_bias[...] = lows[embed : embed + grad_bias.shape[0], :]
 
 
 def call(kernel, name, out, *args, scalars=0, limit=12, space=pltpu.VMEM, scratch=()):
@@ -357,6 +364,10 @@
     )(*args)
 
 
+def sets(rows, embed, width):
+    return [((rows, embed), f32), ((rows, width), bf16), ((rows, width), f32)]
+
+
 def slots(owner, row, nt, me_t):
     refs = row.shape[0]
     cap = 2 * refs // nt
@@ -366,20 +377,18 @@
     for k in range(1, nt):
         wanted = owner == (me_t ^ k)
         pick = wanted[None, :] & (slot[None, :] == jnp.arange(cap, dtype=jnp.int32)[:, None])
-        ask = jnp.max(jnp.where(pick, row[None, :], -1), axis=1)
-        found.append((pick, jnp.where(ask < 0, -1, me_t ^ k)[None, :], ask[None, :]))
+        found.append((pick, jnp.max(jnp.where(pick, row[None, :], -1), axis=1)[None, :]))
     return found
 
 
-def pick_kernel(me_ref, owner, row, recording, rows):
-    wanted = jnp.where(owner[...] == me_ref[0], row[...], -1)
-    one_hot = hot_columns(wanted, recording.shape[0])
+def pick_kernel(row, recording, rows):
+    one_hot = hot_columns(row[...], recording.shape[0])
     rows[...] = tn_dot(one_hot, recording[...]).astype(bf16)
 
 
-def pick_rows(me, owner, row, recording):
+def pick_rows(row, recording):
     out = [((row.shape[1], recording.shape[1]), bf16)]
-    return call(pick_kernel, "pick", out, me, owner, row, recording, scalars=1)[0]
+    return call(pick_kernel, "pick", out, row, recording)[0]
 
 
 def on_device(
@@ -410,76 +419,88 @@
     owner, row = pos_owner.reshape(1, refs), pos_row.reshape(1, refs)
     ref_ids, neg_ids = ref_animal[None, :], neg_animal[None, :]
     if nt == 2:
-        asks = [(None, owner, row)]
+        asks = [(None, row)]
     else:
         asks = slots(pos_owner[:, 0], pos_row, nt, me_t)
-    asked = [(swap(o, "tm", k, nt), swap(r, "tm", k, nt)) for k, (_, o, r) in enumerate(asks, 1)]
+    asked = [swap(ask, "tm", k, nt) for k, (_, ask) in enumerate(asks, 1)]
     weights = (w_in, bias_animal, w_out)
-    inputs = (*weights, neg_ids, neg_rows, ref_ids, ref_rows, owner, row, recording)
+    hidden_width = w_in.shape[1]
+    inputs = (*weights, neg_ids, neg_rows)
     inputs = [pltpu.with_memory_space_constraint(x, pltpu.HBM) for x in inputs]
-    u, neg_unit, own, wide = call(
+    negs = neg_rows.shape[0]
+    here, *inputs = lax.optimization_barrier((here, *inputs))
+    neg_unit, wide = call(
         functools.partial(front_kernel, len(inputs)),
         "front",
-        [
-            ((refs, embed), bf16),
-            ((neg_rows.shape[0], embed), bf16),
-            ((refs, recording.shape[1]), bf16),
-            ((neg_rows.shape[0], channels + embed), bf16),
-        ],
-        here,
+        [((negs, embed), bf16), ((negs, channels + embed), bf16)],
         *inputs,
-        scalars=1,
         space=pltpu.HBM,
         scratch=[pltpu.VMEM(x.shape, x.dtype) for x in inputs]
         + [pltpu.SemaphoreType.DMA((len(inputs),))],
     )
-    found = [pick_rows(here, o, r, recording) for o, r in asked]
-    neg_unit, found = lax.optimization_barrier((neg_unit, found))
+    found = [pick_rows(ask, recording) for ask in asked]
+    neg_unit, found, wide = lax.optimization_barrier((neg_unit, found, wide))
     got = [swap(f, "tm", k, nt) for k, f in enumerate(found, 1)]
     near = near_masks(nb)
     wide = spread(wide, near[:1], nb)
-    pool, wide = gather_batch(neg_unit, nb, w, wide)
+    pool, wide, (ref_rows, row) = gather_batch(neg_unit, nb, w, wide, (ref_rows, row))
     wide = spread(wide, near[1:], nb)
+    u, ref_latent, ref_hidden, ref_slope = call(
+        refs_kernel,
+        "refs",
+        [((refs, embed), bf16), *sets(refs, embed, hidden_width)],
+        *(ref_rows, ref_ids, *weights),
+    )
+    own = pick_rows(row, recording)
     got = [
         g if pick is None else jnp.dot(pick.T.astype(bf16), g, preferred_element_type=bf16)
-        for (pick, _, _), g in zip(asks, got)
+        for (pick, _), g in zip(asks, got)
     ]
 
     scale = float(refs * n) ** (-0.5) / logit_sharpness_divisor
     half = pool.shape[0] // 2
-    out = [(ref_rows.shape, bf16), ((half, embed), f32), ((half, embed), bf16), ((1, refs), f32)]
+    out = [(ref_rows.shape, bf16), (u.shape, f32), ((refs, hidden_width), f32)]
+    out += [((half, embed), f32), ((half, embed), bf16), ((1, refs), f32)]
     out += [(u.shape, f32), (u.shape, f32)]
-    pos_rows, kept, sent, loss, grad_ref, grad_pos = call(
+    pos_rows, pos_latent, pos_pre, kept, sent, loss, grad_ref, grad_pos = call(
         functools.partial(score_kernel, scale, len(got), kept_order(nb)),
         "scores",
         out,
         w["b", 0].reshape(1),
+        here,
+        owner,
         own,
         ref_ids,
         u,
         pool,
         *weights,
         *got,
-        scalars=1,
+        scalars=2,
         limit=max(12, 20 * refs * pool.shape[0] >> 20),
         scratch=[pltpu.VMEM((pool.shape[0], embed), f32)],
     )
     pieces = 1 << len(near)
-    columns = w_in.shape[1]
     total = call(
         functools.partial(two_sets_kernel, pieces),
         "backward",
-        [((channels + 2 * embed, columns), bf16)],
-        *(ref_rows, ref_ids, grad_ref),
-        *(pos_rows, ref_ids, grad_pos),
-        *weights,
+        [((channels + 2 * embed, hidden_width), bf16)],
+        ref_ids,
+        *(ref_rows, ref_latent, ref_hidden, ref_slope, grad_ref),
+        *(pos_rows, pos_latent, pos_pre, grad_pos),
+        w_out,
     )[0]
     mine, wide = scatter_batch(kept, sent, nb, wide)
-    mine, total = near_sum(mine, near[0], nb, total)
+    wide = spread(wide, [1], nb)
     parts = split_pair(total, nb, nt, w)
-    mine, parts = near_sum(mine, near[1], nb, parts)
+    mine, (parts, wide) = near_sum(mine, near[0], nb, (parts, wide))
+    near_values = call(
+        near_forward_kernel,
+        "near_forward",
+        sets(wide.shape[0], embed, hidden_width),
+        *(wide, *weights),
+    )
     terms = split_near(parts, nb, nt)
-    wide = spread(wide, [1], nb)
+    mine, near_values = near_sum(mine, near[1], nb, near_values)
     mine = mine.astype(bf16)
     other = swap(mine, "batch", 1, nb)
     total = call(
@@ -487,19 +508,20 @@
         "backward_near",
         [(terms[0].shape, bf16)],
         w["at"].reshape(1),
-        *(wide, mine, other, *weights, *terms),
+        *(wide, *near_values, mine, other, w_out, *terms),
         scalars=1,
-        scratch=[pltpu.VMEM((2 * embed, columns), f32)],
+        scratch=[pltpu.VMEM((2 * embed, hidden_width), f32)],
     )[0]
     own, other = finish_sum(total, nb, nt, w)
+    places = [w[tuple(m * nt for m in near), j].reshape(1) for j in range(pieces)]
     grad_w_in, grad_w_out, grad_bias = call(
         functools.partial(finish_kernel, pieces),
         "finish",
         [(w_in.shape, bf16), (w_out.shape, f32), (bias_animal.shape, f32)],
         w[(nt,), 0].reshape(1),
-        own,
-        other,
-        scalars=1,
+        *(*places, *own, *other),
+        scalars=1 + pieces,
+        scratch=[pltpu.VMEM((2 * embed, hidden_width), f32)],
     )
     return (loss.reshape(refs), grad_w_in, grad_w_out, grad_bias)
 

time: 83.4 us -> 77.8 us (0.933)
  waiting for transfers between devices: 36.5 us -> 33.7 us
  starting transfers between devices: 32.1 us -> 30.6 us
  Pallas kernels: 12.6 us -> 11.2 us
    ppermute x29 -> x31, waiting for transfers between devices: 36.5 us -> 33.7 us  [swap(): return lax.ppermute(x, axes, [(i, i ^ mask) for i in range(n)])]
    ppermute x29 -> x31, starting transfers between devices: 32.1 us -> 30.6 us  [swap(): return lax.ppermute(x, axes, [(i, i ^ mask) for i in range(n)])]
    pallas_call x6 -> x9, Pallas kernels: 12.6 us -> 11.2 us  [call(): pl.pallas_call(kernel, name=name, out_shape=shapes, in_specs=[pl.BlockSpe...]
  transfers between devices with their start and end apart: 29 -> 31, of which waited for: 20 -> 17; matrix products, arithmetic and copies ran while one was open for 1% -> 1% of each run, Pallas kernels for 11% -> 12%
where the time goes in v4:
time: 77.8 us; the launch traced here: 77.6 us
  waiting for transfers between devices  33.7 us (43%)
  starting transfers between devices  30.6 us (39%)
  Pallas kernels  11.2 us (14%)
  between operations  1.04 us (1%)
    ppermute x31, waiting for transfers between devices, swap(): return lax.ppermute(x, axes, [(i, i ^ mask) for i in range(n)])  33.7 us
    ppermute x31, starting transfers between devices, swap(): return lax.ppermute(x, axes, [(i, i ^ mask) for i in range(n)])  30.6 us
    pallas_call x9, Pallas kernels, call(): pl.pallas_call(kernel, name=name, out_shape=shapes, in_specs=[pl.BlockSpe...  11.2 us
  transfers between devices with their start and end apart: 31, of which 17 were waited for; matrix products, arithmetic and copies ran while one was open for 1% of the time, Pallas kernels for 12%

profile of v4, /device:TPU:0, one launch (start us, length us, event | category | flops | bytes accessed | tf_op | source)
XLA Modules:
  0.0 77.6 jit_solution(18004402858236938234)
XLA Ops:
  0.6 3.0 %collective-permute-start = (s32[1,256]{1,0:T(1,128)}, s32[1,256]{1,0:T(1,128)S(1)}, u32[]{:S(2)}, u32[]{:S(2)}) collective-permute-start(s32[1,256]{1,0:T(1,128)} %bitcast.123), channel_id=1, source_target_pairs={{0,1},{1,0},{2,3},{3,2},{4,5},{5,4},{6,7},{7,6},{8,9},{9,8},{10,11... | collective-permute-start | bytes 3080 | tf_op jit(solution)/shard_map/ppermute | solution.py:19
  3.6 2.0 %front.1 = (bf16[64,128]{1,0:T(8,128)(2,1)S(1)}, bf16[64,1152]{1,0:T(8,128)(2,1)S(1)}) custom-call(bf16[1024,512]{1,0:T(8,128)(2,1)} %w_in.5, f32[8,512]{1,0:T(8,128)} %bias.5, bf16[512,128]{1,0:T(8,128)(2,1)} %w_out.9, s32[1,64]{1,0:T(1,128)} %bitcast.126, bf16[64,1024]{1,0:T(8,128)(2,1)} %refs_4_), custom_call_target="tpu_custom_call" | custom-call | tf_op jit(solution)/shard_map/front/pallas_call | solution.py:356
  6.2 2.9 %collective-permute-start.1 = (bf16[64,128]{1,0:T(8,128)(2,1)S(1)}, bf16[64,128]{1,0:T(8,128)(2,1)S(1)}, u32[]{:S(2)}, u32[]{:S(2)}) collective-permute-start(bf16[64,128]{1,0:T(8,128)(2,1)S(1)} %get-tuple-element.88), channel_id=1, source_target_pairs={{0,16},{2,18},{4,20},{6,22},{8,24},{10,26},{12,28},{14,30},{16,0},... | collective-permute-start | bytes 49160 | tf_op jit(solution)/shard_map/ppermute | solution.py:19
  9.1 1.5 %collective-permute-start.3 = (bf16[64,1152]{1,0:T(8,128)(2,1)S(1)}, bf16[64,1152]{1,0:T(8,128)(2,1)S(1)}, u32[]{:S(2)}, u32[]{:S(2)}) collective-permute-start(bf16[64,1152]{1,0:T(8,128)(2,1)S(1)} %get-tuple-element.96), channel_id=1, source_target_pairs={{0,4},{2,6},{4,0},{6,2},{8,12},{10,14},{12,8},{14,10},{16,20},{18,... | collective-permute-start | bytes 442376 | tf_op jit(solution)/shard_map/ppermute | solution.py:19
  10.6 1.5 %collective-permute-start.6 = (bf16[256,1024]{1,0:T(8,128)(2,1)S(1)}, bf16[256,1024]{1,0:T(8,128)(2,1)S(1)}, u32[]{:S(2)}, u32[]{:S(2)}) collective-permute-start(bf16[256,1024]{1,0:T(8,128)(2,1)S(1)} %pick.2), channel_id=1, source_target_pairs={{0,1},{1,0},{2,3},{3,2},{4,5},{5,4},{6,7},{7,6},{8,9},{9,8},{10,11... | collective-permute-start | bytes 1572872 | tf_op jit(solution)/shard_map/ppermute | solution.py:19
  12.2 1.6 %collective-permute-start.2 = (bf16[128,128]{1,0:T(8,128)(2,1)S(1)}, bf16[128,128]{1,0:T(8,128)(2,1)S(1)}, u32[]{:S(2)}, u32[]{:S(2)}) collective-permute-start(bf16[128,128]{1,0:T(8,128)(2,1)S(1)} %pad_maximum_fusion.6), channel_id=1, source_target_pairs={{0,8},{2,10},{4,12},{6,14},{8,0},{10,2},{12,4},{14,6},{16,24},{18,... | collective-permute-start | bytes 98312 | tf_op jit(solution)/shard_map/ppermute | solution.py:19
  16.8 1.6 %collective-permute-start.8 = (bf16[128,1152]{1,0:T(8,128)(2,1)S(1)}, bf16[128,1152]{1,0:T(8,128)(2,1)S(1)}, u32[]{:S(2)}, u32[]{:S(2)}) collective-permute-start(bf16[128,1152]{1,0:T(8,128)(2,1)S(1)} %pad_maximum_fusion.2), channel_id=1, source_target_pairs={{0,8},{2,10},{4,12},{6,14},{8,0},{10,2},{12,4},{14,6},{16,24},{18,... | collective-permute-start | bytes 884744 | tf_op jit(solution)/shard_map/ppermute | solution.py:19
  18.4 2.2 %collective-permute-done.4 = bf16[256,128]{1,0:T(8,128)(2,1)S(1)} collective-permute-done((bf16[256,128]{1,0:T(8,128)(2,1)S(1)}, bf16[256,128]{1,0:T(8,128)(2,1)S(1)}, u32[]{:S(2)}, u32[]{:S(2)}) %collective-permute-start.4) | collective-permute-done | bytes 65568 | tf_op jit(solution)/shard_map/ppermute | solution.py:19
  23.2 2.3 %scores.1 = (bf16[256,1024]{1,0:T(8,128)(2,1)S(1)}, f32[256,128]{1,0:T(8,128)S(1)}, f32[256,512]{1,0:T(8,128)S(1)}, f32[512,128]{1,0:T(8,128)S(1)}, bf16[512,128...) custom-call(s32[1]{0:T(128)} %bitcast.1.me_ref, s32[1]{0:T(128)} %bitcast.here_ref, ...), custom_call_target="tpu_custom_call" | custom-call | tf_op jit(solution)/shard_map/scores/pallas_call | solution.py:356
  28.2 6.2 %collective-permute-done.9 = bf16[256,128]{1,0:T(8,128)(2,1)S(1)} collective-permute-done((bf16[256,128]{1,0:T(8,128)(2,1)S(1)}, bf16[256,128]{1,0:T(8,128)(2,1)S(1)}, u32[]{:S(2)}, u32[]{:S(2)}) %collective-permute-start.9) | collective-permute-done | bytes 65568 | tf_op jit(solution)/shard_map/ppermute | solution.py:19
  35.3 1.6 %near_forward.1 = (f32[512,128]{1,0:T(8,128)S(1)}, bf16[512,512]{1,0:T(8,128)(2,1)S(1)}, f32[512,512]{1,0:T(8,128)S(1)}) custom-call(bf16[512,1152]{1,0:T(8,128)(2,1)S(1)} %pad_maximum_fusion.wide, bf16[1024,512]{1,0:T(8,128)(2,1)S(1)} %copy-done, f32[8,512]{1,0:T(8,128)S(1)} %copy-done.4, bf16[512,128]{1,0:T(8,128)(2,1)S(1)} %copy-done.1), custom_call_target="tpu_custom_call" | custom-call | tf_op jit(solution)/shard_map/near_forward/pallas_call | solution.py:356
  36.9 2.2 %collective-permute-done.12 = bf16[256,128]{1,0:T(8,128)(2,1)S(1)} collective-permute-done((bf16[256,128]{1,0:T(8,128)(2,1)S(1)}, bf16[256,128]{1,0:T(8,128)(2,1)S(1)}, u32[]{:S(2)}, u32[]{:S(2)}) %collective-permute-start.12) | collective-permute-done | bytes 65568 | tf_op jit(solution)/shard_map/ppermute | solution.py:19
  39.9 1.9 %collective-permute-start.16 = (bf16[160,512]{1,0:T(8,128)(2,1)S(1)}, bf16[160,512]{1,0:T(8,128)(2,1)S(1)}, u32[]{:S(2)}, u32[]{:S(2)}) collective-permute-start(bf16[160,512]{1,0:T(8,128)(2,1)S(1)} %get-tuple-element.143), channel_id=1, source_target_pairs={{0,8},{1,9},{2,10},{3,11},{4,12},{5,13},{6,14},{7,15},{8,0},{9,1},... | collective-permute-start | bytes 491528 | tf_op jit(solution)/shard_map/ppermute | solution.py:19
  44.3 1.8 %collective-permute-done.15.refs_1_ = bf16[160,512]{1,0:T(8,128)(2,1)S(1)} collective-permute-done((bf16[160,512]{1,0:T(8,128)(2,1)S(1)}, bf16[160,512]{1,0:T(8,128)(2,1)S(1)}, u32[]{:S(2)}, u32[]{:S(2)}) %collective-permute-start.15) | collective-permute-done | bytes 163872 | tf_op jit(solution)/shard_map/ppermute | solution.py:19
  46.1 2.4 %collective-permute-done.17.refs_3_ = bf16[160,512]{1,0:T(8,128)(2,1)S(1)} collective-permute-done((bf16[160,512]{1,0:T(8,128)(2,1)S(1)}, bf16[160,512]{1,0:T(8,128)(2,1)S(1)}, u32[]{:S(2)}, u32[]{:S(2)}) %collective-permute-start.17) | collective-permute-done | bytes 163872 | tf_op jit(solution)/shard_map/ppermute | solution.py:19
  49.1 3.7 %collective-permute-start.20 = (bf16[40,512]{1,0:T(8,128)(2,1)S(1)}, bf16[40,512]{1,0:T(8,128)(2,1)S(1)}, u32[]{:S(2)}, u32[]{:S(2)}) collective-permute-start(bf16[40,512]{1,0:T(8,128)(2,1)S(1)} %get-tuple-element.159), channel_id=1, source_target_pairs={{0,17},{1,16},{2,19},{3,18},{4,21},{5,20},{6,23},{7,22},{8,25},{9,... | collective-permute-start | bytes 122888 | tf_op jit(solution)/shard_map/ppermute | solution.py:19
  55.0 2.8 %collective-permute-done.19 = bf16[40,512]{1,0:T(8,128)(2,1)S(1)} collective-permute-done((bf16[40,512]{1,0:T(8,128)(2,1)S(1)}, bf16[40,512]{1,0:T(8,128)(2,1)S(1)}, u32[]{:S(2)}, u32[]{:S(2)}) %collective-permute-start.19) | collective-permute-done | bytes 40992 | tf_op jit(solution)/shard_map/ppermute | solution.py:19
  58.7 1.6 %collective-permute-start.22 = (bf16[40,512]{1,0:T(8,128)(2,1)S(1)}, bf16[40,512]{1,0:T(8,128)(2,1)S(1)}, u32[]{:S(2)}, u32[]{:S(2)}) collective-permute-start(bf16[40,512]{1,0:T(8,128)(2,1)S(1)} %get-tuple-element.153), channel_id=1, source_target_pairs={{0,16},{1,17},{2,18},{3,19},{4,20},{5,21},{6,22},{7,23},{8,24},{9,... | collective-permute-start | bytes 122888 | tf_op jit(solution)/shard_map/ppermute | solution.py:19
  60.3 2.0 %collective-permute-start.23 = (bf16[40,512]{1,0:T(8,128)(2,1)S(1)}, bf16[40,512]{1,0:T(8,128)(2,1)S(1)}, u32[]{:S(2)}, u32[]{:S(2)}) collective-permute-start(bf16[40,512]{1,0:T(8,128)(2,1)S(1)} %get-tuple-element.153), channel_id=1, source_target_pairs={{0,17},{1,16},{2,19},{3,18},{4,21},{5,20},{6,23},{7,22},{8,25},{9,... | collective-permute-start | bytes 122888 | tf_op jit(solution)/shard_map/ppermute | solution.py:19
  62.3 1.6 %collective-permute-done.22 = bf16[40,512]{1,0:T(8,128)(2,1)S(1)} collective-permute-done((bf16[40,512]{1,0:T(8,128)(2,1)S(1)}, bf16[40,512]{1,0:T(8,128)(2,1)S(1)}, u32[]{:S(2)}, u32[]{:S(2)}) %collective-permute-start.22) | collective-permute-done | bytes 40992 | tf_op jit(solution)/shard_map/ppermute | solution.py:19
  63.8 2.6 %collective-permute-done.23 = bf16[40,512]{1,0:T(8,128)(2,1)S(1)} collective-permute-done((bf16[40,512]{1,0:T(8,128)(2,1)S(1)}, bf16[40,512]{1,0:T(8,128)(2,1)S(1)}, u32[]{:S(2)}, u32[]{:S(2)}) %collective-permute-start.23) | collective-permute-done | bytes 40992 | tf_op jit(solution)/shard_map/ppermute | solution.py:19
  68.3 1.7 %collective-permute-start.26 = (bf16[160,512]{1,0:T(8,128)(2,1)S(1)}, bf16[160,512]{1,0:T(8,128)(2,1)S(1)}, u32[]{:S(2)}, u32[]{:S(2)}) collective-permute-start(bf16[160,512]{1,0:T(8,128)(2,1)S(1)} %bitcast.116), channel_id=1, source_target_pairs={{0,12},{1,13},{2,14},{3,15},{4,8},{5,9},{6,10},{7,11},{8,4},{9,5},... | collective-permute-start | bytes 491528 | tf_op jit(solution)/shard_map/ppermute | solution.py:19
  69.9 1.8 %collective-permute-done.24.refs_5_ = bf16[160,512]{1,0:T(8,128)(2,1)S(1)} collective-permute-done((bf16[160,512]{1,0:T(8,128)(2,1)S(1)}, bf16[160,512]{1,0:T(8,128)(2,1)S(1)}, u32[]{:S(2)}, u32[]{:S(2)}) %collective-permute-start.24) | collective-permute-done | bytes 163872 | tf_op jit(solution)/shard_map/ppermute | solution.py:19
  72.3 2.7 %collective-permute-done.26.refs_7_ = bf16[160,512]{1,0:T(8,128)(2,1)S(1)} collective-permute-done((bf16[160,512]{1,0:T(8,128)(2,1)S(1)}, bf16[160,512]{1,0:T(8,128)(2,1)S(1)}, u32[]{:S(2)}, u32[]{:S(2)}) %collective-permute-start.26) | collective-permute-done | bytes 163872 | tf_op jit(solution)/shard_map/ppermute | solution.py:19
  (102 shorter events, 21.6 us)
Async XLA Ops:
  0.6 5.0 %collective-permute-start = (s32[1,256]{1,0:T(1,128)}, s32[1,256]{1,0:T(1,128)S(1)}, u32[]{:S(2)}, u32[]{:S(2)}) collective-permute-start(s32[1,256]{1,0:T(1,128)} %bitcast.123), channel_id=1, source_target_pairs={{0,1},{1,0},{2,3},{3,2},{4,5},{5,4},{6,7},{7,6},{8,9},{9,8},{10,11... | collective-permute-start | bytes 3080 | tf_op jit(solution)/shard_map/ppermute | solution.py:19
  6.2 6.0 %collective-permute-start.1 = (bf16[64,128]{1,0:T(8,128)(2,1)S(1)}, bf16[64,128]{1,0:T(8,128)(2,1)S(1)}, u32[]{:S(2)}, u32[]{:S(2)}) collective-permute-start(bf16[64,128]{1,0:T(8,128)(2,1)S(1)} %get-tuple-element.88), channel_id=1, source_target_pairs={{0,16},{2,18},{4,20},{6,22},{8,24},{10,26},{12,28},{14,30},{16,0},... | collective-permute-start | bytes 49160 | tf_op jit(solution)/shard_map/ppermute | solution.py:19
  9.1 7.1 %collective-permute-start.3 = (bf16[64,1152]{1,0:T(8,128)(2,1)S(1)}, bf16[64,1152]{1,0:T(8,128)(2,1)S(1)}, u32[]{:S(2)}, u32[]{:S(2)}) collective-permute-start(bf16[64,1152]{1,0:T(8,128)(2,1)S(1)} %get-tuple-element.96), channel_id=1, source_target_pairs={{0,4},{2,6},{4,0},{6,2},{8,12},{10,14},{12,8},{14,10},{16,20},{18,... | collective-permute-start | bytes 442376 | tf_op jit(solution)/shard_map/ppermute | solution.py:19
  10.6 12.6 %collective-permute-start.6 = (bf16[256,1024]{1,0:T(8,128)(2,1)S(1)}, bf16[256,1024]{1,0:T(8,128)(2,1)S(1)}, u32[]{:S(2)}, u32[]{:S(2)}) collective-permute-start(bf16[256,1024]{1,0:T(8,128)(2,1)S(1)} %pick.2), channel_id=1, source_target_pairs={{0,1},{1,0},{2,3},{3,2},{4,5},{5,4},{6,7},{7,6},{8,9},{9,8},{10,11... | collective-permute-start | bytes 1572872 | tf_op jit(solution)/shard_map/ppermute | solution.py:19
  16.3 4.3 %collective-permute-start.4 = (bf16[256,128]{1,0:T(8,128)(2,1)S(1)}, bf16[256,128]{1,0:T(8,128)(2,1)S(1)}, u32[]{:S(2)}, u32[]{:S(2)}) collective-permute-start(bf16[256,128]{1,0:T(8,128)(2,1)S(1)} %pad_maximum_fusion.4), channel_id=1, source_target_pairs={{0,4},{2,6},{4,0},{6,2},{8,12},{10,14},{12,8},{14,10},{16,20},{18,... | collective-permute-start | bytes 196616 | tf_op jit(solution)/shard_map/ppermute | solution.py:19
  16.8 10.8 %collective-permute-start.8 = (bf16[128,1152]{1,0:T(8,128)(2,1)S(1)}, bf16[128,1152]{1,0:T(8,128)(2,1)S(1)}, u32[]{:S(2)}, u32[]{:S(2)}) collective-permute-start(bf16[128,1152]{1,0:T(8,128)(2,1)S(1)} %pad_maximum_fusion.2), channel_id=1, source_target_pairs={{0,8},{2,10},{4,12},{6,14},{8,0},{10,2},{12,4},{14,6},{16,24},{18,... | collective-permute-start | bytes 884744 | tf_op jit(solution)/shard_map/ppermute | solution.py:19
  27.0 7.4 %collective-permute-start.10 = (bf16[640,512]{1,0:T(8,128)(2,1)S(1)}, bf16[640,512]{1,0:T(8,128)(2,1)S(1)}, u32[]{:S(2)}, u32[]{:S(2)}) collective-permute-start(bf16[640,512]{1,0:T(8,128)(2,1)S(1)} %dynamic-slice_bitcast_fusion), channel_id=1, source_target_pairs={{0,2},{1,3},{2,0},{3,1},{4,6},{5,7},{6,4},{7,5},{8,10},{9,11},{10,... | collective-permute-start | bytes 1966088 | tf_op jit(solution)/shard_map/ppermute | solution.py:19
  27.7 6.6 %collective-permute-start.9 = (bf16[256,128]{1,0:T(8,128)(2,1)S(1)}, bf16[256,128]{1,0:T(8,128)(2,1)S(1)}, u32[]{:S(2)}, u32[]{:S(2)}) collective-permute-start(bf16[256,128]{1,0:T(8,128)(2,1)S(1)} %slice.168), channel_id=1, source_target_pairs={{0,16},{2,18},{4,20},{6,22},{8,24},{10,26},{12,28},{14,30},{16,0},... | collective-permute-start | bytes 196616 | tf_op jit(solution)/shard_map/ppermute | solution.py:19
  28.2 6.4 %collective-permute-start.11 = (bf16[256,1152]{1,0:T(8,128)(2,1)S(1)}, bf16[256,1152]{1,0:T(8,128)(2,1)S(1)}, u32[]{:S(2)}, u32[]{:S(2)}) collective-permute-start(bf16[256,1152]{1,0:T(8,128)(2,1)S(1)} %pad_maximum_fusion.1), channel_id=1, source_target_pairs={{0,2},{2,0},{4,6},{6,4},{8,10},{10,8},{12,14},{14,12},{16,18},{18,... | collective-permute-start | bytes 1769480 | tf_op jit(solution)/shard_map/ppermute | solution.py:19
  34.8 4.3 %collective-permute-start.12 = (bf16[256,128]{1,0:T(8,128)(2,1)S(1)}, bf16[256,128]{1,0:T(8,128)(2,1)S(1)}, u32[]{:S(2)}, u32[]{:S(2)}) collective-permute-start(bf16[256,128]{1,0:T(8,128)(2,1)S(1)} %fusion.5), channel_id=1, source_target_pairs={{0,4},{2,6},{4,0},{6,2},{8,12},{10,14},{12,8},{14,10},{16,20},{18,... | collective-permute-start | bytes 196616 | tf_op jit(solution)/shard_map/ppermute | solution.py:19
  39.1 5.0 %collective-permute-start.13 = (bf16[256,128]{1,0:T(8,128)(2,1)S(1)}, bf16[256,128]{1,0:T(8,128)(2,1)S(1)}, u32[]{:S(2)}, u32[]{:S(2)}) collective-permute-start(bf16[256,128]{1,0:T(8,128)(2,1)S(1)} %fusion.1), channel_id=1, source_target_pairs={{0,8},{2,10},{4,12},{6,14},{8,0},{10,2},{12,4},{14,6},{16,24},{18,... | collective-permute-start | bytes 196616 | tf_op jit(solution)/shard_map/ppermute | solution.py:19
  39.4 6.7 %collective-permute-start.15 = (bf16[160,512]{1,0:T(8,128)(2,1)S(1)}, bf16[160,512]{1,0:T(8,128)(2,1)S(1)}, u32[]{:S(2)}, u32[]{:S(2)}) collective-permute-start(bf16[160,512]{1,0:T(8,128)(2,1)S(1)} %get-tuple-element.142), channel_id=1, source_target_pairs={{0,4},{1,5},{2,6},{3,7},{4,0},{5,1},{6,2},{7,3},{8,12},{9,13},{10,... | collective-permute-start | bytes 491528 | tf_op jit(solution)/shard_map/ppermute | solution.py:19
  39.9 6.2 %collective-permute-start.16 = (bf16[160,512]{1,0:T(8,128)(2,1)S(1)}, bf16[160,512]{1,0:T(8,128)(2,1)S(1)}, u32[]{:S(2)}, u32[]{:S(2)}) collective-permute-start(bf16[160,512]{1,0:T(8,128)(2,1)S(1)} %get-tuple-element.143), channel_id=1, source_target_pairs={{0,8},{1,9},{2,10},{3,11},{4,12},{5,13},{6,14},{7,15},{8,0},{9,1},... | collective-permute-start | bytes 491528 | tf_op jit(solution)/shard_map/ppermute | solution.py:19
  41.7 6.7 %collective-permute-start.17 = (bf16[160,512]{1,0:T(8,128)(2,1)S(1)}, bf16[160,512]{1,0:T(8,128)(2,1)S(1)}, u32[]{:S(2)}, u32[]{:S(2)}) collective-permute-start(bf16[160,512]{1,0:T(8,128)(2,1)S(1)} %get-tuple-element.144), channel_id=1, source_target_pairs={{0,12},{1,13},{2,14},{3,15},{4,8},{5,9},{6,10},{7,11},{8,4},{9,5},... | collective-permute-start | bytes 491528 | tf_op jit(solution)/shard_map/ppermute | solution.py:19
  49.1 5.9 %collective-permute-start.20 = (bf16[40,512]{1,0:T(8,128)(2,1)S(1)}, bf16[40,512]{1,0:T(8,128)(2,1)S(1)}, u32[]{:S(2)}, u32[]{:S(2)}) collective-permute-start(bf16[40,512]{1,0:T(8,128)(2,1)S(1)} %get-tuple-element.159), channel_id=1, source_target_pairs={{0,17},{1,16},{2,19},{3,18},{4,21},{5,20},{6,23},{7,22},{8,25},{9,... | collective-permute-start | bytes 122888 | tf_op jit(solution)/shard_map/ppermute | solution.py:19
  52.8 4.9 %collective-permute-start.19 = (bf16[40,512]{1,0:T(8,128)(2,1)S(1)}, bf16[40,512]{1,0:T(8,128)(2,1)S(1)}, u32[]{:S(2)}, u32[]{:S(2)}) collective-permute-start(bf16[40,512]{1,0:T(8,128)(2,1)S(1)} %get-tuple-element.160), channel_id=1, source_target_pairs={{0,16},{1,17},{2,18},{3,19},{4,20},{5,21},{6,22},{7,23},{8,24},{9,... | collective-permute-start | bytes 122888 | tf_op jit(solution)/shard_map/ppermute | solution.py:19
  52.8 4.9 %collective-permute-start.18 = (bf16[40,512]{1,0:T(8,128)(2,1)S(1)}, bf16[40,512]{1,0:T(8,128)(2,1)S(1)}, u32[]{:S(2)}, u32[]{:S(2)}) collective-permute-start(bf16[40,512]{1,0:T(8,128)(2,1)S(1)} %get-tuple-element.158), channel_id=1, source_target_pairs={{0,1},{1,0},{2,3},{3,2},{4,5},{5,4},{6,7},{7,6},{8,9},{9,8},{10,11... | collective-permute-start | bytes 122888 | tf_op jit(solution)/shard_map/ppermute | solution.py:19
  57.8 4.5 %collective-permute-start.21 = (bf16[40,512]{1,0:T(8,128)(2,1)S(1)}, bf16[40,512]{1,0:T(8,128)(2,1)S(1)}, u32[]{:S(2)}, u32[]{:S(2)}) collective-permute-start(bf16[40,512]{1,0:T(8,128)(2,1)S(1)} %get-tuple-element.153), channel_id=1, source_target_pairs={{0,1},{1,0},{2,3},{3,2},{4,5},{5,4},{6,7},{7,6},{8,9},{9,8},{10,11... | collective-permute-start | bytes 122888 | tf_op jit(solution)/shard_map/ppermute | solution.py:19
  58.7 5.1 %collective-permute-start.22 = (bf16[40,512]{1,0:T(8,128)(2,1)S(1)}, bf16[40,512]{1,0:T(8,128)(2,1)S(1)}, u32[]{:S(2)}, u32[]{:S(2)}) collective-permute-start(bf16[40,512]{1,0:T(8,128)(2,1)S(1)} %get-tuple-element.153), channel_id=1, source_target_pairs={{0,16},{1,17},{2,18},{3,19},{4,20},{5,21},{6,22},{7,23},{8,24},{9,... | collective-permute-start | bytes 122888 | tf_op jit(solution)/shard_map/ppermute | solution.py:19
  60.3 6.2 %collective-permute-start.23 = (bf16[40,512]{1,0:T(8,128)(2,1)S(1)}, bf16[40,512]{1,0:T(8,128)(2,1)S(1)}, u32[]{:S(2)}, u32[]{:S(2)}) collective-permute-start(bf16[40,512]{1,0:T(8,128)(2,1)S(1)} %get-tuple-element.153), channel_id=1, source_target_pairs={{0,17},{1,16},{2,19},{3,18},{4,21},{5,20},{6,23},{7,22},{8,25},{9,... | collective-permute-start | bytes 122888 | tf_op jit(solution)/shard_map/ppermute | solution.py:19
  66.5 5.3 %collective-permute-start.24 = (bf16[160,512]{1,0:T(8,128)(2,1)S(1)}, bf16[160,512]{1,0:T(8,128)(2,1)S(1)}, u32[]{:S(2)}, u32[]{:S(2)}) collective-permute-start(bf16[160,512]{1,0:T(8,128)(2,1)S(1)} %bitcast.114), channel_id=1, source_target_pairs={{0,4},{1,5},{2,6},{3,7},{4,0},{5,1},{6,2},{7,3},{8,12},{9,13},{10,... | collective-permute-start | bytes 491528 | tf_op jit(solution)/shard_map/ppermute | solution.py:19
  66.9 5.3 %collective-permute-start.25 = (bf16[160,512]{1,0:T(8,128)(2,1)S(1)}, bf16[160,512]{1,0:T(8,128)(2,1)S(1)}, u32[]{:S(2)}, u32[]{:S(2)}) collective-permute-start(bf16[160,512]{1,0:T(8,128)(2,1)S(1)} %bitcast.115), channel_id=1, source_target_pairs={{0,8},{1,9},{2,10},{3,11},{4,12},{5,13},{6,14},{7,15},{8,0},{9,1},... | collective-permute-start | bytes 491528 | tf_op jit(solution)/shard_map/ppermute | solution.py:19
  68.3 6.7 %collective-permute-start.26 = (bf16[160,512]{1,0:T(8,128)(2,1)S(1)}, bf16[160,512]{1,0:T(8,128)(2,1)S(1)}, u32[]{:S(2)}, u32[]{:S(2)}) collective-permute-start(bf16[160,512]{1,0:T(8,128)(2,1)S(1)} %bitcast.116), channel_id=1, source_target_pairs={{0,12},{1,13},{2,14},{3,15},{4,8},{5,9},{6,10},{7,11},{8,4},{9,5},... | collective-permute-start | bytes 491528 | tf_op jit(solution)/shard_map/ppermute | solution.py:19
  69.9 5.1 %collective-permute-start.27 = (bf16[160,512]{1,0:T(8,128)(2,1)S(1)}, bf16[160,512]{1,0:T(8,128)(2,1)S(1)}, u32[]{:S(2)}, u32[]{:S(2)}) collective-permute-start(bf16[160,512]{1,0:T(8,128)(2,1)S(1)} %bitcast.117), channel_id=1, source_target_pairs={{0,2},{1,3},{2,0},{3,1},{4,6},{5,7},{6,4},{7,5},{8,10},{9,11},{10,... | collective-permute-start | bytes 491528 | tf_op jit(solution)/shard_map/ppermute | solution.py:19
  (15 other events, 82.2 us)

commit v5 on v4

--- a/solution.py
+++ b/solution.py
@@ -137,7 +137,7 @@
     got = [x] + [swap(x, AXES, m, n) for m in found[1:]]
     for j, g in enumerate(got):
         out = put(out, g, w[tuple(group), j])
-    return out.reshape(len(found) * x.shape[0], x.shape[1])
+    return out
 
 
 def finish_sum(x, nb, nt, w):
@@ -146,24 +146,20 @@
     for group in far_groups(nb, nt):
         found = members(group)
         size = len(found)
-        if x.shape[0] % (8 * size):
+        if x.ndim == 2 or x.shape[0] != size:
             terms = [x.astype(f32)] + [swap(x, AXES, m, n).astype(f32) for m in found[1:]]
             while len(terms) > 1:
                 terms = [a + b for a, b in zip(terms[::2], terms[1::2])]
             x = terms[0].astype(bf16)
             continue
-        xs = x.reshape(size, x.shape[0] // size, x.shape[1])
-        got = [
-            swap(take(xs, w[tuple(group), j]), AXES, found[j], n)
-            for j in range(1, size)
-        ]
-        own = take(xs, w[tuple(group), 0]).astype(f32)
+        got = [swap(take(x, w[tuple(group), j]), AXES, found[j], n) for j in range(1, size)]
+        own = take(x, w[tuple(group), 0]).astype(f32)
         x = sum((g.astype(f32) for g in got), own).astype(bf16)
         done.append(group)
     for group in reversed(done):
         x = join(x, group, w, n)
     found = members([m * nt for m in near_masks(nb)])
-    own = [x] + [swap(x, AXES, m, n) for m in found[1:]]
+    own = [x] + [swap(x, AXES, m, n) for m in found[:0:-1]][::-1]
     return own, [swap(x, AXES, nt, n) for x in own]
 
 
@@ -247,25 +243,31 @@
         out[...] = value
 
 
-def score_kernel(
-    scale, count, order, me_ref, here_ref, owner, own, ids, u_ref, pool_ref, w_in, bias, w_out, *refs
-):
+def exponent_kernel(u_ref, pool_ref, exponent_ref):
+    scores = nt_dot(u_ref[...], pool_ref[...]) / logit_sharpness_divisor
+    exponent_ref[...] = jnp.exp(scores - shift_bound)
+
+
+def positives_kernel(here_ref, owner, own, ids, w_in, bias, w_out, *refs):
+    gots, (rows_ref, unit_ref, latent_ref, pre_ref) = refs[:-4], refs[-4:]
     held = jnp.where(owner[...] == here_ref[0], 1.0, 0.0)
     held = jnp.broadcast_to(held, (w_out.shape[1], held.shape[1])).T[:, :1] > 0.5
-    rows = refs[0][...]
-    for got in refs[1:count]:
+    rows = gots[0][...]
+    for got in gots[1:]:
         rows = rows + got[...]
     rows = jnp.where(held, own[...].astype(f32), rows.astype(f32)).astype(bf16)
-    rows_ref, latent_ref, pre_ref, kept_ref, sent_ref, loss_ref, grad_ref, grad_pos = refs[count:-1]
-    share_ref = refs[-1]
     rows_ref[...] = rows
     values = forward(rows, hot_columns(ids[...], w_out.shape[1]), w_in, bias, w_out)
-    v = values[0]
-    latent_ref[...], pre_ref[...] = values[1], values[4]
+    unit_ref[...], latent_ref[...], pre_ref[...] = values[0], values[1], values[4]
+
+
+def score_kernel(scale, order, me_ref, u_ref, v_ref, pool_ref, exponent_ref, *refs):
+    kept_ref, sent_ref, loss_ref, grad_ref, grad_pos, share_ref = refs
+    v = v_ref[...]
     u, pool = u_ref[...], pool_ref[...]
     uf, vf = u.astype(f32), v.astype(f32)
     pos_score = jnp.sum(uf * vf, axis=1, keepdims=True) / logit_sharpness_divisor
-    exponent = jnp.exp(nt_dot(u, pool) / logit_sharpness_divisor - shift_bound)
+    exponent = exponent_ref[...]
     pos_exp = jnp.exp(pos_score - shift_bound)
     normalizer = pos_exp + jnp.sum(exponent, axis=1, keepdims=True)
     weights = (exponent / normalizer).astype(bf16)
@@ -291,12 +293,12 @@
     return grad_latent, (nt_dot(grad_latent, w_out[...]) * slope).astype(bf16)
 
 
-def piece_sizes(channels, embed, pieces):
-    return channels // (2 * pieces), embed // pieces
+def piece_sizes(channels, embed, animals, pieces):
+    return channels // (2 * pieces), embed // (2 * pieces), -(-animals // 8) * 8
 
 
 def two_sets_kernel(
-    pieces, ids, a_rows, a_latent, a_hidden, a_slope, a_grad, b_rows, b_latent, b_pre, b_grad, w_out, total
+    pieces, animals, ids, a_rows, a_latent, a_hidden, a_slope, a_grad, b_rows, b_latent, b_pre, b_grad, w_out, total
 ):
     embed, channels = w_out.shape[1], a_rows.shape[1]
     one_hot = hot_columns(ids[...], embed)
@@ -307,46 +309,54 @@
     low = tn_dot(a_latent_grad, a_hidden[...]) + tn_dot(b_latent_grad, b_hidden)
     animal = jnp.dot(one_hot, a_pre_grad, preferred_element_type=f32)
     animal = animal + jnp.dot(one_hot, b_pre_grad, preferred_element_type=f32)
-    top, small = piece_sizes(channels, embed, pieces)
+    top, small, biases = piece_sizes(channels, embed, animals, pieces)
     for i in range(2 * pieces):
-        at, q = i * (top + small), i % pieces
-        below = low if i < pieces else animal
+        at = i * (top + small + biases)
         total[at : at + top, :] = big[i * top : (i + 1) * top].astype(bf16)
-        total[at + top : at + top + small, :] = below[q * small : (q + 1) * small].astype(bf16)
-
-
-def near_kernel(pieces, at_ref, wide, latent, hidden, slope, mine, other, w_out, *refs):
+        total[at + top : at + top + small, :] = low[i * small : (i + 1) * small].astype(bf16)
+        total[at + top + small : at + top + small + biases, :] = animal[:biases].astype(bf16)
+
+
+def near_kernel(pieces, animals, at_ref, wide, latent, hidden, slope, mine, other, w_out, *refs):
     terms, out, smalls = refs[:pieces], refs[pieces], refs[pieces + 1]
     embed = w_out.shape[1]
     channels = wide.shape[1] - embed
     grad_unit = jnp.concatenate([mine[...], other[...]], 0).astype(f32)
     one_hot = wide[:, channels:]
     grad_latent, grad_pre = pulled_back(latent[...], slope[...], grad_unit, w_out)
-    top, small = piece_sizes(channels, embed, pieces)
-    smalls[:embed, :] = tn_dot(grad_latent, hidden[...])
-    smalls[embed:, :] = tn_dot(one_hot, grad_pre)
+    top, small, biases = piece_sizes(channels, embed, animals, pieces)
+    smalls[...] = tn_dot(grad_latent, hidden[...])
     at = at_ref[0]
     big = tn_dot(wide[:, pl.ds(pl.multiple_of(at * top, top), top)], grad_pre)
     low = smalls[pl.ds(pl.multiple_of(at * small, small), small), :]
     got = terms[0][...].astype(f32)
     for term in terms[1:]:
         got = got + term[...].astype(f32)
-    out[:top, :] = (got[:top] + big).astype(bf16)
-    out[top:, :] = (got[top:] + low).astype(bf16)
+    got = got + jnp.concatenate([big, low, tn_dot(one_hot, grad_pre)[:biases]], 0)
+    blocks, _, width = out.shape
+    for i in range(blocks):
+        out[i] = got[:, i * width : (i + 1) * width].astype(bf16)
 
 
 def finish_kernel(pieces, core_ref, *refs):
     places, own, other = (refs[i * pieces : (i + 1) * pieces] for i in range(3))
-    grad_w_in, grad_w_out, grad_bias, lows = refs[3 * pieces :]
-    embed = grad_w_out.shape[1]
-    top, small = piece_sizes(grad_w_in.shape[0], embed, pieces)
+    grad_w_in, grad_w_out, grad_bias, lows, bias_rows = refs[3 * pieces :]
+    animals = grad_bias.shape[0]
+    top, small, biases = piece_sizes(grad_w_in.shape[0], grad_w_out.shape[1], animals, pieces)
+    blocks, _, width = own[0].shape
     for half, held in ((core_ref[0], own), (1 - core_ref[0], other)):
         for place_ref, piece in zip(places, held):
             at = half * pieces + place_ref[0]
-            grad_w_in[pl.ds(pl.multiple_of(at * top, top), top), :] = piece[:top, :]
-            lows[pl.ds(pl.multiple_of(at * small, small), small), :] = piece[top:, :].astype(f32)
-    grad_w_out[...] = lows[:embed, :].T
-    grad_bias[...] = lows[embed : embed + grad_bias.shape[0], :]
+            tops = pl.ds(pl.multiple_of(at * top, top), top)
+            rows = pl.ds(pl.multiple_of(at * small, small), small)
+            last = pl.ds(pl.multiple_of(at * biases, biases), biases)
+            for i in range(blocks):
+                columns = slice(i * width, (i + 1) * width)
+                grad_w_in[tops, columns] = piece[i, :top, :]
+                lows[rows, columns] = piece[i, top : top + small, :].astype(f32)
+                bias_rows[last, columns] = piece[i, top + small :, :].astype(f32)
+    grad_w_out[...] = lows[...].T
+    grad_bias[...] = bias_rows[:animals, :]
 
 
 def call(kernel, name, out, *args, scalars=0, limit=12, space=pltpu.VMEM, scratch=()):
@@ -458,32 +468,38 @@
     ]
 
     scale = float(refs * n) ** (-0.5) / logit_sharpness_divisor
+    exponent = call(
+        exponent_kernel,
+        "exponents",
+        [((refs, pool.shape[0]), f32)],
+        *(u, pool),
+        limit=max(12, 12 * refs * pool.shape[0] >> 20),
+    )[0]
+    pos_rows, v, pos_latent, pos_pre = call(
+        positives_kernel,
+        "positives",
+        [(ref_rows.shape, bf16), (u.shape, bf16), (u.shape, f32), ((refs, hidden_width), f32)],
+        *(here, owner, own, ref_ids, *weights, *got),
+        scalars=1,
+    )
     half = pool.shape[0] // 2
-    out = [(ref_rows.shape, bf16), (u.shape, f32), ((refs, hidden_width), f32)]
-    out += [((half, embed), f32), ((half, embed), bf16), ((1, refs), f32)]
+    out = [((half, embed), f32), ((half, embed), bf16), ((1, refs), f32)]
     out += [(u.shape, f32), (u.shape, f32)]
-    pos_rows, pos_latent, pos_pre, kept, sent, loss, grad_ref, grad_pos = call(
-        functools.partial(score_kernel, scale, len(got), kept_order(nb)),
+    kept, sent, loss, grad_ref, grad_pos = call(
+        functools.partial(score_kernel, scale, kept_order(nb)),
         "scores",
         out,
-        w["b", 0].reshape(1),
-        here,
-        owner,
-        own,
-        ref_ids,
-        u,
-        pool,
-        *weights,
-        *got,
-        scalars=2,
+        *(w["b", 0].reshape(1), u, v, pool, exponent),
+        scalars=1,
         limit=max(12, 20 * refs * pool.shape[0] >> 20),
         scratch=[pltpu.VMEM((pool.shape[0], embed), f32)],
     )
     pieces = 1 << len(near)
+    piece_rows = sum(piece_sizes(channels, embed, animals, pieces))
     total = call(
-        functools.partial(two_sets_kernel, pieces),
+        functools.partial(two_sets_kernel, pieces, animals),
         "backward",
-        [((channels + 2 * embed, hidden_width), bf16)],
+        [((2 * pieces * piece_rows, hidden_width), bf16)],
         ref_ids,
         *(ref_rows, ref_latent, ref_hidden, ref_slope, grad_ref),
         *(pos_rows, pos_latent, pos_pre, grad_pos),
@@ -504,13 +520,13 @@
     mine = mine.astype(bf16)
     other = swap(mine, "batch", 1, nb)
     total = call(
-        functools.partial(near_kernel, pieces),
+        functools.partial(near_kernel, pieces, animals),
         "backward_near",
-        [(terms[0].shape, bf16)],
+        [((hidden_width // 128, piece_rows, 128), bf16)],
         w["at"].reshape(1),
         *(wide, *near_values, mine, other, w_out, *terms),
         scalars=1,
-        scratch=[pltpu.VMEM((2 * embed, hidden_width), f32)],
+        scratch=[pltpu.VMEM((embed, hidden_width), f32)],
     )[0]
     own, other = finish_sum(total, nb, nt, w)
     places = [w[tuple(m * nt for m in near), j].reshape(1) for j in range(pieces)]
@@ -521,7 +537,10 @@
         w[(nt,), 0].reshape(1),
         *(*places, *own, *other),
         scalars=1 + pieces,
-        scratch=[pltpu.VMEM((2 * embed, hidden_width), f32)],
+        scratch=[
+            pltpu.VMEM((embed, hidden_width), f32),
+            pltpu.VMEM((2 * pieces * piece_sizes(channels, embed, animals, pieces)[2], hidden_width), f32),
+        ],
     )
     return (loss.reshape(refs), grad_w_in, grad_w_out, grad_bias)
 

time: 77.8 us -> 77.6 us (level)
  waiting for transfers between devices: 33.7 us -> 30.4 us
  starting transfers between devices: 30.6 us -> 33.4 us
    ppermute x31, waiting for transfers between devices: 33.7 us -> 30.4 us  [swap(): return lax.ppermute(x, axes, [(i, i ^ mask) for i in range(n)])]
    ppermute x31, starting transfers between devices: 30.6 us -> 33.4 us  [swap(): return lax.ppermute(x, axes, [(i, i ^ mask) for i in range(n)])]
    pallas_call x9 -> x11, Pallas kernels: 11.2 us -> 11.5 us  [call(): pl.pallas_call(kernel, name=name, out_shape=shapes, in_specs=[pl.BlockSpe...]
where the time goes in v5:
time: 77.6 us; the launch traced here: 77.4 us
  starting transfers between devices  33.4 us (43%)
  waiting for transfers between devices  30.4 us (39%)
  Pallas kernels  11.5 us (15%)
  between operations  1.07 us (1%)
    ppermute x31, starting transfers between devices, swap(): return lax.ppermute(x, axes, [(i, i ^ mask) for i in range(n)])  33.4 us
    ppermute x31, waiting for transfers between devices, swap(): return lax.ppermute(x, axes, [(i, i ^ mask) for i in range(n)])  30.4 us
    pallas_call x11, Pallas kernels, call(): pl.pallas_call(kernel, name=name, out_shape=shapes, in_specs=[pl.BlockSpe...  11.5 us
  transfers between devices with their start and end apart: 31, of which 17 were waited for; matrix products, arithmetic and copies ran while one was open for 1% of the time, Pallas kernels for 12%

profile of v5, /device:TPU:0, one launch (start us, length us, event | category | flops | bytes accessed | tf_op | source)
XLA Modules:
  0.0 77.4 jit_solution(641334361063977587)
XLA Ops:
  0.6 3.0 %collective-permute-start = (s32[1,256]{1,0:T(1,128)}, s32[1,256]{1,0:T(1,128)S(1)}, u32[]{:S(2)}, u32[]{:S(2)}) collective-permute-start(s32[1,256]{1,0:T(1,128)} %bitcast.115), channel_id=1, source_target_pairs={{0,1},{1,0},{2,3},{3,2},{4,5},{5,4},{6,7},{7,6},{8,9},{9,8},{10,11... | collective-permute-start | bytes 3080 | tf_op jit(solution)/shard_map/ppermute | solution.py:19
  3.6 2.0 %front.1 = (bf16[64,128]{1,0:T(8,128)(2,1)S(1)}, bf16[64,1152]{1,0:T(8,128)(2,1)S(1)}) custom-call(bf16[1024,512]{1,0:T(8,128)(2,1)} %w_in.5, f32[8,512]{1,0:T(8,128)} %bias.5, bf16[512,128]{1,0:T(8,128)(2,1)} %w_out.9, s32[1,64]{1,0:T(1,128)} %bitcast.118, bf16[64,1024]{1,0:T(8,128)(2,1)} %refs_4_), custom_call_target="tpu_custom_call" | custom-call | tf_op jit(solution)/shard_map/front/pallas_call | solution.py:366
  6.2 2.9 %collective-permute-start.1 = (bf16[64,128]{1,0:T(8,128)(2,1)S(1)}, bf16[64,128]{1,0:T(8,128)(2,1)S(1)}, u32[]{:S(2)}, u32[]{:S(2)}) collective-permute-start(bf16[64,128]{1,0:T(8,128)(2,1)S(1)} %get-tuple-element.88), channel_id=1, source_target_pairs={{0,16},{2,18},{4,20},{6,22},{8,24},{10,26},{12,28},{14,30},{16,0},... | collective-permute-start | bytes 49160 | tf_op jit(solution)/shard_map/ppermute | solution.py:19
  10.6 1.5 %collective-permute-start.4 = (bf16[64,1152]{1,0:T(8,128)(2,1)S(1)}, bf16[64,1152]{1,0:T(8,128)(2,1)S(1)}, u32[]{:S(2)}, u32[]{:S(2)}) collective-permute-start(bf16[64,1152]{1,0:T(8,128)(2,1)S(1)} %get-tuple-element.99), channel_id=1, source_target_pairs={{0,4},{2,6},{4,0},{6,2},{8,12},{10,14},{12,8},{14,10},{16,20},{18,... | collective-permute-start | bytes 442376 | tf_op jit(solution)/shard_map/ppermute | solution.py:19
  12.2 1.6 %collective-permute-start.3 = (bf16[128,128]{1,0:T(8,128)(2,1)S(1)}, bf16[128,128]{1,0:T(8,128)(2,1)S(1)}, u32[]{:S(2)}, u32[]{:S(2)}) collective-permute-start(bf16[128,128]{1,0:T(8,128)(2,1)S(1)} %pad_maximum_fusion.6), channel_id=1, source_target_pairs={{0,8},{2,10},{4,12},{6,14},{8,0},{10,2},{12,4},{14,6},{16,24},{18,... | collective-permute-start | bytes 98312 | tf_op jit(solution)/shard_map/ppermute | solution.py:19
  17.4 1.6 %collective-permute-start.8 = (bf16[128,1152]{1,0:T(8,128)(2,1)S(1)}, bf16[128,1152]{1,0:T(8,128)(2,1)S(1)}, u32[]{:S(2)}, u32[]{:S(2)}) collective-permute-start(bf16[128,1152]{1,0:T(8,128)(2,1)S(1)} %pad_maximum_fusion.2), channel_id=1, source_target_pairs={{0,8},{2,10},{4,12},{6,14},{8,0},{10,2},{12,4},{14,6},{16,24},{18,... | collective-permute-start | bytes 884744 | tf_op jit(solution)/shard_map/ppermute | solution.py:19
  19.0 1.6 %collective-permute-done.5 = bf16[256,128]{1,0:T(8,128)(2,1)S(1)} collective-permute-done((bf16[256,128]{1,0:T(8,128)(2,1)S(1)}, bf16[256,128]{1,0:T(8,128)(2,1)S(1)}, u32[]{:S(2)}, u32[]{:S(2)}) %collective-permute-start.5) | collective-permute-done | bytes 65568 | tf_op jit(solution)/shard_map/ppermute | solution.py:19
  26.9 1.5 %collective-permute-start.9 = (bf16[256,128]{1,0:T(8,128)(2,1)S(1)}, bf16[256,128]{1,0:T(8,128)(2,1)S(1)}, u32[]{:S(2)}, u32[]{:S(2)}) collective-permute-start(bf16[256,128]{1,0:T(8,128)(2,1)S(1)} %slice.168), channel_id=1, source_target_pairs={{0,16},{2,18},{4,20},{6,22},{8,24},{10,26},{12,28},{14,30},{16,0},... | collective-permute-start | bytes 196616 | tf_op jit(solution)/shard_map/ppermute | solution.py:19
  28.4 5.1 %collective-permute-done.9 = bf16[256,128]{1,0:T(8,128)(2,1)S(1)} collective-permute-done((bf16[256,128]{1,0:T(8,128)(2,1)S(1)}, bf16[256,128]{1,0:T(8,128)(2,1)S(1)}, u32[]{:S(2)}, u32[]{:S(2)}) %collective-permute-start.9) | collective-permute-done | bytes 65568 | tf_op jit(solution)/shard_map/ppermute | solution.py:19
  35.0 1.6 %near_forward.1 = (f32[512,128]{1,0:T(8,128)S(1)}, bf16[512,512]{1,0:T(8,128)(2,1)S(1)}, f32[512,512]{1,0:T(8,128)S(1)}) custom-call(bf16[512,1152]{1,0:T(8,128)(2,1)S(1)} %pad_maximum_fusion.wide, bf16[1024,512]{1,0:T(8,128)(2,1)S(1)} %copy-done, f32[8,512]{1,0:T(8,128)S(1)} %copy-done.4, bf16[512,128]{1,0:T(8,128)(2,1)S(1)} %copy-done.1), custom_call_target="tpu_custom_call" | custom-call | tf_op jit(solution)/shard_map/near_forward/pallas_call | solution.py:366
  36.6 1.6 %collective-permute-done.12 = bf16[256,128]{1,0:T(8,128)(2,1)S(1)} collective-permute-done((bf16[256,128]{1,0:T(8,128)(2,1)S(1)}, bf16[256,128]{1,0:T(8,128)(2,1)S(1)}, u32[]{:S(2)}, u32[]{:S(2)}) %collective-permute-start.12) | collective-permute-done | bytes 65568 | tf_op jit(solution)/shard_map/ppermute | solution.py:19
  39.6 1.9 %collective-permute-start.16 = (bf16[152,512]{1,0:T(8,128)(2,1)S(1)}, bf16[152,512]{1,0:T(8,128)(2,1)S(1)}, u32[]{:S(2)}, u32[]{:S(2)}) collective-permute-start(bf16[152,512]{1,0:T(8,128)(2,1)S(1)} %get-tuple-element.145), channel_id=1, source_target_pairs={{0,8},{1,9},{2,10},{3,11},{4,12},{5,13},{6,14},{7,15},{8,0},{9,1},... | collective-permute-start | bytes 466952 | tf_op jit(solution)/shard_map/ppermute | solution.py:19
  43.5 1.6 %collective-permute-done.15.refs_1_ = bf16[152,512]{1,0:T(8,128)(2,1)S(1)} collective-permute-done((bf16[152,512]{1,0:T(8,128)(2,1)S(1)}, bf16[152,512]{1,0:T(8,128)(2,1)S(1)}, u32[]{:S(2)}, u32[]{:S(2)}) %collective-permute-start.15) | collective-permute-done | bytes 155680 | tf_op jit(solution)/shard_map/ppermute | solution.py:19
  45.9 1.7 %collective-permute-done.17.refs_3_ = bf16[152,512]{1,0:T(8,128)(2,1)S(1)} collective-permute-done((bf16[152,512]{1,0:T(8,128)(2,1)S(1)}, bf16[152,512]{1,0:T(8,128)(2,1)S(1)}, u32[]{:S(2)}, u32[]{:S(2)}) %collective-permute-start.17) | collective-permute-done | bytes 155680 | tf_op jit(solution)/shard_map/ppermute | solution.py:19
  48.2 4.4 %collective-permute-start.20 = (bf16[152,128]{1,0:T(8,128)(2,1)S(1)}, bf16[152,128]{1,0:T(8,128)(2,1)S(1)}, u32[]{:S(2)}, u32[]{:S(2)}) collective-permute-start(bf16[152,128]{1,0:T(8,128)(2,1)S(1)} %get-tuple-element.161), channel_id=1, source_target_pairs={{0,17},{1,16},{2,19},{3,18},{4,21},{5,20},{6,23},{7,22},{8,25},{9,... | collective-permute-start | bytes 116744 | tf_op jit(solution)/shard_map/ppermute | solution.py:19
  53.3 1.8 %collective-permute-done.20 = bf16[152,128]{1,0:T(8,128)(2,1)S(1)} collective-permute-done((bf16[152,128]{1,0:T(8,128)(2,1)S(1)}, bf16[152,128]{1,0:T(8,128)(2,1)S(1)}, u32[]{:S(2)}, u32[]{:S(2)}) %collective-permute-start.20) | collective-permute-done | bytes 38944 | tf_op jit(solution)/shard_map/ppermute | solution.py:19
  55.1 2.4 %collective-permute-done.19 = bf16[152,128]{1,0:T(8,128)(2,1)S(1)} collective-permute-done((bf16[152,128]{1,0:T(8,128)(2,1)S(1)}, bf16[152,128]{1,0:T(8,128)(2,1)S(1)}, u32[]{:S(2)}, u32[]{:S(2)}) %collective-permute-start.19) | collective-permute-done | bytes 38944 | tf_op jit(solution)/shard_map/ppermute | solution.py:19
  58.5 1.6 %collective-permute-start.22 = (bf16[152,128]{1,0:T(8,128)(2,1)S(1)}, bf16[152,128]{1,0:T(8,128)(2,1)S(1)}, u32[]{:S(2)}, u32[]{:S(2)}) collective-permute-start(bf16[152,128]{1,0:T(8,128)(2,1)S(1)} %get-tuple-element.155), channel_id=1, source_target_pairs={{0,16},{1,17},{2,18},{3,19},{4,20},{5,21},{6,22},{7,23},{8,24},{9,... | collective-permute-start | bytes 116744 | tf_op jit(solution)/shard_map/ppermute | solution.py:19
  60.1 1.9 %collective-permute-start.23 = (bf16[152,128]{1,0:T(8,128)(2,1)S(1)}, bf16[152,128]{1,0:T(8,128)(2,1)S(1)}, u32[]{:S(2)}, u32[]{:S(2)}) collective-permute-start(bf16[152,128]{1,0:T(8,128)(2,1)S(1)} %get-tuple-element.155), channel_id=1, source_target_pairs={{0,17},{1,16},{2,19},{3,18},{4,21},{5,20},{6,23},{7,22},{8,25},{9,... | collective-permute-start | bytes 116744 | tf_op jit(solution)/shard_map/ppermute | solution.py:19
  62.1 1.6 %collective-permute-done.22 = bf16[152,128]{1,0:T(8,128)(2,1)S(1)} collective-permute-done((bf16[152,128]{1,0:T(8,128)(2,1)S(1)}, bf16[152,128]{1,0:T(8,128)(2,1)S(1)}, u32[]{:S(2)}, u32[]{:S(2)}) %collective-permute-start.22) | collective-permute-done | bytes 38944 | tf_op jit(solution)/shard_map/ppermute | solution.py:19
  63.7 2.7 %collective-permute-done.23 = bf16[152,128]{1,0:T(8,128)(2,1)S(1)} collective-permute-done((bf16[152,128]{1,0:T(8,128)(2,1)S(1)}, bf16[152,128]{1,0:T(8,128)(2,1)S(1)}, u32[]{:S(2)}, u32[]{:S(2)}) %collective-permute-start.23) | collective-permute-done | bytes 38944 | tf_op jit(solution)/shard_map/ppermute | solution.py:19
  68.1 1.8 %collective-permute-start.26 = (bf16[4,152,128]{2,1,0:T(8,128)(2,1)S(1)}, bf16[4,152,128]{2,1,0:T(8,128)(2,1)S(1)}, u32[]{:S(2)}, u32[]{:S(2)}) collective-permute-start(bf16[4,152,128]{2,1,0:T(8,128)(2,1)S(1)} %bitcast_dynamic-update-slice_fusion.refs_4_), channel_id=1, source_target_pairs={{0,12},{1,13},{2,14},{3,15},{4,8},{5,9},{6,10},{7,11},{8,4},{9,5},... | collective-permute-start | bytes 466952 | tf_op jit(solution)/shard_map/ppermute | solution.py:19
  69.9 1.7 %collective-permute-done.24.refs_5_ = bf16[4,152,128]{2,1,0:T(8,128)(2,1)S(1)} collective-permute-done((bf16[4,152,128]{2,1,0:T(8,128)(2,1)S(1)}, bf16[4,152,128]{2,1,0:T(8,128)(2,1)S(1)}, u32[]{:S(2)}, u32[]{:S(2)}) %collective-permute-start.24) | collective-permute-done | bytes 155680 | tf_op jit(solution)/shard_map/ppermute | solution.py:19
  72.2 2.6 %collective-permute-done.26.refs_7_ = bf16[4,152,128]{2,1,0:T(8,128)(2,1)S(1)} collective-permute-done((bf16[4,152,128]{2,1,0:T(8,128)(2,1)S(1)}, bf16[4,152,128]{2,1,0:T(8,128)(2,1)S(1)}, u32[]{:S(2)}, u32[]{:S(2)}) %collective-permute-start.26) | collective-permute-done | bytes 155680 | tf_op jit(solution)/shard_map/ppermute | solution.py:19
  (104 shorter events, 24.4 us)
Async XLA Ops:
  0.6 5.0 %collective-permute-start = (s32[1,256]{1,0:T(1,128)}, s32[1,256]{1,0:T(1,128)S(1)}, u32[]{:S(2)}, u32[]{:S(2)}) collective-permute-start(s32[1,256]{1,0:T(1,128)} %bitcast.115), channel_id=1, source_target_pairs={{0,1},{1,0},{2,3},{3,2},{4,5},{5,4},{6,7},{7,6},{8,9},{9,8},{10,11... | collective-permute-start | bytes 3080 | tf_op jit(solution)/shard_map/ppermute | solution.py:19
  6.2 6.0 %collective-permute-start.1 = (bf16[64,128]{1,0:T(8,128)(2,1)S(1)}, bf16[64,128]{1,0:T(8,128)(2,1)S(1)}, u32[]{:S(2)}, u32[]{:S(2)}) collective-permute-start(bf16[64,128]{1,0:T(8,128)(2,1)S(1)} %get-tuple-element.88), channel_id=1, source_target_pairs={{0,16},{2,18},{4,20},{6,22},{8,24},{10,26},{12,28},{14,30},{16,0},... | collective-permute-start | bytes 49160 | tf_op jit(solution)/shard_map/ppermute | solution.py:19
  9.1 13.3 %collective-permute-start.2 = (bf16[256,1024]{1,0:T(8,128)(2,1)S(1)}, bf16[256,1024]{1,0:T(8,128)(2,1)S(1)}, u32[]{:S(2)}, u32[]{:S(2)}) collective-permute-start(bf16[256,1024]{1,0:T(8,128)(2,1)S(1)} %pick.2), channel_id=1, source_target_pairs={{0,1},{1,0},{2,3},{3,2},{4,5},{5,4},{6,7},{7,6},{8,9},{9,8},{10,11... | collective-permute-start | bytes 1572872 | tf_op jit(solution)/shard_map/ppermute | solution.py:19
  10.6 5.6 %collective-permute-start.4 = (bf16[64,1152]{1,0:T(8,128)(2,1)S(1)}, bf16[64,1152]{1,0:T(8,128)(2,1)S(1)}, u32[]{:S(2)}, u32[]{:S(2)}) collective-permute-start(bf16[64,1152]{1,0:T(8,128)(2,1)S(1)} %get-tuple-element.99), channel_id=1, source_target_pairs={{0,4},{2,6},{4,0},{6,2},{8,12},{10,14},{12,8},{14,10},{16,20},{18,... | collective-permute-start | bytes 442376 | tf_op jit(solution)/shard_map/ppermute | solution.py:19
  16.3 4.3 %collective-permute-start.5 = (bf16[256,128]{1,0:T(8,128)(2,1)S(1)}, bf16[256,128]{1,0:T(8,128)(2,1)S(1)}, u32[]{:S(2)}, u32[]{:S(2)}) collective-permute-start(bf16[256,128]{1,0:T(8,128)(2,1)S(1)} %pad_maximum_fusion.4), channel_id=1, source_target_pairs={{0,4},{2,6},{4,0},{6,2},{8,12},{10,14},{12,8},{14,10},{16,20},{18,... | collective-permute-start | bytes 196616 | tf_op jit(solution)/shard_map/ppermute | solution.py:19
  17.4 9.4 %collective-permute-start.8 = (bf16[128,1152]{1,0:T(8,128)(2,1)S(1)}, bf16[128,1152]{1,0:T(8,128)(2,1)S(1)}, u32[]{:S(2)}, u32[]{:S(2)}) collective-permute-start(bf16[128,1152]{1,0:T(8,128)(2,1)S(1)} %pad_maximum_fusion.2), channel_id=1, source_target_pairs={{0,8},{2,10},{4,12},{6,14},{8,0},{10,2},{12,4},{14,6},{16,24},{18,... | collective-permute-start | bytes 884744 | tf_op jit(solution)/shard_map/ppermute | solution.py:19
  26.4 7.2 %collective-permute-start.10 = (bf16[608,512]{1,0:T(8,128)(2,1)S(1)}, bf16[608,512]{1,0:T(8,128)(2,1)S(1)}, u32[]{:S(2)}, u32[]{:S(2)}) collective-permute-start(bf16[608,512]{1,0:T(8,128)(2,1)S(1)} %dynamic-slice_bitcast_fusion), channel_id=1, source_target_pairs={{0,2},{1,3},{2,0},{3,1},{4,6},{5,7},{6,4},{7,5},{8,10},{9,11},{10,... | collective-permute-start | bytes 1867784 | tf_op jit(solution)/shard_map/ppermute | solution.py:19
  26.9 6.6 %collective-permute-start.9 = (bf16[256,128]{1,0:T(8,128)(2,1)S(1)}, bf16[256,128]{1,0:T(8,128)(2,1)S(1)}, u32[]{:S(2)}, u32[]{:S(2)}) collective-permute-start(bf16[256,128]{1,0:T(8,128)(2,1)S(1)} %slice.168), channel_id=1, source_target_pairs={{0,16},{2,18},{4,20},{6,22},{8,24},{10,26},{12,28},{14,30},{16,0},... | collective-permute-start | bytes 196616 | tf_op jit(solution)/shard_map/ppermute | solution.py:19
  28.4 5.4 %collective-permute-start.11 = (bf16[256,1152]{1,0:T(8,128)(2,1)S(1)}, bf16[256,1152]{1,0:T(8,128)(2,1)S(1)}, u32[]{:S(2)}, u32[]{:S(2)}) collective-permute-start(bf16[256,1152]{1,0:T(8,128)(2,1)S(1)} %pad_maximum_fusion.1), channel_id=1, source_target_pairs={{0,2},{2,0},{4,6},{6,4},{8,10},{10,8},{12,14},{14,12},{16,18},{18,... | collective-permute-start | bytes 1769480 | tf_op jit(solution)/shard_map/ppermute | solution.py:19
  33.9 4.3 %collective-permute-start.12 = (bf16[256,128]{1,0:T(8,128)(2,1)S(1)}, bf16[256,128]{1,0:T(8,128)(2,1)S(1)}, u32[]{:S(2)}, u32[]{:S(2)}) collective-permute-start(bf16[256,128]{1,0:T(8,128)(2,1)S(1)} %fusion.5), channel_id=1, source_target_pairs={{0,4},{2,6},{4,0},{6,2},{8,12},{10,14},{12,8},{14,10},{16,20},{18,... | collective-permute-start | bytes 196616 | tf_op jit(solution)/shard_map/ppermute | solution.py:19
  38.3 5.1 %collective-permute-start.13 = (bf16[256,128]{1,0:T(8,128)(2,1)S(1)}, bf16[256,128]{1,0:T(8,128)(2,1)S(1)}, u32[]{:S(2)}, u32[]{:S(2)}) collective-permute-start(bf16[256,128]{1,0:T(8,128)(2,1)S(1)} %fusion.1), channel_id=1, source_target_pairs={{0,8},{2,10},{4,12},{6,14},{8,0},{10,2},{12,4},{14,6},{16,24},{18,... | collective-permute-start | bytes 196616 | tf_op jit(solution)/shard_map/ppermute | solution.py:19
  38.5 6.6 %collective-permute-start.15 = (bf16[152,512]{1,0:T(8,128)(2,1)S(1)}, bf16[152,512]{1,0:T(8,128)(2,1)S(1)}, u32[]{:S(2)}, u32[]{:S(2)}) collective-permute-start(bf16[152,512]{1,0:T(8,128)(2,1)S(1)} %get-tuple-element.144), channel_id=1, source_target_pairs={{0,4},{1,5},{2,6},{3,7},{4,0},{5,1},{6,2},{7,3},{8,12},{9,13},{10,... | collective-permute-start | bytes 466952 | tf_op jit(solution)/shard_map/ppermute | solution.py:19
  39.6 6.3 %collective-permute-start.16 = (bf16[152,512]{1,0:T(8,128)(2,1)S(1)}, bf16[152,512]{1,0:T(8,128)(2,1)S(1)}, u32[]{:S(2)}, u32[]{:S(2)}) collective-permute-start(bf16[152,512]{1,0:T(8,128)(2,1)S(1)} %get-tuple-element.145), channel_id=1, source_target_pairs={{0,8},{1,9},{2,10},{3,11},{4,12},{5,13},{6,14},{7,15},{8,0},{9,1},... | collective-permute-start | bytes 466952 | tf_op jit(solution)/shard_map/ppermute | solution.py:19
  41.4 6.1 %collective-permute-start.17 = (bf16[152,512]{1,0:T(8,128)(2,1)S(1)}, bf16[152,512]{1,0:T(8,128)(2,1)S(1)}, u32[]{:S(2)}, u32[]{:S(2)}) collective-permute-start(bf16[152,512]{1,0:T(8,128)(2,1)S(1)} %get-tuple-element.146), channel_id=1, source_target_pairs={{0,12},{1,13},{2,14},{3,15},{4,8},{5,9},{6,10},{7,11},{8,4},{9,5},... | collective-permute-start | bytes 466952 | tf_op jit(solution)/shard_map/ppermute | solution.py:19
  48.2 6.9 %collective-permute-start.20 = (bf16[152,128]{1,0:T(8,128)(2,1)S(1)}, bf16[152,128]{1,0:T(8,128)(2,1)S(1)}, u32[]{:S(2)}, u32[]{:S(2)}) collective-permute-start(bf16[152,128]{1,0:T(8,128)(2,1)S(1)} %get-tuple-element.161), channel_id=1, source_target_pairs={{0,17},{1,16},{2,19},{3,18},{4,21},{5,20},{6,23},{7,22},{8,25},{9,... | collective-permute-start | bytes 116744 | tf_op jit(solution)/shard_map/ppermute | solution.py:19
  52.7 4.9 %collective-permute-start.19 = (bf16[152,128]{1,0:T(8,128)(2,1)S(1)}, bf16[152,128]{1,0:T(8,128)(2,1)S(1)}, u32[]{:S(2)}, u32[]{:S(2)}) collective-permute-start(bf16[152,128]{1,0:T(8,128)(2,1)S(1)} %get-tuple-element.162), channel_id=1, source_target_pairs={{0,16},{1,17},{2,18},{3,19},{4,20},{5,21},{6,22},{7,23},{8,24},{9,... | collective-permute-start | bytes 116744 | tf_op jit(solution)/shard_map/ppermute | solution.py:19
  52.7 4.9 %collective-permute-start.18 = (bf16[152,128]{1,0:T(8,128)(2,1)S(1)}, bf16[152,128]{1,0:T(8,128)(2,1)S(1)}, u32[]{:S(2)}, u32[]{:S(2)}) collective-permute-start(bf16[152,128]{1,0:T(8,128)(2,1)S(1)} %get-tuple-element.160), channel_id=1, source_target_pairs={{0,1},{1,0},{2,3},{3,2},{4,5},{5,4},{6,7},{7,6},{8,9},{9,8},{10,11... | collective-permute-start | bytes 116744 | tf_op jit(solution)/shard_map/ppermute | solution.py:19
  57.6 4.5 %collective-permute-start.21 = (bf16[152,128]{1,0:T(8,128)(2,1)S(1)}, bf16[152,128]{1,0:T(8,128)(2,1)S(1)}, u32[]{:S(2)}, u32[]{:S(2)}) collective-permute-start(bf16[152,128]{1,0:T(8,128)(2,1)S(1)} %get-tuple-element.155), channel_id=1, source_target_pairs={{0,1},{1,0},{2,3},{3,2},{4,5},{5,4},{6,7},{7,6},{8,9},{9,8},{10,11... | collective-permute-start | bytes 116744 | tf_op jit(solution)/shard_map/ppermute | solution.py:19
  58.5 5.2 %collective-permute-start.22 = (bf16[152,128]{1,0:T(8,128)(2,1)S(1)}, bf16[152,128]{1,0:T(8,128)(2,1)S(1)}, u32[]{:S(2)}, u32[]{:S(2)}) collective-permute-start(bf16[152,128]{1,0:T(8,128)(2,1)S(1)} %get-tuple-element.155), channel_id=1, source_target_pairs={{0,16},{1,17},{2,18},{3,19},{4,20},{5,21},{6,22},{7,23},{8,24},{9,... | collective-permute-start | bytes 116744 | tf_op jit(solution)/shard_map/ppermute | solution.py:19
  60.1 6.2 %collective-permute-start.23 = (bf16[152,128]{1,0:T(8,128)(2,1)S(1)}, bf16[152,128]{1,0:T(8,128)(2,1)S(1)}, u32[]{:S(2)}, u32[]{:S(2)}) collective-permute-start(bf16[152,128]{1,0:T(8,128)(2,1)S(1)} %get-tuple-element.155), channel_id=1, source_target_pairs={{0,17},{1,16},{2,19},{3,18},{4,21},{5,20},{6,23},{7,22},{8,25},{9,... | collective-permute-start | bytes 116744 | tf_op jit(solution)/shard_map/ppermute | solution.py:19
  66.4 5.3 %collective-permute-start.24 = (bf16[4,152,128]{2,1,0:T(8,128)(2,1)S(1)}, bf16[4,152,128]{2,1,0:T(8,128)(2,1)S(1)}, u32[]{:S(2)}, u32[]{:S(2)}) collective-permute-start(bf16[4,152,128]{2,1,0:T(8,128)(2,1)S(1)} %bitcast_dynamic-update-slice_fusion.refs_4_), channel_id=1, source_target_pairs={{0,4},{1,5},{2,6},{3,7},{4,0},{5,1},{6,2},{7,3},{8,12},{9,13},{10,... | collective-permute-start | bytes 466952 | tf_op jit(solution)/shard_map/ppermute | solution.py:19
  66.9 5.2 %collective-permute-start.25 = (bf16[4,152,128]{2,1,0:T(8,128)(2,1)S(1)}, bf16[4,152,128]{2,1,0:T(8,128)(2,1)S(1)}, u32[]{:S(2)}, u32[]{:S(2)}) collective-permute-start(bf16[4,152,128]{2,1,0:T(8,128)(2,1)S(1)} %bitcast_dynamic-update-slice_fusion.refs_4_), channel_id=1, source_target_pairs={{0,8},{1,9},{2,10},{3,11},{4,12},{5,13},{6,14},{7,15},{8,0},{9,1},... | collective-permute-start | bytes 466952 | tf_op jit(solution)/shard_map/ppermute | solution.py:19
  68.1 6.7 %collective-permute-start.26 = (bf16[4,152,128]{2,1,0:T(8,128)(2,1)S(1)}, bf16[4,152,128]{2,1,0:T(8,128)(2,1)S(1)}, u32[]{:S(2)}, u32[]{:S(2)}) collective-permute-start(bf16[4,152,128]{2,1,0:T(8,128)(2,1)S(1)} %bitcast_dynamic-update-slice_fusion.refs_4_), channel_id=1, source_target_pairs={{0,12},{1,13},{2,14},{3,15},{4,8},{5,9},{6,10},{7,11},{8,4},{9,5},... | collective-permute-start | bytes 466952 | tf_op jit(solution)/shard_map/ppermute | solution.py:19
  69.9 4.9 %collective-permute-start.27 = (bf16[4,152,128]{2,1,0:T(8,128)(2,1)S(1)}, bf16[4,152,128]{2,1,0:T(8,128)(2,1)S(1)}, u32[]{:S(2)}, u32[]{:S(2)}) collective-permute-start(bf16[4,152,128]{2,1,0:T(8,128)(2,1)S(1)} %bitcast_dynamic-update-slice_fusion.refs_4_), channel_id=1, source_target_pairs={{0,2},{1,3},{2,0},{3,1},{4,6},{5,7},{6,4},{7,5},{8,10},{9,11},{10,... | collective-permute-start | bytes 466952 | tf_op jit(solution)/shard_map/ppermute | solution.py:19
  (15 other events, 79.2 us)

commit v6 on v5

--- a/solution.py
+++ b/solution.py
@@ -25,7 +25,7 @@
 
 def gather_batch(x, nb, w, wide, later):
     masks = batch_masks(nb)
-    order = masks[2:][::-1] + masks[1:2] + masks[:1]
+    order = masks[-1:] + masks[1:-2][::-1] + masks[-2:-1] + masks[:1]
     rows = x.shape[0]
     parts = {0: x}
     for m in order:
@@ -33,7 +33,7 @@
         block = jnp.concatenate([parts[k] for k in keys], 0) if len(keys) > 1 else parts[keys[0]]
         if len(keys) == 2:
             block, later = lax.optimization_barrier((block, later))
-        if m == masks[1]:
+        if m == masks[-2]:
             block, wide = lax.optimization_barrier((block, wide))
         got = swap(block, "batch", m, nb)
         for i, k in enumerate(keys):
@@ -54,29 +54,23 @@
     return x
 
 
+def wide_masks(nb):
+    return batch_masks(nb)[:-3:-1]
+
+
 def kept_order(nb):
-    masks = batch_masks(nb)
-    high = [sum(m for i, m in enumerate(masks[3:]) if j >> i & 1) for j in range(nb >> 3)]
-    return [h ^ k for h in high for k in members(near_masks(nb))]
-
-
-def scatter_batch(kept, sent, nb, wide):
+    masks = batch_masks(nb)[1:-2]
+    high = [sum(m for i, m in enumerate(masks) if j >> i & 1) for j in range(1 << len(masks))]
+    return [h ^ k for h in high for k in members(wide_masks(nb))]
+
+
+def scatter_batch(kept, sent, nb):
     masks = batch_masks(nb)
     x = kept + swap(sent, "batch", masks[0], nb).astype(f32)
-    for m in masks[3:][::-1]:
+    for m in masks[1:-2][::-1]:
         half = x.shape[0] // 2
-        send, wide = lax.optimization_barrier((x[half:].astype(bf16), wide))
-        x = x[:half] + swap(send, "batch", m, nb).astype(f32)
-    return x, wide
-
-
-def near_sum(x, m, nb, other):
-    keep = members(near_masks(nb))
-    send, other = lax.optimization_barrier((x.astype(bf16), other))
-    got = swap(send, "batch", m, nb)
-    rows = x.shape[0] // len(keep)
-    at = [keep.index(k ^ m) * rows for k in keep]
-    return x + jnp.concatenate([got[i : i + rows] for i in at], 0).astype(f32), other
+        x = x[:half] + swap(x[half:].astype(bf16), "batch", m, nb).astype(f32)
+    return x
 
 
 def far_groups(nb, nt):
@@ -111,7 +105,6 @@
         p = place(me, group)
         for j in range(1 << len(group)):
             w[tuple(group), j] = p ^ j
-    w["at"] = w[(nt,), 0] * (1 << len(near)) + w[tuple(near), 0]
     return w
 
 
@@ -312,27 +305,32 @@
     top, small, biases = piece_sizes(channels, embed, animals, pieces)
     for i in range(2 * pieces):
         at = i * (top + small + biases)
-        total[at : at + top, :] = big[i * top : (i + 1) * top].astype(bf16)
-        total[at + top : at + top + small, :] = low[i * small : (i + 1) * small].astype(bf16)
-        total[at + top + small : at + top + small + biases, :] = animal[:biases].astype(bf16)
-
-
-def near_kernel(pieces, animals, at_ref, wide, latent, hidden, slope, mine, other, w_out, *refs):
-    terms, out, smalls = refs[:pieces], refs[pieces], refs[pieces + 1]
+        total[at : at + top, :] = big[i * top : (i + 1) * top]
+        total[at + top : at + top + small, :] = low[i * small : (i + 1) * small]
+        total[at + top + small : at + top + small + biases, :] = animal[:biases]
+
+
+def negatives_kernel(pieces, animals, wide, latent, hidden, slope, grad, w_out, before, total):
     embed = w_out.shape[1]
     channels = wide.shape[1] - embed
-    grad_unit = jnp.concatenate([mine[...], other[...]], 0).astype(f32)
-    one_hot = wide[:, channels:]
-    grad_latent, grad_pre = pulled_back(latent[...], slope[...], grad_unit, w_out)
+    grad_latent, grad_pre = pulled_back(latent[...], slope[...], grad[...], w_out)
+    big = tn_dot(wide[:, :channels], grad_pre)
+    low = tn_dot(grad_latent, hidden[...])
+    animal = tn_dot(wide[:, channels:], grad_pre)
     top, small, biases = piece_sizes(channels, embed, animals, pieces)
-    smalls[...] = tn_dot(grad_latent, hidden[...])
-    at = at_ref[0]
-    big = tn_dot(wide[:, pl.ds(pl.multiple_of(at * top, top), top)], grad_pre)
-    low = smalls[pl.ds(pl.multiple_of(at * small, small), small), :]
+    for i in range(2 * pieces):
+        at = i * (top + small + biases)
+        ends = (at, at + top, at + top + small, at + top + small + biases)
+        terms = (big[i * top : (i + 1) * top], low[i * small : (i + 1) * small], animal[:biases])
+        for start, end, term in zip(ends, ends[1:], terms):
+            total[start:end, :] = (before[start:end, :] + term).astype(bf16)
+
+
+def piece_kernel(*refs):
+    terms, out = refs[:-1], refs[-1]
     got = terms[0][...].astype(f32)
     for term in terms[1:]:
         got = got + term[...].astype(f32)
-    got = got + jnp.concatenate([big, low, tn_dot(one_hot, grad_pre)[:biases]], 0)
     blocks, _, width = out.shape
     for i in range(blocks):
         out[i] = got[:, i * width : (i + 1) * width].astype(bf16)
@@ -452,9 +450,10 @@
     neg_unit, found, wide = lax.optimization_barrier((neg_unit, found, wide))
     got = [swap(f, "tm", k, nt) for k, f in enumerate(found, 1)]
     near = near_masks(nb)
-    wide = spread(wide, near[:1], nb)
+    shared = wide_masks(nb)
+    wide = spread(wide, shared[:1], nb)
     pool, wide, (ref_rows, row) = gather_batch(neg_unit, nb, w, wide, (ref_rows, row))
-    wide = spread(wide, near[1:], nb)
+    wide = spread(wide, shared[1:], nb)
     u, ref_latent, ref_hidden, ref_slope = call(
         refs_kernel,
         "refs",
@@ -499,34 +498,31 @@
     total = call(
         functools.partial(two_sets_kernel, pieces, animals),
         "backward",
-        [((2 * pieces * piece_rows, hidden_width), bf16)],
+        [((2 * pieces * piece_rows, hidden_width), f32)],
         ref_ids,
         *(ref_rows, ref_latent, ref_hidden, ref_slope, grad_ref),
         *(pos_rows, pos_latent, pos_pre, grad_pos),
         w_out,
     )[0]
-    mine, wide = scatter_batch(kept, sent, nb, wide)
-    wide = spread(wide, [1], nb)
-    parts = split_pair(total, nb, nt, w)
-    mine, (parts, wide) = near_sum(mine, near[0], nb, (parts, wide))
     near_values = call(
         near_forward_kernel,
         "near_forward",
         sets(wide.shape[0], embed, hidden_width),
         *(wide, *weights),
     )
-    terms = split_near(parts, nb, nt)
-    mine, near_values = near_sum(mine, near[1], nb, near_values)
-    mine = mine.astype(bf16)
-    other = swap(mine, "batch", 1, nb)
+    mine = scatter_batch(kept, sent, nb)
     total = call(
-        functools.partial(near_kernel, pieces, animals),
-        "backward_near",
+        functools.partial(negatives_kernel, pieces, animals),
+        "negatives",
+        [(total.shape, bf16)],
+        *(wide, *near_values, mine, w_out, total),
+    )[0]
+    parts = split_pair(total, nb, nt, w)
+    total = call(
+        piece_kernel,
+        "piece",
         [((hidden_width // 128, piece_rows, 128), bf16)],
-        w["at"].reshape(1),
-        *(wide, *near_values, mine, other, w_out, *terms),
-        scalars=1,
-        scratch=[pltpu.VMEM((embed, hidden_width), f32)],
+        *split_near(parts, nb, nt),
     )[0]
     own, other = finish_sum(total, nb, nt, w)
     places = [w[tuple(m * nt for m in near), j].reshape(1) for j in range(pieces)]

time: 77.6 us -> 75.4 us (0.972)
  starting transfers between devices: 33.4 us -> 29.3 us
  waiting for transfers between devices: 30.4 us -> 32.9 us
    ppermute x31 -> x27, starting transfers between devices: 33.4 us -> 29.3 us  [swap(): return lax.ppermute(x, axes, [(i, i ^ mask) for i in range(n)])]
    ppermute x31 -> x27, waiting for transfers between devices: 30.4 us -> 32.9 us  [swap(): return lax.ppermute(x, axes, [(i, i ^ mask) for i in range(n)])]
    pallas_call x11 -> x12, Pallas kernels: 11.5 us -> 11.1 us  [call(): pl.pallas_call(kernel, name=name, out_shape=shapes, in_specs=[pl.BlockSpe...]
  transfers between devices with their start and end apart: 31 -> 27, of which waited for: 17 -> 18; matrix products, arithmetic and copies ran while one was open for 1% -> 1% of each run, Pallas kernels for 12% -> 11%
where the time goes in v6:
time: 75.4 us; the launch traced here: 75.3 us
  waiting for transfers between devices  32.9 us (44%)
  starting transfers between devices  29.3 us (39%)
  Pallas kernels  11.1 us (15%)
  between operations  1.03 us (1%)
    ppermute x27, waiting for transfers between devices, swap(): return lax.ppermute(x, axes, [(i, i ^ mask) for i in range(n)])  32.9 us
    ppermute x27, starting transfers between devices, swap(): return lax.ppermute(x, axes, [(i, i ^ mask) for i in range(n)])  29.3 us
    pallas_call x12, Pallas kernels, call(): pl.pallas_call(kernel, name=name, out_shape=shapes, in_specs=[pl.BlockSpe...  11.1 us
  transfers between devices with their start and end apart: 27, of which 18 were waited for; matrix products, arithmetic and copies ran while one was open for 1% of the time, Pallas kernels for 11%

profile of v6, /device:TPU:0, one launch (start us, length us, event | category | flops | bytes accessed | tf_op | source)
XLA Modules:
  0.0 75.3 jit_solution(1174212062234911142)
XLA Ops:
  0.6 3.0 %collective-permute-start = (s32[1,256]{1,0:T(1,128)}, s32[1,256]{1,0:T(1,128)S(1)}, u32[]{:S(2)}, u32[]{:S(2)}) collective-permute-start(s32[1,256]{1,0:T(1,128)} %bitcast.114), channel_id=1, source_target_pairs={{0,1},{1,0},{2,3},{3,2},{4,5},{5,4},{6,7},{7,6},{8,9},{9,8},{10,11... | collective-permute-start | bytes 3080 | tf_op jit(solution)/shard_map/ppermute | solution.py:19
  3.6 2.0 %front.1 = (bf16[64,128]{1,0:T(8,128)(2,1)S(1)}, bf16[64,1152]{1,0:T(8,128)(2,1)S(1)}) custom-call(bf16[1024,512]{1,0:T(8,128)(2,1)} %w_in.5, f32[8,512]{1,0:T(8,128)} %bias.5, bf16[512,128]{1,0:T(8,128)(2,1)} %w_out.9, s32[1,64]{1,0:T(1,128)} %bitcast.117, bf16[64,1024]{1,0:T(8,128)(2,1)} %refs_4_), custom_call_target="tpu_custom_call" | custom-call | tf_op jit(solution)/shard_map/front/pallas_call | solution.py:364
  6.2 2.9 %collective-permute-start.1 = (bf16[64,128]{1,0:T(8,128)(2,1)S(1)}, bf16[64,128]{1,0:T(8,128)(2,1)S(1)}, u32[]{:S(2)}, u32[]{:S(2)}) collective-permute-start(bf16[64,128]{1,0:T(8,128)(2,1)S(1)} %get-tuple-element.75), channel_id=1, source_target_pairs={{0,16},{2,18},{4,20},{6,22},{8,24},{10,26},{12,28},{14,30},{16,0},... | collective-permute-start | bytes 49160 | tf_op jit(solution)/shard_map/ppermute | solution.py:19
  9.2 1.7 %collective-permute-start.2 = (bf16[256,1024]{1,0:T(8,128)(2,1)S(1)}, bf16[256,1024]{1,0:T(8,128)(2,1)S(1)}, u32[]{:S(2)}, u32[]{:S(2)}) collective-permute-start(bf16[256,1024]{1,0:T(8,128)(2,1)S(1)} %pick.2), channel_id=1, source_target_pairs={{0,1},{1,0},{2,3},{3,2},{4,5},{5,4},{6,7},{7,6},{8,9},{9,8},{10,11... | collective-permute-start | bytes 1572872 | tf_op jit(solution)/shard_map/ppermute | solution.py:19
  11.0 1.7 %collective-permute-start.3 = (bf16[128,128]{1,0:T(8,128)(2,1)S(1)}, bf16[128,128]{1,0:T(8,128)(2,1)S(1)}, u32[]{:S(2)}, u32[]{:S(2)}) collective-permute-start(bf16[128,128]{1,0:T(8,128)(2,1)S(1)} %pad_maximum_fusion.3), channel_id=1, source_target_pairs={{0,4},{2,6},{4,0},{6,2},{8,12},{10,14},{12,8},{14,10},{16,20},{18,... | collective-permute-start | bytes 98312 | tf_op jit(solution)/shard_map/ppermute | solution.py:19
  15.0 3.1 %collective-permute-done.4 = bf16[64,1152]{1,0:T(8,128)(2,1)S(1)} collective-permute-done((bf16[64,1152]{1,0:T(8,128)(2,1)S(1)}, bf16[64,1152]{1,0:T(8,128)(2,1)S(1)}, u32[]{:S(2)}, u32[]{:S(2)}) %collective-permute-start.4) | collective-permute-done | bytes 147488 | tf_op jit(solution)/shard_map/ppermute | solution.py:19
  18.3 2.0 %collective-permute-start.7 = (bf16[128,1152]{1,0:T(8,128)(2,1)S(1)}, bf16[128,1152]{1,0:T(8,128)(2,1)S(1)}, u32[]{:S(2)}, u32[]{:S(2)}) collective-permute-start(bf16[128,1152]{1,0:T(8,128)(2,1)S(1)} %pad_maximum_fusion), channel_id=1, source_target_pairs={{0,8},{2,10},{4,12},{6,14},{8,0},{10,2},{12,4},{14,6},{16,24},{18,... | collective-permute-start | bytes 884744 | tf_op jit(solution)/shard_map/ppermute | solution.py:19
  20.3 3.0 %collective-permute-done.5 = bf16[256,128]{1,0:T(8,128)(2,1)S(1)} collective-permute-done((bf16[256,128]{1,0:T(8,128)(2,1)S(1)}, bf16[256,128]{1,0:T(8,128)(2,1)S(1)}, u32[]{:S(2)}, u32[]{:S(2)}) %collective-permute-start.5) | collective-permute-done | bytes 65568 | tf_op jit(solution)/shard_map/ppermute | solution.py:19
  28.7 1.6 %collective-permute-start.9 = (bf16[256,128]{1,0:T(8,128)(2,1)S(1)}, bf16[256,128]{1,0:T(8,128)(2,1)S(1)}, u32[]{:S(2)}, u32[]{:S(2)}) collective-permute-start(bf16[256,128]{1,0:T(8,128)(2,1)S(1)} %slice.128), channel_id=1, source_target_pairs={{0,4},{2,6},{4,0},{6,2},{8,12},{10,14},{12,8},{14,10},{16,20},{18,... | collective-permute-start | bytes 196616 | tf_op jit(solution)/shard_map/ppermute | solution.py:19
  34.0 2.0 %collective-permute-done.10 = bf16[608,512]{1,0:T(8,128)(2,1)S(1)} collective-permute-done((bf16[608,512]{1,0:T(8,128)(2,1)S(1)}, bf16[608,512]{1,0:T(8,128)(2,1)S(1)}, u32[]{:S(2)}, u32[]{:S(2)}) %collective-permute-start.10) | collective-permute-done | bytes 622624 | tf_op jit(solution)/shard_map/ppermute | solution.py:19
  37.9 2.0 %collective-permute-start.13 = (bf16[152,512]{1,0:T(8,128)(2,1)S(1)}, bf16[152,512]{1,0:T(8,128)(2,1)S(1)}, u32[]{:S(2)}, u32[]{:S(2)}) collective-permute-start(bf16[152,512]{1,0:T(8,128)(2,1)S(1)} %get-tuple-element.130), channel_id=1, source_target_pairs={{0,12},{1,13},{2,14},{3,15},{4,8},{5,9},{6,10},{7,11},{8,4},{9,5},... | collective-permute-start | bytes 466952 | tf_op jit(solution)/shard_map/ppermute | solution.py:19
  39.8 2.6 %collective-permute-done.11.refs_1_ = bf16[152,512]{1,0:T(8,128)(2,1)S(1)} collective-permute-done((bf16[152,512]{1,0:T(8,128)(2,1)S(1)}, bf16[152,512]{1,0:T(8,128)(2,1)S(1)}, u32[]{:S(2)}, u32[]{:S(2)}) %collective-permute-start.11) | collective-permute-done | bytes 155680 | tf_op jit(solution)/shard_map/ppermute | solution.py:19
  42.4 2.4 %collective-permute-done.12.refs_2_ = bf16[152,512]{1,0:T(8,128)(2,1)S(1)} collective-permute-done((bf16[152,512]{1,0:T(8,128)(2,1)S(1)}, bf16[152,512]{1,0:T(8,128)(2,1)S(1)}, u32[]{:S(2)}, u32[]{:S(2)}) %collective-permute-start.12) | collective-permute-done | bytes 155680 | tf_op jit(solution)/shard_map/ppermute | solution.py:19
  44.8 2.2 %collective-permute-done.13.refs_3_ = bf16[152,512]{1,0:T(8,128)(2,1)S(1)} collective-permute-done((bf16[152,512]{1,0:T(8,128)(2,1)S(1)}, bf16[152,512]{1,0:T(8,128)(2,1)S(1)}, u32[]{:S(2)}, u32[]{:S(2)}) %collective-permute-start.13) | collective-permute-done | bytes 155680 | tf_op jit(solution)/shard_map/ppermute | solution.py:19
  48.1 1.8 %collective-permute-start.15 = (bf16[152,128]{1,0:T(8,128)(2,1)S(1)}, bf16[152,128]{1,0:T(8,128)(2,1)S(1)}, u32[]{:S(2)}, u32[]{:S(2)}) collective-permute-start(bf16[152,128]{1,0:T(8,128)(2,1)S(1)} %get-tuple-element.136), channel_id=1, source_target_pairs={{0,16},{1,17},{2,18},{3,19},{4,20},{5,21},{6,22},{7,23},{8,24},{9,... | collective-permute-start | bytes 116744 | tf_op jit(solution)/shard_map/ppermute | solution.py:19
  49.9 1.6 %collective-permute-start.16 = (bf16[152,128]{1,0:T(8,128)(2,1)S(1)}, bf16[152,128]{1,0:T(8,128)(2,1)S(1)}, u32[]{:S(2)}, u32[]{:S(2)}) collective-permute-start(bf16[152,128]{1,0:T(8,128)(2,1)S(1)} %get-tuple-element.135), channel_id=1, source_target_pairs={{0,17},{1,16},{2,19},{3,18},{4,21},{5,20},{6,23},{7,22},{8,25},{9,... | collective-permute-start | bytes 116744 | tf_op jit(solution)/shard_map/ppermute | solution.py:19
  51.5 2.4 %collective-permute-done.15 = bf16[152,128]{1,0:T(8,128)(2,1)S(1)} collective-permute-done((bf16[152,128]{1,0:T(8,128)(2,1)S(1)}, bf16[152,128]{1,0:T(8,128)(2,1)S(1)}, u32[]{:S(2)}, u32[]{:S(2)}) %collective-permute-start.15) | collective-permute-done | bytes 38944 | tf_op jit(solution)/shard_map/ppermute | solution.py:19
  53.9 1.8 %collective-permute-done.16 = bf16[152,128]{1,0:T(8,128)(2,1)S(1)} collective-permute-done((bf16[152,128]{1,0:T(8,128)(2,1)S(1)}, bf16[152,128]{1,0:T(8,128)(2,1)S(1)}, u32[]{:S(2)}, u32[]{:S(2)}) %collective-permute-start.16) | collective-permute-done | bytes 38944 | tf_op jit(solution)/shard_map/ppermute | solution.py:19
  58.0 2.2 %collective-permute-start.19 = (bf16[152,128]{1,0:T(8,128)(2,1)S(1)}, bf16[152,128]{1,0:T(8,128)(2,1)S(1)}, u32[]{:S(2)}, u32[]{:S(2)}) collective-permute-start(bf16[152,128]{1,0:T(8,128)(2,1)S(1)} %get-tuple-element.129), channel_id=1, source_target_pairs={{0,17},{1,16},{2,19},{3,18},{4,21},{5,20},{6,23},{7,22},{8,25},{9,... | collective-permute-start | bytes 116744 | tf_op jit(solution)/shard_map/ppermute | solution.py:19
  61.4 2.8 %collective-permute-done.19 = bf16[152,128]{1,0:T(8,128)(2,1)S(1)} collective-permute-done((bf16[152,128]{1,0:T(8,128)(2,1)S(1)}, bf16[152,128]{1,0:T(8,128)(2,1)S(1)}, u32[]{:S(2)}, u32[]{:S(2)}) %collective-permute-start.19) | collective-permute-done | bytes 38944 | tf_op jit(solution)/shard_map/ppermute | solution.py:19
  64.2 1.6 %collective-permute-start.20 = (bf16[4,152,128]{2,1,0:T(8,128)(2,1)S(1)}, bf16[4,152,128]{2,1,0:T(8,128)(2,1)S(1)}, u32[]{:S(2)}, u32[]{:S(2)}) collective-permute-start(bf16[4,152,128]{2,1,0:T(8,128)(2,1)S(1)} %bitcast_dynamic-update-slice_fusion.refs_4_), channel_id=1, source_target_pairs={{0,4},{1,5},{2,6},{3,7},{4,0},{5,1},{6,2},{7,3},{8,12},{9,13},{10,... | collective-permute-start | bytes 466952 | tf_op jit(solution)/shard_map/ppermute | solution.py:19
  66.1 1.6 %collective-permute-start.22 = (bf16[4,152,128]{2,1,0:T(8,128)(2,1)S(1)}, bf16[4,152,128]{2,1,0:T(8,128)(2,1)S(1)}, u32[]{:S(2)}, u32[]{:S(2)}) collective-permute-start(bf16[4,152,128]{2,1,0:T(8,128)(2,1)S(1)} %bitcast_dynamic-update-slice_fusion.refs_4_), channel_id=1, source_target_pairs={{0,12},{1,13},{2,14},{3,15},{4,8},{5,9},{6,10},{7,11},{8,4},{9,5},... | collective-permute-start | bytes 466952 | tf_op jit(solution)/shard_map/ppermute | solution.py:19
  67.7 1.7 %collective-permute-done.20.refs_5_ = bf16[4,152,128]{2,1,0:T(8,128)(2,1)S(1)} collective-permute-done((bf16[4,152,128]{2,1,0:T(8,128)(2,1)S(1)}, bf16[4,152,128]{2,1,0:T(8,128)(2,1)S(1)}, u32[]{:S(2)}, u32[]{:S(2)}) %collective-permute-start.20) | collective-permute-done | bytes 155680 | tf_op jit(solution)/shard_map/ppermute | solution.py:19
  71.0 1.6 %collective-permute-done.22.refs_7_ = bf16[4,152,128]{2,1,0:T(8,128)(2,1)S(1)} collective-permute-done((bf16[4,152,128]{2,1,0:T(8,128)(2,1)S(1)}, bf16[4,152,128]{2,1,0:T(8,128)(2,1)S(1)}, u32[]{:S(2)}, u32[]{:S(2)}) %collective-permute-start.22) | collective-permute-done | bytes 155680 | tf_op jit(solution)/shard_map/ppermute | solution.py:19
  (93 shorter events, 23.1 us)
Async XLA Ops:
  0.6 5.0 %collective-permute-start = (s32[1,256]{1,0:T(1,128)}, s32[1,256]{1,0:T(1,128)S(1)}, u32[]{:S(2)}, u32[]{:S(2)}) collective-permute-start(s32[1,256]{1,0:T(1,128)} %bitcast.114), channel_id=1, source_target_pairs={{0,1},{1,0},{2,3},{3,2},{4,5},{5,4},{6,7},{7,6},{8,9},{9,8},{10,11... | collective-permute-start | bytes 3080 | tf_op jit(solution)/shard_map/ppermute | solution.py:19
  6.2 4.8 %collective-permute-start.1 = (bf16[64,128]{1,0:T(8,128)(2,1)S(1)}, bf16[64,128]{1,0:T(8,128)(2,1)S(1)}, u32[]{:S(2)}, u32[]{:S(2)}) collective-permute-start(bf16[64,128]{1,0:T(8,128)(2,1)S(1)} %get-tuple-element.75), channel_id=1, source_target_pairs={{0,16},{2,18},{4,20},{6,22},{8,24},{10,26},{12,28},{14,30},{16,0},... | collective-permute-start | bytes 49160 | tf_op jit(solution)/shard_map/ppermute | solution.py:19
  9.1 9.0 %collective-permute-start.4 = (bf16[64,1152]{1,0:T(8,128)(2,1)S(1)}, bf16[64,1152]{1,0:T(8,128)(2,1)S(1)}, u32[]{:S(2)}, u32[]{:S(2)}) collective-permute-start(bf16[64,1152]{1,0:T(8,128)(2,1)S(1)} %get-tuple-element.86), channel_id=1, source_target_pairs={{0,16},{2,18},{4,20},{6,22},{8,24},{10,26},{12,28},{14,30},{16,0},... | collective-permute-start | bytes 442376 | tf_op jit(solution)/shard_map/ppermute | solution.py:19
  9.2 15.9 %collective-permute-start.2 = (bf16[256,1024]{1,0:T(8,128)(2,1)S(1)}, bf16[256,1024]{1,0:T(8,128)(2,1)S(1)}, u32[]{:S(2)}, u32[]{:S(2)}) collective-permute-start(bf16[256,1024]{1,0:T(8,128)(2,1)S(1)} %pick.2), channel_id=1, source_target_pairs={{0,1},{1,0},{2,3},{3,2},{4,5},{5,4},{6,7},{7,6},{8,9},{9,8},{10,11... | collective-permute-start | bytes 1572872 | tf_op jit(solution)/shard_map/ppermute | solution.py:19
  11.0 4.0 %collective-permute-start.3 = (bf16[128,128]{1,0:T(8,128)(2,1)S(1)}, bf16[128,128]{1,0:T(8,128)(2,1)S(1)}, u32[]{:S(2)}, u32[]{:S(2)}) collective-permute-start(bf16[128,128]{1,0:T(8,128)(2,1)S(1)} %pad_maximum_fusion.3), channel_id=1, source_target_pairs={{0,4},{2,6},{4,0},{6,2},{8,12},{10,14},{12,8},{14,10},{16,20},{18,... | collective-permute-start | bytes 98312 | tf_op jit(solution)/shard_map/ppermute | solution.py:19
  18.2 5.1 %collective-permute-start.5 = (bf16[256,128]{1,0:T(8,128)(2,1)S(1)}, bf16[256,128]{1,0:T(8,128)(2,1)S(1)}, u32[]{:S(2)}, u32[]{:S(2)}) collective-permute-start(bf16[256,128]{1,0:T(8,128)(2,1)S(1)} %pad_maximum_fusion.2), channel_id=1, source_target_pairs={{0,8},{2,10},{4,12},{6,14},{8,0},{10,2},{12,4},{14,6},{16,24},{18,... | collective-permute-start | bytes 196616 | tf_op jit(solution)/shard_map/ppermute | solution.py:19
  18.3 12.1 %collective-permute-start.7 = (bf16[128,1152]{1,0:T(8,128)(2,1)S(1)}, bf16[128,1152]{1,0:T(8,128)(2,1)S(1)}, u32[]{:S(2)}, u32[]{:S(2)}) collective-permute-start(bf16[128,1152]{1,0:T(8,128)(2,1)S(1)} %pad_maximum_fusion), channel_id=1, source_target_pairs={{0,8},{2,10},{4,12},{6,14},{8,0},{10,2},{12,4},{14,6},{16,24},{18,... | collective-permute-start | bytes 884744 | tf_op jit(solution)/shard_map/ppermute | solution.py:19
  28.7 4.3 %collective-permute-start.9 = (bf16[256,128]{1,0:T(8,128)(2,1)S(1)}, bf16[256,128]{1,0:T(8,128)(2,1)S(1)}, u32[]{:S(2)}, u32[]{:S(2)}) collective-permute-start(bf16[256,128]{1,0:T(8,128)(2,1)S(1)} %slice.128), channel_id=1, source_target_pairs={{0,4},{2,6},{4,0},{6,2},{8,12},{10,14},{12,8},{14,10},{16,20},{18,... | collective-permute-start | bytes 196616 | tf_op jit(solution)/shard_map/ppermute | solution.py:19
  33.9 2.1 %collective-permute-start.10 = (bf16[608,512]{1,0:T(8,128)(2,1)S(1)}, bf16[608,512]{1,0:T(8,128)(2,1)S(1)}, u32[]{:S(2)}, u32[]{:S(2)}) collective-permute-start(bf16[608,512]{1,0:T(8,128)(2,1)S(1)} %dynamic-slice_bitcast_fusion), channel_id=1, source_target_pairs={{0,2},{1,3},{2,0},{3,1},{4,6},{5,7},{6,4},{7,5},{8,10},{9,11},{10,... | collective-permute-start | bytes 1867784 | tf_op jit(solution)/shard_map/ppermute | solution.py:19
  36.3 6.1 %collective-permute-start.11 = (bf16[152,512]{1,0:T(8,128)(2,1)S(1)}, bf16[152,512]{1,0:T(8,128)(2,1)S(1)}, u32[]{:S(2)}, u32[]{:S(2)}) collective-permute-start(bf16[152,512]{1,0:T(8,128)(2,1)S(1)} %get-tuple-element.132), channel_id=1, source_target_pairs={{0,4},{1,5},{2,6},{3,7},{4,0},{5,1},{6,2},{7,3},{8,12},{9,13},{10,... | collective-permute-start | bytes 466952 | tf_op jit(solution)/shard_map/ppermute | solution.py:19
  37.9 6.9 %collective-permute-start.12 = (bf16[152,512]{1,0:T(8,128)(2,1)S(1)}, bf16[152,512]{1,0:T(8,128)(2,1)S(1)}, u32[]{:S(2)}, u32[]{:S(2)}) collective-permute-start(bf16[152,512]{1,0:T(8,128)(2,1)S(1)} %get-tuple-element.131), channel_id=1, source_target_pairs={{0,8},{1,9},{2,10},{3,11},{4,12},{5,13},{6,14},{7,15},{8,0},{9,1},... | collective-permute-start | bytes 466952 | tf_op jit(solution)/shard_map/ppermute | solution.py:19
  37.9 9.1 %collective-permute-start.13 = (bf16[152,512]{1,0:T(8,128)(2,1)S(1)}, bf16[152,512]{1,0:T(8,128)(2,1)S(1)}, u32[]{:S(2)}, u32[]{:S(2)}) collective-permute-start(bf16[152,512]{1,0:T(8,128)(2,1)S(1)} %get-tuple-element.130), channel_id=1, source_target_pairs={{0,12},{1,13},{2,14},{3,15},{4,8},{5,9},{6,10},{7,11},{8,4},{9,5},... | collective-permute-start | bytes 466952 | tf_op jit(solution)/shard_map/ppermute | solution.py:19
  47.0 4.5 %collective-permute-start.14 = (bf16[152,128]{1,0:T(8,128)(2,1)S(1)}, bf16[152,128]{1,0:T(8,128)(2,1)S(1)}, u32[]{:S(2)}, u32[]{:S(2)}) collective-permute-start(bf16[152,128]{1,0:T(8,128)(2,1)S(1)} %get-tuple-element.134), channel_id=1, source_target_pairs={{0,1},{1,0},{2,3},{3,2},{4,5},{5,4},{6,7},{7,6},{8,9},{9,8},{10,11... | collective-permute-start | bytes 116744 | tf_op jit(solution)/shard_map/ppermute | solution.py:19
  48.1 5.8 %collective-permute-start.15 = (bf16[152,128]{1,0:T(8,128)(2,1)S(1)}, bf16[152,128]{1,0:T(8,128)(2,1)S(1)}, u32[]{:S(2)}, u32[]{:S(2)}) collective-permute-start(bf16[152,128]{1,0:T(8,128)(2,1)S(1)} %get-tuple-element.136), channel_id=1, source_target_pairs={{0,16},{1,17},{2,18},{3,19},{4,20},{5,21},{6,22},{7,23},{8,24},{9,... | collective-permute-start | bytes 116744 | tf_op jit(solution)/shard_map/ppermute | solution.py:19
  49.9 5.8 %collective-permute-start.16 = (bf16[152,128]{1,0:T(8,128)(2,1)S(1)}, bf16[152,128]{1,0:T(8,128)(2,1)S(1)}, u32[]{:S(2)}, u32[]{:S(2)}) collective-permute-start(bf16[152,128]{1,0:T(8,128)(2,1)S(1)} %get-tuple-element.135), channel_id=1, source_target_pairs={{0,17},{1,16},{2,19},{3,18},{4,21},{5,20},{6,23},{7,22},{8,25},{9,... | collective-permute-start | bytes 116744 | tf_op jit(solution)/shard_map/ppermute | solution.py:19
  55.7 4.5 %collective-permute-start.17 = (bf16[152,128]{1,0:T(8,128)(2,1)S(1)}, bf16[152,128]{1,0:T(8,128)(2,1)S(1)}, u32[]{:S(2)}, u32[]{:S(2)}) collective-permute-start(bf16[152,128]{1,0:T(8,128)(2,1)S(1)} %get-tuple-element.129), channel_id=1, source_target_pairs={{0,1},{1,0},{2,3},{3,2},{4,5},{5,4},{6,7},{7,6},{8,9},{9,8},{10,11... | collective-permute-start | bytes 116744 | tf_op jit(solution)/shard_map/ppermute | solution.py:19
  56.5 4.9 %collective-permute-start.18 = (bf16[152,128]{1,0:T(8,128)(2,1)S(1)}, bf16[152,128]{1,0:T(8,128)(2,1)S(1)}, u32[]{:S(2)}, u32[]{:S(2)}) collective-permute-start(bf16[152,128]{1,0:T(8,128)(2,1)S(1)} %get-tuple-element.129), channel_id=1, source_target_pairs={{0,16},{1,17},{2,18},{3,19},{4,20},{5,21},{6,22},{7,23},{8,24},{9,... | collective-permute-start | bytes 116744 | tf_op jit(solution)/shard_map/ppermute | solution.py:19
  58.0 6.2 %collective-permute-start.19 = (bf16[152,128]{1,0:T(8,128)(2,1)S(1)}, bf16[152,128]{1,0:T(8,128)(2,1)S(1)}, u32[]{:S(2)}, u32[]{:S(2)}) collective-permute-start(bf16[152,128]{1,0:T(8,128)(2,1)S(1)} %get-tuple-element.129), channel_id=1, source_target_pairs={{0,17},{1,16},{2,19},{3,18},{4,21},{5,20},{6,23},{7,22},{8,25},{9,... | collective-permute-start | bytes 116744 | tf_op jit(solution)/shard_map/ppermute | solution.py:19
  64.2 5.3 %collective-permute-start.20 = (bf16[4,152,128]{2,1,0:T(8,128)(2,1)S(1)}, bf16[4,152,128]{2,1,0:T(8,128)(2,1)S(1)}, u32[]{:S(2)}, u32[]{:S(2)}) collective-permute-start(bf16[4,152,128]{2,1,0:T(8,128)(2,1)S(1)} %bitcast_dynamic-update-slice_fusion.refs_4_), channel_id=1, source_target_pairs={{0,4},{1,5},{2,6},{3,7},{4,0},{5,1},{6,2},{7,3},{8,12},{9,13},{10,... | collective-permute-start | bytes 466952 | tf_op jit(solution)/shard_map/ppermute | solution.py:19
  65.8 5.2 %collective-permute-start.21 = (bf16[4,152,128]{2,1,0:T(8,128)(2,1)S(1)}, bf16[4,152,128]{2,1,0:T(8,128)(2,1)S(1)}, u32[]{:S(2)}, u32[]{:S(2)}) collective-permute-start(bf16[4,152,128]{2,1,0:T(8,128)(2,1)S(1)} %bitcast_dynamic-update-slice_fusion.refs_4_), channel_id=1, source_target_pairs={{0,8},{1,9},{2,10},{3,11},{4,12},{5,13},{6,14},{7,15},{8,0},{9,1},... | collective-permute-start | bytes 466952 | tf_op jit(solution)/shard_map/ppermute | solution.py:19
  66.1 6.5 %collective-permute-start.22 = (bf16[4,152,128]{2,1,0:T(8,128)(2,1)S(1)}, bf16[4,152,128]{2,1,0:T(8,128)(2,1)S(1)}, u32[]{:S(2)}, u32[]{:S(2)}) collective-permute-start(bf16[4,152,128]{2,1,0:T(8,128)(2,1)S(1)} %bitcast_dynamic-update-slice_fusion.refs_4_), channel_id=1, source_target_pairs={{0,12},{1,13},{2,14},{3,15},{4,8},{5,9},{6,10},{7,11},{8,4},{9,5},... | collective-permute-start | bytes 466952 | tf_op jit(solution)/shard_map/ppermute | solution.py:19
  67.7 4.9 %collective-permute-start.23 = (bf16[4,152,128]{2,1,0:T(8,128)(2,1)S(1)}, bf16[4,152,128]{2,1,0:T(8,128)(2,1)S(1)}, u32[]{:S(2)}, u32[]{:S(2)}) collective-permute-start(bf16[4,152,128]{2,1,0:T(8,128)(2,1)S(1)} %bitcast_dynamic-update-slice_fusion.refs_4_), channel_id=1, source_target_pairs={{0,2},{1,3},{2,0},{3,1},{4,6},{5,7},{6,4},{7,5},{8,10},{9,11},{10,... | collective-permute-start | bytes 466952 | tf_op jit(solution)/shard_map/ppermute | solution.py:19
  69.5 3.1 %collective-permute-start.24 = (bf16[4,152,128]{2,1,0:T(8,128)(2,1)S(1)}, bf16[4,152,128]{2,1,0:T(8,128)(2,1)S(1)}, u32[]{:S(2)}, u32[]{:S(2)}) collective-permute-start(bf16[4,152,128]{2,1,0:T(8,128)(2,1)S(1)} %collective-permute-done.20.refs_5_), channel_id=1, source_target_pairs={{0,2},{1,3},{2,0},{3,1},{4,6},{5,7},{6,4},{7,5},{8,10},{9,11},{10,... | collective-permute-start | bytes 466952 | tf_op jit(solution)/shard_map/ppermute | solution.py:19
  71.0 1.6 %collective-permute-start.25 = (bf16[4,152,128]{2,1,0:T(8,128)(2,1)S(1)}, bf16[4,152,128]{2,1,0:T(8,128)(2,1)S(1)}, u32[]{:S(2)}, u32[]{:S(2)}) collective-permute-start(bf16[4,152,128]{2,1,0:T(8,128)(2,1)S(1)} %collective-permute-done.21.refs_6_), channel_id=1, source_target_pairs={{0,2},{1,3},{2,0},{3,1},{4,6},{5,7},{6,4},{7,5},{8,10},{9,11},{10,... | collective-permute-start | bytes 466952 | tf_op jit(solution)/shard_map/ppermute | solution.py:19
  (11 other events, 61.4 us)

commit v7 on v6

--- a/solution.py
+++ b/solution.py
@@ -55,7 +55,7 @@
 
 
 def wide_masks(nb):
-    return batch_masks(nb)[:-3:-1]
+    return batch_masks(nb)[-2:]
 
 
 def kept_order(nb):
@@ -74,7 +74,7 @@
 
 
 def far_groups(nb, nt):
-    rest = [1 << i for i in range(nt.bit_length() - 1)] + [m * nt for m in batch_masks(nb)[3:]]
+    rest = [m * nt for m in batch_masks(nb)[3:]] + [1 << i for i in range(nt.bit_length() - 1)]
     return [rest[i : i + 2] for i in range(0, len(rest), 2)]
 
 

time: 75.4 us -> 74.7 us (level)
  waiting for transfers between devices: 32.9 us -> 30 us
  starting transfers between devices: 29.3 us -> 31.5 us
    ppermute x27, waiting for transfers between devices: 32.9 us -> 30 us  [swap(): return lax.ppermute(x, axes, [(i, i ^ mask) for i in range(n)])]
    ppermute x27, starting transfers between devices: 29.3 us -> 31.5 us  [swap(): return lax.ppermute(x, axes, [(i, i ^ mask) for i in range(n)])]
  transfers between devices with their start and end apart: 27 -> 27, of which waited for: 18 -> 20; matrix products, arithmetic and copies ran while one was open for 1% -> 1% of each run, Pallas kernels for 11% -> 11%
where the time goes in v7:
time: 74.7 us; the launch traced here: 74.5 us
  starting transfers between devices  31.5 us (42%)
  waiting for transfers between devices  30 us (40%)
  Pallas kernels  11.1 us (15%)
  between operations  1.03 us (1%)
    ppermute x27, starting transfers between devices, swap(): return lax.ppermute(x, axes, [(i, i ^ mask) for i in range(n)])  31.5 us
    ppermute x27, waiting for transfers between devices, swap(): return lax.ppermute(x, axes, [(i, i ^ mask) for i in range(n)])  30 us
    pallas_call x12, Pallas kernels, call(): pl.pallas_call(kernel, name=name, out_shape=shapes, in_specs=[pl.BlockSpe...  11.1 us
  transfers between devices with their start and end apart: 27, of which 20 were waited for; matrix products, arithmetic and copies ran while one was open for 1% of the time, Pallas kernels for 11%

profile of v7, /device:TPU:0, one launch (start us, length us, event | category | flops | bytes accessed | tf_op | source)
XLA Modules:
  0.0 74.5 jit_solution(14587777918594299294)
XLA Ops:
  0.6 3.0 %collective-permute-start = (s32[1,256]{1,0:T(1,128)}, s32[1,256]{1,0:T(1,128)S(1)}, u32[]{:S(2)}, u32[]{:S(2)}) collective-permute-start(s32[1,256]{1,0:T(1,128)} %bitcast.114), channel_id=1, source_target_pairs={{0,1},{1,0},{2,3},{3,2},{4,5},{5,4},{6,7},{7,6},{8,9},{9,8},{10,11... | collective-permute-start | bytes 3080 | tf_op jit(solution)/shard_map/ppermute | solution.py:19
  3.6 2.0 %front.1 = (bf16[64,128]{1,0:T(8,128)(2,1)S(1)}, bf16[64,1152]{1,0:T(8,128)(2,1)S(1)}) custom-call(bf16[1024,512]{1,0:T(8,128)(2,1)} %w_in.5, f32[8,512]{1,0:T(8,128)} %bias.5, bf16[512,128]{1,0:T(8,128)(2,1)} %w_out.9, s32[1,64]{1,0:T(1,128)} %bitcast.117, bf16[64,1024]{1,0:T(8,128)(2,1)} %refs_4_), custom_call_target="tpu_custom_call" | custom-call | tf_op jit(solution)/shard_map/front/pallas_call | solution.py:364
  6.2 2.9 %collective-permute-start.1 = (bf16[64,128]{1,0:T(8,128)(2,1)S(1)}, bf16[64,128]{1,0:T(8,128)(2,1)S(1)}, u32[]{:S(2)}, u32[]{:S(2)}) collective-permute-start(bf16[64,128]{1,0:T(8,128)(2,1)S(1)} %get-tuple-element.75), channel_id=1, source_target_pairs={{0,16},{2,18},{4,20},{6,22},{8,24},{10,26},{12,28},{14,30},{16,0},... | collective-permute-start | bytes 49160 | tf_op jit(solution)/shard_map/ppermute | solution.py:19
  9.1 1.6 %collective-permute-start.4 = (bf16[64,1152]{1,0:T(8,128)(2,1)S(1)}, bf16[64,1152]{1,0:T(8,128)(2,1)S(1)}, u32[]{:S(2)}, u32[]{:S(2)}) collective-permute-start(bf16[64,1152]{1,0:T(8,128)(2,1)S(1)} %get-tuple-element.86), channel_id=1, source_target_pairs={{0,8},{2,10},{4,12},{6,14},{8,0},{10,2},{12,4},{14,6},{16,24},{18,... | collective-permute-start | bytes 442376 | tf_op jit(solution)/shard_map/ppermute | solution.py:19
  12.3 1.6 %collective-permute-start.3 = (bf16[128,128]{1,0:T(8,128)(2,1)S(1)}, bf16[128,128]{1,0:T(8,128)(2,1)S(1)}, u32[]{:S(2)}, u32[]{:S(2)}) collective-permute-start(bf16[128,128]{1,0:T(8,128)(2,1)S(1)} %pad_maximum_fusion.3), channel_id=1, source_target_pairs={{0,4},{2,6},{4,0},{6,2},{8,12},{10,14},{12,8},{14,10},{16,20},{18,... | collective-permute-start | bytes 98312 | tf_op jit(solution)/shard_map/ppermute | solution.py:19
  16.9 2.7 %collective-permute-start.7 = (bf16[128,1152]{1,0:T(8,128)(2,1)S(1)}, bf16[128,1152]{1,0:T(8,128)(2,1)S(1)}, u32[]{:S(2)}, u32[]{:S(2)}) collective-permute-start(bf16[128,1152]{1,0:T(8,128)(2,1)S(1)} %pad_maximum_fusion), channel_id=1, source_target_pairs={{0,16},{2,18},{4,20},{6,22},{8,24},{10,26},{12,28},{14,30},{16,0},... | collective-permute-start | bytes 884744 | tf_op jit(solution)/shard_map/ppermute | solution.py:19
  26.9 1.6 %collective-permute-start.9 = (bf16[256,128]{1,0:T(8,128)(2,1)S(1)}, bf16[256,128]{1,0:T(8,128)(2,1)S(1)}, u32[]{:S(2)}, u32[]{:S(2)}) collective-permute-start(bf16[256,128]{1,0:T(8,128)(2,1)S(1)} %slice.128), channel_id=1, source_target_pairs={{0,4},{2,6},{4,0},{6,2},{8,12},{10,14},{12,8},{14,10},{16,20},{18,... | collective-permute-start | bytes 196616 | tf_op jit(solution)/shard_map/ppermute | solution.py:19
  28.5 1.6 %collective-permute-done.7 = bf16[128,1152]{1,0:T(8,128)(2,1)S(1)} collective-permute-done((bf16[128,1152]{1,0:T(8,128)(2,1)S(1)}, bf16[128,1152]{1,0:T(8,128)(2,1)S(1)}, u32[]{:S(2)}, u32[]{:S(2)}) %collective-permute-start.7) | collective-permute-done | bytes 294944 | tf_op jit(solution)/shard_map/ppermute | solution.py:19
  33.5 2.0 %collective-permute-done.10 = bf16[608,512]{1,0:T(8,128)(2,1)S(1)} collective-permute-done((bf16[608,512]{1,0:T(8,128)(2,1)S(1)}, bf16[608,512]{1,0:T(8,128)(2,1)S(1)}, u32[]{:S(2)}, u32[]{:S(2)}) %collective-permute-start.10) | collective-permute-done | bytes 622624 | tf_op jit(solution)/shard_map/ppermute | solution.py:19
  35.8 1.6 %collective-permute-start.11 = (bf16[152,512]{1,0:T(8,128)(2,1)S(1)}, bf16[152,512]{1,0:T(8,128)(2,1)S(1)}, u32[]{:S(2)}, u32[]{:S(2)}) collective-permute-start(bf16[152,512]{1,0:T(8,128)(2,1)S(1)} %get-tuple-element.132), channel_id=1, source_target_pairs={{0,4},{1,5},{2,6},{3,7},{4,0},{5,1},{6,2},{7,3},{8,12},{9,13},{10,... | collective-permute-start | bytes 466952 | tf_op jit(solution)/shard_map/ppermute | solution.py:19
  37.4 2.0 %collective-permute-start.13 = (bf16[152,512]{1,0:T(8,128)(2,1)S(1)}, bf16[152,512]{1,0:T(8,128)(2,1)S(1)}, u32[]{:S(2)}, u32[]{:S(2)}) collective-permute-start(bf16[152,512]{1,0:T(8,128)(2,1)S(1)} %get-tuple-element.130), channel_id=1, source_target_pairs={{0,12},{1,13},{2,14},{3,15},{4,8},{5,9},{6,10},{7,11},{8,4},{9,5},... | collective-permute-start | bytes 466952 | tf_op jit(solution)/shard_map/ppermute | solution.py:19
  39.3 2.6 %collective-permute-done.11.refs_1_ = bf16[152,512]{1,0:T(8,128)(2,1)S(1)} collective-permute-done((bf16[152,512]{1,0:T(8,128)(2,1)S(1)}, bf16[152,512]{1,0:T(8,128)(2,1)S(1)}, u32[]{:S(2)}, u32[]{:S(2)}) %collective-permute-start.11) | collective-permute-done | bytes 155680 | tf_op jit(solution)/shard_map/ppermute | solution.py:19
  41.9 2.4 %collective-permute-done.12.refs_2_ = bf16[152,512]{1,0:T(8,128)(2,1)S(1)} collective-permute-done((bf16[152,512]{1,0:T(8,128)(2,1)S(1)}, bf16[152,512]{1,0:T(8,128)(2,1)S(1)}, u32[]{:S(2)}, u32[]{:S(2)}) %collective-permute-start.12) | collective-permute-done | bytes 155680 | tf_op jit(solution)/shard_map/ppermute | solution.py:19
  44.3 2.2 %collective-permute-done.13.refs_3_ = bf16[152,512]{1,0:T(8,128)(2,1)S(1)} collective-permute-done((bf16[152,512]{1,0:T(8,128)(2,1)S(1)}, bf16[152,512]{1,0:T(8,128)(2,1)S(1)}, u32[]{:S(2)}, u32[]{:S(2)}) %collective-permute-start.13) | collective-permute-done | bytes 155680 | tf_op jit(solution)/shard_map/ppermute | solution.py:19
  48.8 2.3 %collective-permute-start.16 = (bf16[152,128]{1,0:T(8,128)(2,1)S(1)}, bf16[152,128]{1,0:T(8,128)(2,1)S(1)}, u32[]{:S(2)}, u32[]{:S(2)}) collective-permute-start(bf16[152,128]{1,0:T(8,128)(2,1)S(1)} %get-tuple-element.135), channel_id=1, source_target_pairs={{0,17},{1,16},{2,19},{3,18},{4,21},{5,20},{6,23},{7,22},{8,25},{9,... | collective-permute-start | bytes 116744 | tf_op jit(solution)/shard_map/ppermute | solution.py:19
  51.9 2.7 %collective-permute-done.16 = bf16[152,128]{1,0:T(8,128)(2,1)S(1)} collective-permute-done((bf16[152,128]{1,0:T(8,128)(2,1)S(1)}, bf16[152,128]{1,0:T(8,128)(2,1)S(1)}, u32[]{:S(2)}, u32[]{:S(2)}) %collective-permute-start.16) | collective-permute-done | bytes 38944 | tf_op jit(solution)/shard_map/ppermute | solution.py:19
  54.6 1.7 %collective-permute-start.17 = (bf16[152,128]{1,0:T(8,128)(2,1)S(1)}, bf16[152,128]{1,0:T(8,128)(2,1)S(1)}, u32[]{:S(2)}, u32[]{:S(2)}) collective-permute-start(bf16[152,128]{1,0:T(8,128)(2,1)S(1)} %get-tuple-element.129), channel_id=1, source_target_pairs={{0,16},{1,17},{2,18},{3,19},{4,20},{5,21},{6,22},{7,23},{8,24},{9,... | collective-permute-start | bytes 116744 | tf_op jit(solution)/shard_map/ppermute | solution.py:19
  57.5 1.6 %collective-permute-start.19 = (bf16[152,128]{1,0:T(8,128)(2,1)S(1)}, bf16[152,128]{1,0:T(8,128)(2,1)S(1)}, u32[]{:S(2)}, u32[]{:S(2)}) collective-permute-start(bf16[152,128]{1,0:T(8,128)(2,1)S(1)} %get-tuple-element.129), channel_id=1, source_target_pairs={{0,17},{1,16},{2,19},{3,18},{4,21},{5,20},{6,23},{7,22},{8,25},{9,... | collective-permute-start | bytes 116744 | tf_op jit(solution)/shard_map/ppermute | solution.py:19
  60.3 3.1 %collective-permute-done.19 = bf16[152,128]{1,0:T(8,128)(2,1)S(1)} collective-permute-done((bf16[152,128]{1,0:T(8,128)(2,1)S(1)}, bf16[152,128]{1,0:T(8,128)(2,1)S(1)}, u32[]{:S(2)}, u32[]{:S(2)}) %collective-permute-start.19) | collective-permute-done | bytes 38944 | tf_op jit(solution)/shard_map/ppermute | solution.py:19
  63.4 1.7 %collective-permute-start.20 = (bf16[4,152,128]{2,1,0:T(8,128)(2,1)S(1)}, bf16[4,152,128]{2,1,0:T(8,128)(2,1)S(1)}, u32[]{:S(2)}, u32[]{:S(2)}) collective-permute-start(bf16[4,152,128]{2,1,0:T(8,128)(2,1)S(1)} %bitcast_dynamic-update-slice_fusion.refs_4_), channel_id=1, source_target_pairs={{0,4},{1,5},{2,6},{3,7},{4,0},{5,1},{6,2},{7,3},{8,12},{9,13},{10,... | collective-permute-start | bytes 466952 | tf_op jit(solution)/shard_map/ppermute | solution.py:19
  65.2 1.8 %collective-permute-start.22 = (bf16[4,152,128]{2,1,0:T(8,128)(2,1)S(1)}, bf16[4,152,128]{2,1,0:T(8,128)(2,1)S(1)}, u32[]{:S(2)}, u32[]{:S(2)}) collective-permute-start(bf16[4,152,128]{2,1,0:T(8,128)(2,1)S(1)} %bitcast_dynamic-update-slice_fusion.refs_4_), channel_id=1, source_target_pairs={{0,12},{1,13},{2,14},{3,15},{4,8},{5,9},{6,10},{7,11},{8,4},{9,5},... | collective-permute-start | bytes 466952 | tf_op jit(solution)/shard_map/ppermute | solution.py:19
  67.0 1.7 %collective-permute-done.20.refs_5_ = bf16[4,152,128]{2,1,0:T(8,128)(2,1)S(1)} collective-permute-done((bf16[4,152,128]{2,1,0:T(8,128)(2,1)S(1)}, bf16[4,152,128]{2,1,0:T(8,128)(2,1)S(1)}, u32[]{:S(2)}, u32[]{:S(2)}) %collective-permute-start.20) | collective-permute-done | bytes 155680 | tf_op jit(solution)/shard_map/ppermute | solution.py:19
  68.7 1.6 %collective-permute-done.21.refs_6_ = bf16[4,152,128]{2,1,0:T(8,128)(2,1)S(1)} collective-permute-done((bf16[4,152,128]{2,1,0:T(8,128)(2,1)S(1)}, bf16[4,152,128]{2,1,0:T(8,128)(2,1)S(1)}, u32[]{:S(2)}, u32[]{:S(2)}) %collective-permute-start.21) | collective-permute-done | bytes 155680 | tf_op jit(solution)/shard_map/ppermute | solution.py:19
  70.3 1.5 %collective-permute-done.22.refs_7_ = bf16[4,152,128]{2,1,0:T(8,128)(2,1)S(1)} collective-permute-done((bf16[4,152,128]{2,1,0:T(8,128)(2,1)S(1)}, bf16[4,152,128]{2,1,0:T(8,128)(2,1)S(1)}, u32[]{:S(2)}, u32[]{:S(2)}) %collective-permute-start.22) | collective-permute-done | bytes 155680 | tf_op jit(solution)/shard_map/ppermute | solution.py:19
  (93 shorter events, 24.2 us)
Async XLA Ops:
  0.6 5.0 %collective-permute-start = (s32[1,256]{1,0:T(1,128)}, s32[1,256]{1,0:T(1,128)S(1)}, u32[]{:S(2)}, u32[]{:S(2)}) collective-permute-start(s32[1,256]{1,0:T(1,128)} %bitcast.114), channel_id=1, source_target_pairs={{0,1},{1,0},{2,3},{3,2},{4,5},{5,4},{6,7},{7,6},{8,9},{9,8},{10,11... | collective-permute-start | bytes 3080 | tf_op jit(solution)/shard_map/ppermute | solution.py:19
  6.2 6.0 %collective-permute-start.1 = (bf16[64,128]{1,0:T(8,128)(2,1)S(1)}, bf16[64,128]{1,0:T(8,128)(2,1)S(1)}, u32[]{:S(2)}, u32[]{:S(2)}) collective-permute-start(bf16[64,128]{1,0:T(8,128)(2,1)S(1)} %get-tuple-element.75), channel_id=1, source_target_pairs={{0,16},{2,18},{4,20},{6,22},{8,24},{10,26},{12,28},{14,30},{16,0},... | collective-permute-start | bytes 49160 | tf_op jit(solution)/shard_map/ppermute | solution.py:19
  9.1 7.2 %collective-permute-start.4 = (bf16[64,1152]{1,0:T(8,128)(2,1)S(1)}, bf16[64,1152]{1,0:T(8,128)(2,1)S(1)}, u32[]{:S(2)}, u32[]{:S(2)}) collective-permute-start(bf16[64,1152]{1,0:T(8,128)(2,1)S(1)} %get-tuple-element.86), channel_id=1, source_target_pairs={{0,8},{2,10},{4,12},{6,14},{8,0},{10,2},{12,4},{14,6},{16,24},{18,... | collective-permute-start | bytes 442376 | tf_op jit(solution)/shard_map/ppermute | solution.py:19
  10.7 12.6 %collective-permute-start.2 = (bf16[256,1024]{1,0:T(8,128)(2,1)S(1)}, bf16[256,1024]{1,0:T(8,128)(2,1)S(1)}, u32[]{:S(2)}, u32[]{:S(2)}) collective-permute-start(bf16[256,1024]{1,0:T(8,128)(2,1)S(1)} %pick.2), channel_id=1, source_target_pairs={{0,1},{1,0},{2,3},{3,2},{4,5},{5,4},{6,7},{7,6},{8,9},{9,8},{10,11... | collective-permute-start | bytes 1572872 | tf_op jit(solution)/shard_map/ppermute | solution.py:19
  12.3 4.0 %collective-permute-start.3 = (bf16[128,128]{1,0:T(8,128)(2,1)S(1)}, bf16[128,128]{1,0:T(8,128)(2,1)S(1)}, u32[]{:S(2)}, u32[]{:S(2)}) collective-permute-start(bf16[128,128]{1,0:T(8,128)(2,1)S(1)} %pad_maximum_fusion.3), channel_id=1, source_target_pairs={{0,4},{2,6},{4,0},{6,2},{8,12},{10,14},{12,8},{14,10},{16,20},{18,... | collective-permute-start | bytes 98312 | tf_op jit(solution)/shard_map/ppermute | solution.py:19
  16.3 4.3 %collective-permute-start.5 = (bf16[256,128]{1,0:T(8,128)(2,1)S(1)}, bf16[256,128]{1,0:T(8,128)(2,1)S(1)}, u32[]{:S(2)}, u32[]{:S(2)}) collective-permute-start(bf16[256,128]{1,0:T(8,128)(2,1)S(1)} %pad_maximum_fusion.2), channel_id=1, source_target_pairs={{0,8},{2,10},{4,12},{6,14},{8,0},{10,2},{12,4},{14,6},{16,24},{18,... | collective-permute-start | bytes 196616 | tf_op jit(solution)/shard_map/ppermute | solution.py:19
  16.9 13.2 %collective-permute-start.7 = (bf16[128,1152]{1,0:T(8,128)(2,1)S(1)}, bf16[128,1152]{1,0:T(8,128)(2,1)S(1)}, u32[]{:S(2)}, u32[]{:S(2)}) collective-permute-start(bf16[128,1152]{1,0:T(8,128)(2,1)S(1)} %pad_maximum_fusion), channel_id=1, source_target_pairs={{0,16},{2,18},{4,20},{6,22},{8,24},{10,26},{12,28},{14,30},{16,0},... | collective-permute-start | bytes 884744 | tf_op jit(solution)/shard_map/ppermute | solution.py:19
  26.9 5.7 %collective-permute-start.9 = (bf16[256,128]{1,0:T(8,128)(2,1)S(1)}, bf16[256,128]{1,0:T(8,128)(2,1)S(1)}, u32[]{:S(2)}, u32[]{:S(2)}) collective-permute-start(bf16[256,128]{1,0:T(8,128)(2,1)S(1)} %slice.128), channel_id=1, source_target_pairs={{0,4},{2,6},{4,0},{6,2},{8,12},{10,14},{12,8},{14,10},{16,20},{18,... | collective-permute-start | bytes 196616 | tf_op jit(solution)/shard_map/ppermute | solution.py:19
  33.4 2.1 %collective-permute-start.10 = (bf16[608,512]{1,0:T(8,128)(2,1)S(1)}, bf16[608,512]{1,0:T(8,128)(2,1)S(1)}, u32[]{:S(2)}, u32[]{:S(2)}) collective-permute-start(bf16[608,512]{1,0:T(8,128)(2,1)S(1)} %dynamic-slice_bitcast_fusion), channel_id=1, source_target_pairs={{0,2},{1,3},{2,0},{3,1},{4,6},{5,7},{6,4},{7,5},{8,10},{9,11},{10,... | collective-permute-start | bytes 1867784 | tf_op jit(solution)/shard_map/ppermute | solution.py:19
  35.8 6.1 %collective-permute-start.11 = (bf16[152,512]{1,0:T(8,128)(2,1)S(1)}, bf16[152,512]{1,0:T(8,128)(2,1)S(1)}, u32[]{:S(2)}, u32[]{:S(2)}) collective-permute-start(bf16[152,512]{1,0:T(8,128)(2,1)S(1)} %get-tuple-element.132), channel_id=1, source_target_pairs={{0,4},{1,5},{2,6},{3,7},{4,0},{5,1},{6,2},{7,3},{8,12},{9,13},{10,... | collective-permute-start | bytes 466952 | tf_op jit(solution)/shard_map/ppermute | solution.py:19
  37.4 6.9 %collective-permute-start.12 = (bf16[152,512]{1,0:T(8,128)(2,1)S(1)}, bf16[152,512]{1,0:T(8,128)(2,1)S(1)}, u32[]{:S(2)}, u32[]{:S(2)}) collective-permute-start(bf16[152,512]{1,0:T(8,128)(2,1)S(1)} %get-tuple-element.131), channel_id=1, source_target_pairs={{0,8},{1,9},{2,10},{3,11},{4,12},{5,13},{6,14},{7,15},{8,0},{9,1},... | collective-permute-start | bytes 466952 | tf_op jit(solution)/shard_map/ppermute | solution.py:19
  37.4 9.1 %collective-permute-start.13 = (bf16[152,512]{1,0:T(8,128)(2,1)S(1)}, bf16[152,512]{1,0:T(8,128)(2,1)S(1)}, u32[]{:S(2)}, u32[]{:S(2)}) collective-permute-start(bf16[152,512]{1,0:T(8,128)(2,1)S(1)} %get-tuple-element.130), channel_id=1, source_target_pairs={{0,12},{1,13},{2,14},{3,15},{4,8},{5,9},{6,10},{7,11},{8,4},{9,5},... | collective-permute-start | bytes 466952 | tf_op jit(solution)/shard_map/ppermute | solution.py:19
  46.6 5.2 %collective-permute-start.14 = (bf16[152,128]{1,0:T(8,128)(2,1)S(1)}, bf16[152,128]{1,0:T(8,128)(2,1)S(1)}, u32[]{:S(2)}, u32[]{:S(2)}) collective-permute-start(bf16[152,128]{1,0:T(8,128)(2,1)S(1)} %get-tuple-element.134), channel_id=1, source_target_pairs={{0,16},{1,17},{2,18},{3,19},{4,20},{5,21},{6,22},{7,23},{8,24},{9,... | collective-permute-start | bytes 116744 | tf_op jit(solution)/shard_map/ppermute | solution.py:19
  47.9 4.0 %collective-permute-start.15 = (bf16[152,128]{1,0:T(8,128)(2,1)S(1)}, bf16[152,128]{1,0:T(8,128)(2,1)S(1)}, u32[]{:S(2)}, u32[]{:S(2)}) collective-permute-start(bf16[152,128]{1,0:T(8,128)(2,1)S(1)} %get-tuple-element.136), channel_id=1, source_target_pairs={{0,1},{1,0},{2,3},{3,2},{4,5},{5,4},{6,7},{7,6},{8,9},{9,8},{10,11... | collective-permute-start | bytes 116744 | tf_op jit(solution)/shard_map/ppermute | solution.py:19
  48.8 5.8 %collective-permute-start.16 = (bf16[152,128]{1,0:T(8,128)(2,1)S(1)}, bf16[152,128]{1,0:T(8,128)(2,1)S(1)}, u32[]{:S(2)}, u32[]{:S(2)}) collective-permute-start(bf16[152,128]{1,0:T(8,128)(2,1)S(1)} %get-tuple-element.135), channel_id=1, source_target_pairs={{0,17},{1,16},{2,19},{3,18},{4,21},{5,20},{6,23},{7,22},{8,25},{9,... | collective-permute-start | bytes 116744 | tf_op jit(solution)/shard_map/ppermute | solution.py:19
  54.6 5.2 %collective-permute-start.17 = (bf16[152,128]{1,0:T(8,128)(2,1)S(1)}, bf16[152,128]{1,0:T(8,128)(2,1)S(1)}, u32[]{:S(2)}, u32[]{:S(2)}) collective-permute-start(bf16[152,128]{1,0:T(8,128)(2,1)S(1)} %get-tuple-element.129), channel_id=1, source_target_pairs={{0,16},{1,17},{2,18},{3,19},{4,20},{5,21},{6,22},{7,23},{8,24},{9,... | collective-permute-start | bytes 116744 | tf_op jit(solution)/shard_map/ppermute | solution.py:19
  56.3 4.0 %collective-permute-start.18 = (bf16[152,128]{1,0:T(8,128)(2,1)S(1)}, bf16[152,128]{1,0:T(8,128)(2,1)S(1)}, u32[]{:S(2)}, u32[]{:S(2)}) collective-permute-start(bf16[152,128]{1,0:T(8,128)(2,1)S(1)} %get-tuple-element.129), channel_id=1, source_target_pairs={{0,1},{1,0},{2,3},{3,2},{4,5},{5,4},{6,7},{7,6},{8,9},{9,8},{10,11... | collective-permute-start | bytes 116744 | tf_op jit(solution)/shard_map/ppermute | solution.py:19
  57.5 5.9 %collective-permute-start.19 = (bf16[152,128]{1,0:T(8,128)(2,1)S(1)}, bf16[152,128]{1,0:T(8,128)(2,1)S(1)}, u32[]{:S(2)}, u32[]{:S(2)}) collective-permute-start(bf16[152,128]{1,0:T(8,128)(2,1)S(1)} %get-tuple-element.129), channel_id=1, source_target_pairs={{0,17},{1,16},{2,19},{3,18},{4,21},{5,20},{6,23},{7,22},{8,25},{9,... | collective-permute-start | bytes 116744 | tf_op jit(solution)/shard_map/ppermute | solution.py:19
  63.4 5.3 %collective-permute-start.20 = (bf16[4,152,128]{2,1,0:T(8,128)(2,1)S(1)}, bf16[4,152,128]{2,1,0:T(8,128)(2,1)S(1)}, u32[]{:S(2)}, u32[]{:S(2)}) collective-permute-start(bf16[4,152,128]{2,1,0:T(8,128)(2,1)S(1)} %bitcast_dynamic-update-slice_fusion.refs_4_), channel_id=1, source_target_pairs={{0,4},{1,5},{2,6},{3,7},{4,0},{5,1},{6,2},{7,3},{8,12},{9,13},{10,... | collective-permute-start | bytes 466952 | tf_op jit(solution)/shard_map/ppermute | solution.py:19
  65.1 5.2 %collective-permute-start.21 = (bf16[4,152,128]{2,1,0:T(8,128)(2,1)S(1)}, bf16[4,152,128]{2,1,0:T(8,128)(2,1)S(1)}, u32[]{:S(2)}, u32[]{:S(2)}) collective-permute-start(bf16[4,152,128]{2,1,0:T(8,128)(2,1)S(1)} %bitcast_dynamic-update-slice_fusion.refs_4_), channel_id=1, source_target_pairs={{0,8},{1,9},{2,10},{3,11},{4,12},{5,13},{6,14},{7,15},{8,0},{9,1},... | collective-permute-start | bytes 466952 | tf_op jit(solution)/shard_map/ppermute | solution.py:19
  65.2 6.7 %collective-permute-start.22 = (bf16[4,152,128]{2,1,0:T(8,128)(2,1)S(1)}, bf16[4,152,128]{2,1,0:T(8,128)(2,1)S(1)}, u32[]{:S(2)}, u32[]{:S(2)}) collective-permute-start(bf16[4,152,128]{2,1,0:T(8,128)(2,1)S(1)} %bitcast_dynamic-update-slice_fusion.refs_4_), channel_id=1, source_target_pairs={{0,12},{1,13},{2,14},{3,15},{4,8},{5,9},{6,10},{7,11},{8,4},{9,5},... | collective-permute-start | bytes 466952 | tf_op jit(solution)/shard_map/ppermute | solution.py:19
  67.0 4.9 %collective-permute-start.23 = (bf16[4,152,128]{2,1,0:T(8,128)(2,1)S(1)}, bf16[4,152,128]{2,1,0:T(8,128)(2,1)S(1)}, u32[]{:S(2)}, u32[]{:S(2)}) collective-permute-start(bf16[4,152,128]{2,1,0:T(8,128)(2,1)S(1)} %bitcast_dynamic-update-slice_fusion.refs_4_), channel_id=1, source_target_pairs={{0,2},{1,3},{2,0},{3,1},{4,6},{5,7},{6,4},{7,5},{8,10},{9,11},{10,... | collective-permute-start | bytes 466952 | tf_op jit(solution)/shard_map/ppermute | solution.py:19
  68.7 3.1 %collective-permute-start.24 = (bf16[4,152,128]{2,1,0:T(8,128)(2,1)S(1)}, bf16[4,152,128]{2,1,0:T(8,128)(2,1)S(1)}, u32[]{:S(2)}, u32[]{:S(2)}) collective-permute-start(bf16[4,152,128]{2,1,0:T(8,128)(2,1)S(1)} %collective-permute-done.20.refs_5_), channel_id=1, source_target_pairs={{0,2},{1,3},{2,0},{3,1},{4,6},{5,7},{6,4},{7,5},{8,10},{9,11},{10,... | collective-permute-start | bytes 466952 | tf_op jit(solution)/shard_map/ppermute | solution.py:19
  70.3 1.5 %collective-permute-start.25 = (bf16[4,152,128]{2,1,0:T(8,128)(2,1)S(1)}, bf16[4,152,128]{2,1,0:T(8,128)(2,1)S(1)}, u32[]{:S(2)}, u32[]{:S(2)}) collective-permute-start(bf16[4,152,128]{2,1,0:T(8,128)(2,1)S(1)} %collective-permute-done.21.refs_6_), channel_id=1, source_target_pairs={{0,2},{1,3},{2,0},{3,1},{4,6},{5,7},{6,4},{7,5},{8,10},{9,11},{10,... | collective-permute-start | bytes 466952 | tf_op jit(solution)/shard_map/ppermute | solution.py:19
  (11 other events, 65.3 us)

commit v8 on v7

--- a/solution.py
+++ b/solution.py
@@ -64,13 +64,14 @@
     return [h ^ k for h in high for k in members(wide_masks(nb))]
 
 
-def scatter_batch(kept, sent, nb):
+def scatter_batch(kept, sent, nb, wide):
     masks = batch_masks(nb)
     x = kept + swap(sent, "batch", masks[0], nb).astype(f32)
     for m in masks[1:-2][::-1]:
         half = x.shape[0] // 2
-        x = x[:half] + swap(x[half:].astype(bf16), "batch", m, nb).astype(f32)
-    return x
+        send, wide = lax.optimization_barrier((x[half:].astype(bf16), wide))
+        x = x[:half] + swap(send, "batch", m, nb).astype(f32)
+    return x, wide
 
 
 def far_groups(nb, nt):
@@ -504,13 +505,13 @@
         *(pos_rows, pos_latent, pos_pre, grad_pos),
         w_out,
     )[0]
+    mine, wide = scatter_batch(kept, sent, nb, wide)
     near_values = call(
         near_forward_kernel,
         "near_forward",
         sets(wide.shape[0], embed, hidden_width),
         *(wide, *weights),
     )
-    mine = scatter_batch(kept, sent, nb)
     total = call(
         functools.partial(negatives_kernel, pieces, animals),
         "negatives",

time: 74.7 us -> 76.6 us (1.025)
  waiting for transfers between devices: 30 us -> 32 us
    ppermute x27, waiting for transfers between devices: 30 us -> 32 us  [swap(): return lax.ppermute(x, axes, [(i, i ^ mask) for i in range(n)])]
  transfers between devices with their start and end apart: 27 -> 27, of which waited for: 20 -> 20; matrix products, arithmetic and copies ran while one was open for 1% -> 0% of each run, Pallas kernels for 11% -> 11%
where the time goes in v8:
time: 76.6 us; the launch traced here: 76.5 us
  waiting for transfers between devices  32 us (42%)
  starting transfers between devices  31.5 us (41%)
  Pallas kernels  11.1 us (14%)
  between operations  1.02 us (1%)
    ppermute x27, waiting for transfers between devices, swap(): return lax.ppermute(x, axes, [(i, i ^ mask) for i in range(n)])  32 us
    ppermute x27, starting transfers between devices, swap(): return lax.ppermute(x, axes, [(i, i ^ mask) for i in range(n)])  31.5 us
    pallas_call x12, Pallas kernels, call(): pl.pallas_call(kernel, name=name, out_shape=shapes, in_specs=[pl.BlockSpe...  11.1 us
  transfers between devices with their start and end apart: 27, of which 20 were waited for; matrix products, arithmetic and copies ran while one was open for 0% of the time, Pallas kernels for 11%

profile of v8, /device:TPU:0, one launch (start us, length us, event | category | flops | bytes accessed | tf_op | source)
XLA Modules:
  0.0 76.5 jit_solution(11420130377064111266)
XLA Ops:
  0.6 3.0 %collective-permute-start = (s32[1,256]{1,0:T(1,128)}, s32[1,256]{1,0:T(1,128)S(1)}, u32[]{:S(2)}, u32[]{:S(2)}) collective-permute-start(s32[1,256]{1,0:T(1,128)} %bitcast.114), channel_id=1, source_target_pairs={{0,1},{1,0},{2,3},{3,2},{4,5},{5,4},{6,7},{7,6},{8,9},{9,8},{10,11... | collective-permute-start | bytes 3080 | tf_op jit(solution)/shard_map/ppermute | solution.py:19
  3.6 2.0 %front.1 = (bf16[64,128]{1,0:T(8,128)(2,1)S(1)}, bf16[64,1152]{1,0:T(8,128)(2,1)S(1)}) custom-call(bf16[1024,512]{1,0:T(8,128)(2,1)} %w_in.5, f32[8,512]{1,0:T(8,128)} %bias.5, bf16[512,128]{1,0:T(8,128)(2,1)} %w_out.9, s32[1,64]{1,0:T(1,128)} %bitcast.117, bf16[64,1024]{1,0:T(8,128)(2,1)} %refs_4_), custom_call_target="tpu_custom_call" | custom-call | tf_op jit(solution)/shard_map/front/pallas_call | solution.py:365
  6.2 2.9 %collective-permute-start.1 = (bf16[64,128]{1,0:T(8,128)(2,1)S(1)}, bf16[64,128]{1,0:T(8,128)(2,1)S(1)}, u32[]{:S(2)}, u32[]{:S(2)}) collective-permute-start(bf16[64,128]{1,0:T(8,128)(2,1)S(1)} %get-tuple-element.77), channel_id=1, source_target_pairs={{0,16},{2,18},{4,20},{6,22},{8,24},{10,26},{12,28},{14,30},{16,0},... | collective-permute-start | bytes 49160 | tf_op jit(solution)/shard_map/ppermute | solution.py:19
  9.1 1.6 %collective-permute-start.4 = (bf16[64,1152]{1,0:T(8,128)(2,1)S(1)}, bf16[64,1152]{1,0:T(8,128)(2,1)S(1)}, u32[]{:S(2)}, u32[]{:S(2)}) collective-permute-start(bf16[64,1152]{1,0:T(8,128)(2,1)S(1)} %get-tuple-element.88), channel_id=1, source_target_pairs={{0,8},{2,10},{4,12},{6,14},{8,0},{10,2},{12,4},{14,6},{16,24},{18,... | collective-permute-start | bytes 442376 | tf_op jit(solution)/shard_map/ppermute | solution.py:19
  12.3 1.6 %collective-permute-start.3 = (bf16[128,128]{1,0:T(8,128)(2,1)S(1)}, bf16[128,128]{1,0:T(8,128)(2,1)S(1)}, u32[]{:S(2)}, u32[]{:S(2)}) collective-permute-start(bf16[128,128]{1,0:T(8,128)(2,1)S(1)} %pad_maximum_fusion.4), channel_id=1, source_target_pairs={{0,4},{2,6},{4,0},{6,2},{8,12},{10,14},{12,8},{14,10},{16,20},{18,... | collective-permute-start | bytes 98312 | tf_op jit(solution)/shard_map/ppermute | solution.py:19
  16.9 2.7 %collective-permute-start.8 = (bf16[128,1152]{1,0:T(8,128)(2,1)S(1)}, bf16[128,1152]{1,0:T(8,128)(2,1)S(1)}, u32[]{:S(2)}, u32[]{:S(2)}) collective-permute-start(bf16[128,1152]{1,0:T(8,128)(2,1)S(1)} %pad_maximum_fusion.1), channel_id=1, source_target_pairs={{0,16},{2,18},{4,20},{6,22},{8,24},{10,26},{12,28},{14,30},{16,0},... | collective-permute-start | bytes 884744 | tf_op jit(solution)/shard_map/ppermute | solution.py:19
  25.5 4.6 %collective-permute-done.8 = bf16[128,1152]{1,0:T(8,128)(2,1)S(1)} collective-permute-done((bf16[128,1152]{1,0:T(8,128)(2,1)S(1)}, bf16[128,1152]{1,0:T(8,128)(2,1)S(1)}, u32[]{:S(2)}, u32[]{:S(2)}) %collective-permute-start.8) | collective-permute-done | bytes 294944 | tf_op jit(solution)/shard_map/ppermute | solution.py:19
  30.2 1.6 %collective-permute-start.9 = (bf16[256,128]{1,0:T(8,128)(2,1)S(1)}, bf16[256,128]{1,0:T(8,128)(2,1)S(1)}, u32[]{:S(2)}, u32[]{:S(2)}) collective-permute-start(bf16[256,128]{1,0:T(8,128)(2,1)S(1)} %slice.128), channel_id=1, source_target_pairs={{0,4},{2,6},{4,0},{6,2},{8,12},{10,14},{12,8},{14,10},{16,20},{18,... | collective-permute-start | bytes 196616 | tf_op jit(solution)/shard_map/ppermute | solution.py:19
  35.5 2.0 %collective-permute-done.10 = bf16[608,512]{1,0:T(8,128)(2,1)S(1)} collective-permute-done((bf16[608,512]{1,0:T(8,128)(2,1)S(1)}, bf16[608,512]{1,0:T(8,128)(2,1)S(1)}, u32[]{:S(2)}, u32[]{:S(2)}) %collective-permute-start.10) | collective-permute-done | bytes 622624 | tf_op jit(solution)/shard_map/ppermute | solution.py:19
  37.7 1.6 %collective-permute-start.11 = (bf16[152,512]{1,0:T(8,128)(2,1)S(1)}, bf16[152,512]{1,0:T(8,128)(2,1)S(1)}, u32[]{:S(2)}, u32[]{:S(2)}) collective-permute-start(bf16[152,512]{1,0:T(8,128)(2,1)S(1)} %get-tuple-element.136), channel_id=1, source_target_pairs={{0,4},{1,5},{2,6},{3,7},{4,0},{5,1},{6,2},{7,3},{8,12},{9,13},{10,... | collective-permute-start | bytes 466952 | tf_op jit(solution)/shard_map/ppermute | solution.py:19
  39.3 2.0 %collective-permute-start.13 = (bf16[152,512]{1,0:T(8,128)(2,1)S(1)}, bf16[152,512]{1,0:T(8,128)(2,1)S(1)}, u32[]{:S(2)}, u32[]{:S(2)}) collective-permute-start(bf16[152,512]{1,0:T(8,128)(2,1)S(1)} %get-tuple-element.134), channel_id=1, source_target_pairs={{0,12},{1,13},{2,14},{3,15},{4,8},{5,9},{6,10},{7,11},{8,4},{9,5},... | collective-permute-start | bytes 466952 | tf_op jit(solution)/shard_map/ppermute | solution.py:19
  41.3 2.6 %collective-permute-done.11.refs_1_ = bf16[152,512]{1,0:T(8,128)(2,1)S(1)} collective-permute-done((bf16[152,512]{1,0:T(8,128)(2,1)S(1)}, bf16[152,512]{1,0:T(8,128)(2,1)S(1)}, u32[]{:S(2)}, u32[]{:S(2)}) %collective-permute-start.11) | collective-permute-done | bytes 155680 | tf_op jit(solution)/shard_map/ppermute | solution.py:19
  43.9 2.4 %collective-permute-done.12.refs_2_ = bf16[152,512]{1,0:T(8,128)(2,1)S(1)} collective-permute-done((bf16[152,512]{1,0:T(8,128)(2,1)S(1)}, bf16[152,512]{1,0:T(8,128)(2,1)S(1)}, u32[]{:S(2)}, u32[]{:S(2)}) %collective-permute-start.12) | collective-permute-done | bytes 155680 | tf_op jit(solution)/shard_map/ppermute | solution.py:19
  46.2 2.2 %collective-permute-done.13.refs_3_ = bf16[152,512]{1,0:T(8,128)(2,1)S(1)} collective-permute-done((bf16[152,512]{1,0:T(8,128)(2,1)S(1)}, bf16[152,512]{1,0:T(8,128)(2,1)S(1)}, u32[]{:S(2)}, u32[]{:S(2)}) %collective-permute-start.13) | collective-permute-done | bytes 155680 | tf_op jit(solution)/shard_map/ppermute | solution.py:19
  50.7 2.3 %collective-permute-start.16 = (bf16[152,128]{1,0:T(8,128)(2,1)S(1)}, bf16[152,128]{1,0:T(8,128)(2,1)S(1)}, u32[]{:S(2)}, u32[]{:S(2)}) collective-permute-start(bf16[152,128]{1,0:T(8,128)(2,1)S(1)} %get-tuple-element.139), channel_id=1, source_target_pairs={{0,17},{1,16},{2,19},{3,18},{4,21},{5,20},{6,23},{7,22},{8,25},{9,... | collective-permute-start | bytes 116744 | tf_op jit(solution)/shard_map/ppermute | solution.py:19
  53.8 2.7 %collective-permute-done.16 = bf16[152,128]{1,0:T(8,128)(2,1)S(1)} collective-permute-done((bf16[152,128]{1,0:T(8,128)(2,1)S(1)}, bf16[152,128]{1,0:T(8,128)(2,1)S(1)}, u32[]{:S(2)}, u32[]{:S(2)}) %collective-permute-start.16) | collective-permute-done | bytes 38944 | tf_op jit(solution)/shard_map/ppermute | solution.py:19
  56.5 1.7 %collective-permute-start.17 = (bf16[152,128]{1,0:T(8,128)(2,1)S(1)}, bf16[152,128]{1,0:T(8,128)(2,1)S(1)}, u32[]{:S(2)}, u32[]{:S(2)}) collective-permute-start(bf16[152,128]{1,0:T(8,128)(2,1)S(1)} %get-tuple-element.133), channel_id=1, source_target_pairs={{0,16},{1,17},{2,18},{3,19},{4,20},{5,21},{6,22},{7,23},{8,24},{9,... | collective-permute-start | bytes 116744 | tf_op jit(solution)/shard_map/ppermute | solution.py:19
  59.4 1.6 %collective-permute-start.19 = (bf16[152,128]{1,0:T(8,128)(2,1)S(1)}, bf16[152,128]{1,0:T(8,128)(2,1)S(1)}, u32[]{:S(2)}, u32[]{:S(2)}) collective-permute-start(bf16[152,128]{1,0:T(8,128)(2,1)S(1)} %get-tuple-element.133), channel_id=1, source_target_pairs={{0,17},{1,16},{2,19},{3,18},{4,21},{5,20},{6,23},{7,22},{8,25},{9,... | collective-permute-start | bytes 116744 | tf_op jit(solution)/shard_map/ppermute | solution.py:19
  62.3 3.1 %collective-permute-done.19 = bf16[152,128]{1,0:T(8,128)(2,1)S(1)} collective-permute-done((bf16[152,128]{1,0:T(8,128)(2,1)S(1)}, bf16[152,128]{1,0:T(8,128)(2,1)S(1)}, u32[]{:S(2)}, u32[]{:S(2)}) %collective-permute-start.19) | collective-permute-done | bytes 38944 | tf_op jit(solution)/shard_map/ppermute | solution.py:19
  65.4 1.7 %collective-permute-start.20 = (bf16[4,152,128]{2,1,0:T(8,128)(2,1)S(1)}, bf16[4,152,128]{2,1,0:T(8,128)(2,1)S(1)}, u32[]{:S(2)}, u32[]{:S(2)}) collective-permute-start(bf16[4,152,128]{2,1,0:T(8,128)(2,1)S(1)} %bitcast_dynamic-update-slice_fusion.refs_4_), channel_id=1, source_target_pairs={{0,4},{1,5},{2,6},{3,7},{4,0},{5,1},{6,2},{7,3},{8,12},{9,13},{10,... | collective-permute-start | bytes 466952 | tf_op jit(solution)/shard_map/ppermute | solution.py:19
  67.1 1.8 %collective-permute-start.22 = (bf16[4,152,128]{2,1,0:T(8,128)(2,1)S(1)}, bf16[4,152,128]{2,1,0:T(8,128)(2,1)S(1)}, u32[]{:S(2)}, u32[]{:S(2)}) collective-permute-start(bf16[4,152,128]{2,1,0:T(8,128)(2,1)S(1)} %bitcast_dynamic-update-slice_fusion.refs_4_), channel_id=1, source_target_pairs={{0,12},{1,13},{2,14},{3,15},{4,8},{5,9},{6,10},{7,11},{8,4},{9,5},... | collective-permute-start | bytes 466952 | tf_op jit(solution)/shard_map/ppermute | solution.py:19
  68.9 1.7 %collective-permute-done.20.refs_5_ = bf16[4,152,128]{2,1,0:T(8,128)(2,1)S(1)} collective-permute-done((bf16[4,152,128]{2,1,0:T(8,128)(2,1)S(1)}, bf16[4,152,128]{2,1,0:T(8,128)(2,1)S(1)}, u32[]{:S(2)}, u32[]{:S(2)}) %collective-permute-start.20) | collective-permute-done | bytes 155680 | tf_op jit(solution)/shard_map/ppermute | solution.py:19
  70.7 1.6 %collective-permute-done.21.refs_6_ = bf16[4,152,128]{2,1,0:T(8,128)(2,1)S(1)} collective-permute-done((bf16[4,152,128]{2,1,0:T(8,128)(2,1)S(1)}, bf16[4,152,128]{2,1,0:T(8,128)(2,1)S(1)}, u32[]{:S(2)}, u32[]{:S(2)}) %collective-permute-start.21) | collective-permute-done | bytes 155680 | tf_op jit(solution)/shard_map/ppermute | solution.py:19
  72.3 1.5 %collective-permute-done.22.refs_7_ = bf16[4,152,128]{2,1,0:T(8,128)(2,1)S(1)} collective-permute-done((bf16[4,152,128]{2,1,0:T(8,128)(2,1)S(1)}, bf16[4,152,128]{2,1,0:T(8,128)(2,1)S(1)}, u32[]{:S(2)}, u32[]{:S(2)}) %collective-permute-start.22) | collective-permute-done | bytes 155680 | tf_op jit(solution)/shard_map/ppermute | solution.py:19
  (92 shorter events, 23.2 us)
Async XLA Ops:
  0.6 5.0 %collective-permute-start = (s32[1,256]{1,0:T(1,128)}, s32[1,256]{1,0:T(1,128)S(1)}, u32[]{:S(2)}, u32[]{:S(2)}) collective-permute-start(s32[1,256]{1,0:T(1,128)} %bitcast.114), channel_id=1, source_target_pairs={{0,1},{1,0},{2,3},{3,2},{4,5},{5,4},{6,7},{7,6},{8,9},{9,8},{10,11... | collective-permute-start | bytes 3080 | tf_op jit(solution)/shard_map/ppermute | solution.py:19
  6.2 6.0 %collective-permute-start.1 = (bf16[64,128]{1,0:T(8,128)(2,1)S(1)}, bf16[64,128]{1,0:T(8,128)(2,1)S(1)}, u32[]{:S(2)}, u32[]{:S(2)}) collective-permute-start(bf16[64,128]{1,0:T(8,128)(2,1)S(1)} %get-tuple-element.77), channel_id=1, source_target_pairs={{0,16},{2,18},{4,20},{6,22},{8,24},{10,26},{12,28},{14,30},{16,0},... | collective-permute-start | bytes 49160 | tf_op jit(solution)/shard_map/ppermute | solution.py:19
  9.1 7.2 %collective-permute-start.4 = (bf16[64,1152]{1,0:T(8,128)(2,1)S(1)}, bf16[64,1152]{1,0:T(8,128)(2,1)S(1)}, u32[]{:S(2)}, u32[]{:S(2)}) collective-permute-start(bf16[64,1152]{1,0:T(8,128)(2,1)S(1)} %get-tuple-element.88), channel_id=1, source_target_pairs={{0,8},{2,10},{4,12},{6,14},{8,0},{10,2},{12,4},{14,6},{16,24},{18,... | collective-permute-start | bytes 442376 | tf_op jit(solution)/shard_map/ppermute | solution.py:19
  10.7 12.6 %collective-permute-start.2 = (bf16[256,1024]{1,0:T(8,128)(2,1)S(1)}, bf16[256,1024]{1,0:T(8,128)(2,1)S(1)}, u32[]{:S(2)}, u32[]{:S(2)}) collective-permute-start(bf16[256,1024]{1,0:T(8,128)(2,1)S(1)} %pick.2), channel_id=1, source_target_pairs={{0,1},{1,0},{2,3},{3,2},{4,5},{5,4},{6,7},{7,6},{8,9},{9,8},{10,11... | collective-permute-start | bytes 1572872 | tf_op jit(solution)/shard_map/ppermute | solution.py:19
  12.3 4.0 %collective-permute-start.3 = (bf16[128,128]{1,0:T(8,128)(2,1)S(1)}, bf16[128,128]{1,0:T(8,128)(2,1)S(1)}, u32[]{:S(2)}, u32[]{:S(2)}) collective-permute-start(bf16[128,128]{1,0:T(8,128)(2,1)S(1)} %pad_maximum_fusion.4), channel_id=1, source_target_pairs={{0,4},{2,6},{4,0},{6,2},{8,12},{10,14},{12,8},{14,10},{16,20},{18,... | collective-permute-start | bytes 98312 | tf_op jit(solution)/shard_map/ppermute | solution.py:19
  16.3 4.3 %collective-permute-start.5 = (bf16[256,128]{1,0:T(8,128)(2,1)S(1)}, bf16[256,128]{1,0:T(8,128)(2,1)S(1)}, u32[]{:S(2)}, u32[]{:S(2)}) collective-permute-start(bf16[256,128]{1,0:T(8,128)(2,1)S(1)} %pad_maximum_fusion.3), channel_id=1, source_target_pairs={{0,8},{2,10},{4,12},{6,14},{8,0},{10,2},{12,4},{14,6},{16,24},{18,... | collective-permute-start | bytes 196616 | tf_op jit(solution)/shard_map/ppermute | solution.py:19
  16.9 13.2 %collective-permute-start.8 = (bf16[128,1152]{1,0:T(8,128)(2,1)S(1)}, bf16[128,1152]{1,0:T(8,128)(2,1)S(1)}, u32[]{:S(2)}, u32[]{:S(2)}) collective-permute-start(bf16[128,1152]{1,0:T(8,128)(2,1)S(1)} %pad_maximum_fusion.1), channel_id=1, source_target_pairs={{0,16},{2,18},{4,20},{6,22},{8,24},{10,26},{12,28},{14,30},{16,0},... | collective-permute-start | bytes 884744 | tf_op jit(solution)/shard_map/ppermute | solution.py:19
  25.5 4.7 %collective-permute-start.7 = (bf16[512,128]{1,0:T(8,128)(2,1)S(1)}, bf16[512,128]{1,0:T(8,128)(2,1)S(1)}, u32[]{:S(2)}, u32[]{:S(2)}) collective-permute-start(bf16[512,128]{1,0:T(8,128)(2,1)S(1)} %get-tuple-element.109), channel_id=1, source_target_pairs={{0,2},{2,0},{4,6},{6,4},{8,10},{10,8},{12,14},{14,12},{16,18},{18,... | collective-permute-start | bytes 393224 | tf_op jit(solution)/shard_map/ppermute | solution.py:19
  30.2 4.3 %collective-permute-start.9 = (bf16[256,128]{1,0:T(8,128)(2,1)S(1)}, bf16[256,128]{1,0:T(8,128)(2,1)S(1)}, u32[]{:S(2)}, u32[]{:S(2)}) collective-permute-start(bf16[256,128]{1,0:T(8,128)(2,1)S(1)} %slice.128), channel_id=1, source_target_pairs={{0,4},{2,6},{4,0},{6,2},{8,12},{10,14},{12,8},{14,10},{16,20},{18,... | collective-permute-start | bytes 196616 | tf_op jit(solution)/shard_map/ppermute | solution.py:19
  35.4 2.1 %collective-permute-start.10 = (bf16[608,512]{1,0:T(8,128)(2,1)S(1)}, bf16[608,512]{1,0:T(8,128)(2,1)S(1)}, u32[]{:S(2)}, u32[]{:S(2)}) collective-permute-start(bf16[608,512]{1,0:T(8,128)(2,1)S(1)} %dynamic-slice_bitcast_fusion), channel_id=1, source_target_pairs={{0,2},{1,3},{2,0},{3,1},{4,6},{5,7},{6,4},{7,5},{8,10},{9,11},{10,... | collective-permute-start | bytes 1867784 | tf_op jit(solution)/shard_map/ppermute | solution.py:19
  37.7 6.1 %collective-permute-start.11 = (bf16[152,512]{1,0:T(8,128)(2,1)S(1)}, bf16[152,512]{1,0:T(8,128)(2,1)S(1)}, u32[]{:S(2)}, u32[]{:S(2)}) collective-permute-start(bf16[152,512]{1,0:T(8,128)(2,1)S(1)} %get-tuple-element.136), channel_id=1, source_target_pairs={{0,4},{1,5},{2,6},{3,7},{4,0},{5,1},{6,2},{7,3},{8,12},{9,13},{10,... | collective-permute-start | bytes 466952 | tf_op jit(solution)/shard_map/ppermute | solution.py:19
  39.3 6.9 %collective-permute-start.12 = (bf16[152,512]{1,0:T(8,128)(2,1)S(1)}, bf16[152,512]{1,0:T(8,128)(2,1)S(1)}, u32[]{:S(2)}, u32[]{:S(2)}) collective-permute-start(bf16[152,512]{1,0:T(8,128)(2,1)S(1)} %get-tuple-element.135), channel_id=1, source_target_pairs={{0,8},{1,9},{2,10},{3,11},{4,12},{5,13},{6,14},{7,15},{8,0},{9,1},... | collective-permute-start | bytes 466952 | tf_op jit(solution)/shard_map/ppermute | solution.py:19
  39.3 9.1 %collective-permute-start.13 = (bf16[152,512]{1,0:T(8,128)(2,1)S(1)}, bf16[152,512]{1,0:T(8,128)(2,1)S(1)}, u32[]{:S(2)}, u32[]{:S(2)}) collective-permute-start(bf16[152,512]{1,0:T(8,128)(2,1)S(1)} %get-tuple-element.134), channel_id=1, source_target_pairs={{0,12},{1,13},{2,14},{3,15},{4,8},{5,9},{6,10},{7,11},{8,4},{9,5},... | collective-permute-start | bytes 466952 | tf_op jit(solution)/shard_map/ppermute | solution.py:19
  48.5 5.2 %collective-permute-start.14 = (bf16[152,128]{1,0:T(8,128)(2,1)S(1)}, bf16[152,128]{1,0:T(8,128)(2,1)S(1)}, u32[]{:S(2)}, u32[]{:S(2)}) collective-permute-start(bf16[152,128]{1,0:T(8,128)(2,1)S(1)} %get-tuple-element.138), channel_id=1, source_target_pairs={{0,16},{1,17},{2,18},{3,19},{4,20},{5,21},{6,22},{7,23},{8,24},{9,... | collective-permute-start | bytes 116744 | tf_op jit(solution)/shard_map/ppermute | solution.py:19
  49.8 4.0 %collective-permute-start.15 = (bf16[152,128]{1,0:T(8,128)(2,1)S(1)}, bf16[152,128]{1,0:T(8,128)(2,1)S(1)}, u32[]{:S(2)}, u32[]{:S(2)}) collective-permute-start(bf16[152,128]{1,0:T(8,128)(2,1)S(1)} %get-tuple-element.140), channel_id=1, source_target_pairs={{0,1},{1,0},{2,3},{3,2},{4,5},{5,4},{6,7},{7,6},{8,9},{9,8},{10,11... | collective-permute-start | bytes 116744 | tf_op jit(solution)/shard_map/ppermute | solution.py:19
  50.7 5.8 %collective-permute-start.16 = (bf16[152,128]{1,0:T(8,128)(2,1)S(1)}, bf16[152,128]{1,0:T(8,128)(2,1)S(1)}, u32[]{:S(2)}, u32[]{:S(2)}) collective-permute-start(bf16[152,128]{1,0:T(8,128)(2,1)S(1)} %get-tuple-element.139), channel_id=1, source_target_pairs={{0,17},{1,16},{2,19},{3,18},{4,21},{5,20},{6,23},{7,22},{8,25},{9,... | collective-permute-start | bytes 116744 | tf_op jit(solution)/shard_map/ppermute | solution.py:19
  56.5 5.2 %collective-permute-start.17 = (bf16[152,128]{1,0:T(8,128)(2,1)S(1)}, bf16[152,128]{1,0:T(8,128)(2,1)S(1)}, u32[]{:S(2)}, u32[]{:S(2)}) collective-permute-start(bf16[152,128]{1,0:T(8,128)(2,1)S(1)} %get-tuple-element.133), channel_id=1, source_target_pairs={{0,16},{1,17},{2,18},{3,19},{4,20},{5,21},{6,22},{7,23},{8,24},{9,... | collective-permute-start | bytes 116744 | tf_op jit(solution)/shard_map/ppermute | solution.py:19
  58.3 4.0 %collective-permute-start.18 = (bf16[152,128]{1,0:T(8,128)(2,1)S(1)}, bf16[152,128]{1,0:T(8,128)(2,1)S(1)}, u32[]{:S(2)}, u32[]{:S(2)}) collective-permute-start(bf16[152,128]{1,0:T(8,128)(2,1)S(1)} %get-tuple-element.133), channel_id=1, source_target_pairs={{0,1},{1,0},{2,3},{3,2},{4,5},{5,4},{6,7},{7,6},{8,9},{9,8},{10,11... | collective-permute-start | bytes 116744 | tf_op jit(solution)/shard_map/ppermute | solution.py:19
  59.4 5.9 %collective-permute-start.19 = (bf16[152,128]{1,0:T(8,128)(2,1)S(1)}, bf16[152,128]{1,0:T(8,128)(2,1)S(1)}, u32[]{:S(2)}, u32[]{:S(2)}) collective-permute-start(bf16[152,128]{1,0:T(8,128)(2,1)S(1)} %get-tuple-element.133), channel_id=1, source_target_pairs={{0,17},{1,16},{2,19},{3,18},{4,21},{5,20},{6,23},{7,22},{8,25},{9,... | collective-permute-start | bytes 116744 | tf_op jit(solution)/shard_map/ppermute | solution.py:19
  65.4 5.3 %collective-permute-start.20 = (bf16[4,152,128]{2,1,0:T(8,128)(2,1)S(1)}, bf16[4,152,128]{2,1,0:T(8,128)(2,1)S(1)}, u32[]{:S(2)}, u32[]{:S(2)}) collective-permute-start(bf16[4,152,128]{2,1,0:T(8,128)(2,1)S(1)} %bitcast_dynamic-update-slice_fusion.refs_4_), channel_id=1, source_target_pairs={{0,4},{1,5},{2,6},{3,7},{4,0},{5,1},{6,2},{7,3},{8,12},{9,13},{10,... | collective-permute-start | bytes 466952 | tf_op jit(solution)/shard_map/ppermute | solution.py:19
  67.0 5.2 %collective-permute-start.21 = (bf16[4,152,128]{2,1,0:T(8,128)(2,1)S(1)}, bf16[4,152,128]{2,1,0:T(8,128)(2,1)S(1)}, u32[]{:S(2)}, u32[]{:S(2)}) collective-permute-start(bf16[4,152,128]{2,1,0:T(8,128)(2,1)S(1)} %bitcast_dynamic-update-slice_fusion.refs_4_), channel_id=1, source_target_pairs={{0,8},{1,9},{2,10},{3,11},{4,12},{5,13},{6,14},{7,15},{8,0},{9,1},... | collective-permute-start | bytes 466952 | tf_op jit(solution)/shard_map/ppermute | solution.py:19
  67.1 6.7 %collective-permute-start.22 = (bf16[4,152,128]{2,1,0:T(8,128)(2,1)S(1)}, bf16[4,152,128]{2,1,0:T(8,128)(2,1)S(1)}, u32[]{:S(2)}, u32[]{:S(2)}) collective-permute-start(bf16[4,152,128]{2,1,0:T(8,128)(2,1)S(1)} %bitcast_dynamic-update-slice_fusion.refs_4_), channel_id=1, source_target_pairs={{0,12},{1,13},{2,14},{3,15},{4,8},{5,9},{6,10},{7,11},{8,4},{9,5},... | collective-permute-start | bytes 466952 | tf_op jit(solution)/shard_map/ppermute | solution.py:19
  68.9 4.9 %collective-permute-start.23 = (bf16[4,152,128]{2,1,0:T(8,128)(2,1)S(1)}, bf16[4,152,128]{2,1,0:T(8,128)(2,1)S(1)}, u32[]{:S(2)}, u32[]{:S(2)}) collective-permute-start(bf16[4,152,128]{2,1,0:T(8,128)(2,1)S(1)} %bitcast_dynamic-update-slice_fusion.refs_4_), channel_id=1, source_target_pairs={{0,2},{1,3},{2,0},{3,1},{4,6},{5,7},{6,4},{7,5},{8,10},{9,11},{10,... | collective-permute-start | bytes 466952 | tf_op jit(solution)/shard_map/ppermute | solution.py:19
  70.7 3.1 %collective-permute-start.24 = (bf16[4,152,128]{2,1,0:T(8,128)(2,1)S(1)}, bf16[4,152,128]{2,1,0:T(8,128)(2,1)S(1)}, u32[]{:S(2)}, u32[]{:S(2)}) collective-permute-start(bf16[4,152,128]{2,1,0:T(8,128)(2,1)S(1)} %collective-permute-done.20.refs_5_), channel_id=1, source_target_pairs={{0,2},{1,3},{2,0},{3,1},{4,6},{5,7},{6,4},{7,5},{8,10},{9,11},{10,... | collective-permute-start | bytes 466952 | tf_op jit(solution)/shard_map/ppermute | solution.py:19
  (11 other events, 65.5 us)
